TPU v7x, 1024 devices: a whole 4x8x16 slice. The times are simulated.
1024 devices in a mesh: rep: 16 (over y_hi, x, core), fsdp: 64 (over y_lo, z).
Axes of the slice: x: 4, y: 8 (y_hi: 2, y_lo: 4; y = y_hi * 4 + y_lo), z: 16, core: 2. Of those that a mesh axis runs over, the one named last changes fastest.
Arguments:
- replica_grads: bfloat16 [16, 8192, 8192], P('rep', 'fsdp'), may hold values from -0.19921875 to 0.19921875
- weight: bfloat16 [8192, 8192], P('fsdp'), may hold values from -6 to 6
- moment_one: float32 [1024, 1024], P('rep', 'fsdp'), may hold values from -3 to 3
- moment_two: float32 [1024, 1024], P('rep', 'fsdp'), may hold values from 0.1 to 10
- sign_bits: int32 [8192], replicated, may hold values from 0 to 1
- kept_rows: int32 [1024], replicated, may hold values from 0 to 8191, as said below
- step_count: int32 [], replicated, may hold values from 1 to 7
Outputs:
- new_weight: bfloat16 [8192, 8192], P('fsdp')
- new_moment_one: float32 [1024, 1024], P('rep', 'fsdp')
- new_moment_two: float32 [1024, 1024], P('rep', 'fsdp')
Inputs may be any that keep to these rules, and one draw needn't show every extreme that they name: `kept_rows`: all different; 0 and 8191 are always among them.
All inputs are finite; a program needn't handle non-finite values.
Results may differ from a plain program's by a relative error of at most 0.0049.
Values may be sent and summed in bfloat16 or wider, within the bound.
No kernel may reach another device: no remote copies, remote signals or barrier semaphores. Data moves between devices by JAX's collectives and lax.ppermute only.
A program may use at most 64 MiB of HBM per device.

v0:
```python
import math

import jax
import jax.numpy as jnp
from jax import lax
from jax.sharding import PartitionSpec as P

BETA_ONE = 0.9
BETA_TWO = 0.95
EPSILON = 1e-08
LEARN_RATE = 0.25


def hadamard(order):
    positions = jnp.arange(order, dtype=jnp.int32)
    both = jnp.bitwise_and(positions[:, None], positions[None, :])
    parity = jnp.zeros_like(both)
    for bit_index in range(max(order.bit_length() - 1, 0)):
        parity = parity + jnp.bitwise_and(jnp.right_shift(both, bit_index), 1)
    parity = parity % 2
    return (1 - 2 * parity).astype(jnp.float32)


def transform_last(matrix):
    length = matrix.shape[-1]
    low_len = min(length, 128)
    high_len = length // low_len
    values = matrix.reshape(matrix.shape[:-1] + (high_len, low_len))
    if matrix.dtype == jnp.bfloat16:
        values = jnp.einsum(
            "rab,cb->rac",
            values,
            hadamard(low_len).astype(jnp.bfloat16),
            preferred_element_type=jnp.float32,
        )
    else:
        values = jnp.einsum(
            "rab,cb->rac", values, hadamard(low_len), precision=lax.Precision.HIGHEST
        )
    values = jnp.einsum("rab,ca->rcb", values, hadamard(high_len), precision=lax.Precision.HIGHEST)
    return values.reshape(matrix.shape)


def transform_rows(matrix):
    length = matrix.shape[0]
    low_len = min(length, 128)
    high_len = length // low_len
    values = matrix.reshape((high_len, low_len) + matrix.shape[1:])
    values = jnp.einsum("abc,db->adc", values, hadamard(low_len), precision=lax.Precision.HIGHEST)
    values = jnp.einsum("abc,da->dbc", values, hadamard(high_len), precision=lax.Precision.HIGHEST)
    return values.reshape(matrix.shape)


def local(replica_grads, weight, moment_one, moment_two, sign_bits, kept_rows, step_count):
    sign_vec = (1 - 2 * sign_bits).astype(jnp.float32)
    full_len = sign_vec.shape[0]
    kept_len = kept_rows.shape[0]
    norm_scale = 1.0 / math.sqrt(kept_len)
    row_count = moment_one.shape[0]
    local_grads = replica_grads[0]
    summed = lax.psum_scatter(
        local_grads.astype(jnp.float32).astype(jnp.bfloat16), "rep", scatter_dimension=0, tiled=True
    ).astype(jnp.float32)
    row_part = jnp.take(transform_last(summed * sign_vec[None, :]), kept_rows, axis=1) * norm_scale
    row_block = lax.all_gather(row_part.astype(jnp.bfloat16), "rep", axis=0, tiled=True).astype(
        row_part.dtype
    )
    col_panel = lax.all_to_all(
        row_block.astype(jnp.bfloat16), "fsdp", split_axis=1, concat_axis=0, tiled=True
    ).astype(row_block.dtype)
    col_sketch = (
        jnp.take(transform_rows(col_panel * sign_vec[:, None]), kept_rows, axis=0) * norm_scale
    )
    start_row = lax.axis_index("rep") * row_count
    compressed = lax.dynamic_slice_in_dim(col_sketch, start_row, row_count, 0)
    new_one = BETA_ONE * moment_one + (1.0 - BETA_ONE) * compressed
    new_two = BETA_TWO * moment_two + (1.0 - BETA_TWO) * compressed * compressed
    steps_done = step_count.astype(jnp.float32)
    first_fix = 1.0 - jnp.power(jnp.float32(BETA_ONE), steps_done)
    second_fix = 1.0 - jnp.power(jnp.float32(BETA_TWO), steps_done)
    direction = new_one / first_fix / (jnp.sqrt(new_two / second_fix) + EPSILON)
    dir_panel = lax.all_gather(direction, "rep", axis=0, tiled=True)
    placed = jnp.zeros((full_len, dir_panel.shape[1]), jnp.float32).at[kept_rows].set(dir_panel)
    back_bf = (transform_rows(placed) * sign_vec[:, None] * norm_scale).astype(jnp.bfloat16)
    back_rows = lax.all_to_all(back_bf, "fsdp", split_axis=0, concat_axis=1, tiled=True)
    col_fill = (
        jnp.zeros((back_rows.shape[0], full_len), jnp.bfloat16).at[:, kept_rows].set(back_rows)
    )
    update_full = transform_last(col_fill) * sign_vec[None, :] * norm_scale
    new_weight = (weight.astype(jnp.float32) - LEARN_RATE * update_full).astype(jnp.bfloat16)
    return (new_weight, new_one, new_two)


def solution(mesh):
    in_specs = (
        P("rep", "fsdp", None),
        P("fsdp", None),
        P("rep", "fsdp"),
        P("rep", "fsdp"),
        P(),
        P(),
        P(),
    )
    out_specs = (P("fsdp", None), P("rep", "fsdp"), P("rep", "fsdp"))
    return jax.shard_map(local, mesh=mesh, in_specs=in_specs, out_specs=out_specs, check_vma=False)
```

profile of v0, /device:TPU:1, one launch (start us, length us, event | category | flops | bytes accessed | tf_op | source)
XLA Modules:
  0.0 303.2 jit_solution(3705841154536336491)
XLA Ops:
  7.2 0.7 reduce-scatter.2.cloned.1.call-update
  7.9 0.7 compare_and_fusion
  8.6 0.7 broadcast_clamp_fusion
  9.3 0.8 fusion.117
  10.1 122.3 %reduce-scatter.2.cloned.1.call-done = bf16[8,8192]{1,0:T(8,128)(2,1)} async-done(((bf16[128,8192]{1,0:T(8,128)(2,1)}), bf16[8,8192]{1,0:T(8,128)(2,1)}) %reduce-scatter.2.cloned.1.call-update) | async-done | bytes 131088 | tf_op jit(solution)/shard_map/reduce_scatter | solution.py:61
  132.4 0.9 multiply_bitcast_fusion
  133.3 0.4 fusion.12
  133.8 0.4 convolution_bitcast_fusion.2
  134.1 2.6 copy.65
  136.7 5.0 %gather_fusion = f32[1024,8]{1,0:T(8,128)S(1)} fusion(f32[8,8192]{0,1:T(8,128)} %bitcast.67, s32[1024]{0:T(1024)S(1)} %get-tuple-element.20), kind=kCustom, calls=%fused_computation | custom fusion | bytes 69632 | tf_op jit(solution)/shard_map/jit(_take)/gather | solution.py:64
  141.7 0.2 fusion.10
  142.1 29.0 %all_gather.6 = bf16[128,1024]{1,0:T(8,128)(2,1)S(1)} all-gather(bf16[8,1024]{1,0:T(8,128)(2,1)S(1)} %copy.55), channel_id=1, replica_groups=mesh['rep'=16,'fsdp'=64] {'rep'}, dimensions={0}, use_global_device_ids=true | all-gather | bytes 278528 | tf_op jit(solution)/shard_map/all_gather | solution.py:65
  171.1 0.8 copy.56
  171.9 16.2 %all-to-all-start = ((bf16[128,64,16]{0,2,1:T(8,128)(2,1)}), bf16[128,64,16]{0,2,1:T(8,128)(2,1)S(1)}, u32[]{:S(2)}, u32[]{:S(2)}) async-start(bf16[128,64,16]{0,2,1:T(8,128)(2,1)} %bitcast.7), calls=%async_computation.1 | async-start | bytes 524288 | tf_op jit(solution)/shard_map/all_to_all | solution.py:68
  189.0 19.0 %all-to-all-done = bf16[128,64,16]{0,2,1:T(8,128)(2,1)S(1)} async-done(((bf16[128,64,16]{0,2,1:T(8,128)(2,1)}), bf16[128,64,16]{0,2,1:T(8,128)(2,1)S(1)}, u32[]{:S(2)}, u32[]{:S(2)}) %all-to-all-start) | async-done | bytes 262176 | tf_op jit(solution)/shard_map/all_to_all | solution.py:68
  207.9 0.6 convolution_bitcast_fusion.1
  208.6 0.6 fusion.37
  209.2 2.6 copy.66
  211.8 5.0 %gather_fusion.1 = f32[1024,16]{1,0:T(8,128)S(1)} fusion(f32[8192,16]{1,0:T(8,128)} %bitcast.63, s32[1024]{0:T(1024)S(1)} %get-tuple-element.20), kind=kCustom, calls=%fused_computation.1 | custom fusion | bytes 135168 | tf_op jit(solution)/shard_map/jit(_take)/gather | solution.py:72
  216.9 0.6 divide_bitcast_fusion
  217.5 26.1 %all-gather = f32[16,64,16]{1,2,0:T(8,128)S(1)} all-gather(f32[1,64,16]{1,2,0:T(8,128)S(1)} %get-tuple-element.15), channel_id=1, replica_groups=mesh['rep'=16,'fsdp'=64] {'rep'}, dimensions={0}, use_global_device_ids=true | all-gather | bytes 69632 | tf_op jit(solution)/shard_map/all_gather | solution.py:82
  243.6 0.2 copy.67
  243.8 5.2 %scatter_custom_fusion = f32[8192,16]{1,0:T(8,128)} fusion(s32[1024]{0:T(1024)S(1)} %get-tuple-element.21, f32[1024,16]{1,0:T(8,128)S(1)} %bitcast.69, f32[]{:T(128)} %constant.67.clone.1), kind=kCustom, calls=%fused_computation.8 | custom fusion | bytes 524292 | tf_op jit(solution)/shard_map/scatter | solution.py:83
  249.1 2.9 copy.62
  251.9 0.6 convolution_bitcast_fusion
  252.6 0.6 fusion.6
  253.4 25.7 %all_to_all.29 = bf16[64,128,16]{1,2,0:T(8,128)(2,1)S(1)} all-to-all(bf16[64,128,16]{1,2,0:T(8,128)(2,1)S(1)} %copy.63), channel_id=1, replica_groups=mesh['rep'=16,'fsdp'=64] {'fsdp'}, dimensions={0} | all-to-all | bytes 524288 | tf_op jit(solution)/shard_map/all_to_all | solution.py:85
  279.1 4.9 %scatter_custom_fusion.1 = bf16[128,8192]{0,1:T(8,128)(2,1)} fusion(s32[1024]{0:T(1024)S(1)} %get-tuple-element.21, bf16[1024,128]{1,0:T(8,128)(2,1)S(1)} %bitcast.70, bf16[]{:T(256)} %constant.64.clone.1), kind=kCustom, calls=%fused_computation.16 | custom fusion | bytes 2097154 | tf_op jit(solution)/shard_map/scatter | solution.py:87
  283.9 3.3 %copy.64 = bf16[128,64,128]{2,1,0:T(8,128)(2,1)S(1)} copy(bf16[128,64,128]{0,2,1:T(8,128)(2,1)} %bitcast.66) | data formatting | bytes 4194304 | tf_op jit(solution)/shard_map/reshape | solution.py:28
  287.2 0.8 fusion.27
  288.0 4.1 %fusion.34 = f32[64,128,128]{2,0,1:T(8,128)S(1)} fusion(f32[128,64,128]{2,1,0:T(8,128)S(1)} %fusion.27), kind=kOutput, calls=%fused_computation.49 | convolution fusion | flops 805437440 | bytes 8388608 | tf_op jit(solution)/shard_map/rab,ca->rcb/dot_general | solution.py:40
  292.2 4.2 %fusion.2 = bf16[128,8192]{1,0:T(8,128)(2,1)} fusion(f32[16,8,64,128]{3,2,1,0:T(8,128)S(1)} %bitcast.65, bf16[128,8192]{1,0:T(8,128)(2,1)S(1)} %copy-done, f32[8192]{0:T(1024)S(1)} %get-tuple-element.19), kind=kLoop, calls=%fused_computation.7 | loop fusion | flops 5242880 | bytes 8421376 | tf_op jit(solution)/shard_map/convert_element_type | solution.py:90
  (12 shorter events, 0.5 us)
Async XLA Ops:
  7.2 125.2 %reduce-scatter.2.cloned.1.call-start = ((), (), s32[]{:S(2)}) async-start(), calls=%async_computation.3 | async-start | bytes 2228224 | tf_op jit(solution)/shard_map/reduce_scatter | solution.py:61
  171.9 36.0 %all-to-all-start = ((bf16[128,64,16]{0,2,1:T(8,128)(2,1)}), bf16[128,64,16]{0,2,1:T(8,128)(2,1)S(1)}, u32[]{:S(2)}, u32[]{:S(2)}) async-start(bf16[128,64,16]{0,2,1:T(8,128)(2,1)} %bitcast.7), calls=%async_computation.1 | async-start | bytes 524288 | tf_op jit(solution)/shard_map/all_to_all | solution.py:68
  209.2 7.7 %copy-start.1 = (f32[64,16]{0,1:T(8,128)S(1)}, f32[64,16]{0,1:T(8,128)}, u32[]{:S(2)}) copy-start(f32[64,16]{0,1:T(8,128)} %param.10) | copy-start | bytes 12292
  209.2 7.7 %copy-start.2 = (f32[64,16]{0,1:T(8,128)S(1)}, f32[64,16]{0,1:T(8,128)}, u32[]{:S(2)}) copy-start(f32[64,16]{0,1:T(8,128)} %param.9) | copy-start | bytes 12292
  288.0 4.1 %copy-start = (bf16[128,8192]{1,0:T(8,128)(2,1)S(1)}, bf16[128,8192]{1,0:T(8,128)(2,1)}, u32[]{:S(2)}) copy-start(bf16[128,8192]{1,0:T(8,128)(2,1)} %param.8) | copy-start | bytes 6291460
Sparse Core Ops, SparseCore 0:
  13.9 118.3 reduce-scatter.1
where the time goes:
time: 305 us; the launch traced here: 303 us
  waiting for transfers between devices  142 us (47%)
  blocking collectives  80.8 us (26%)
  local copies, waits for them, and re-layouts  32.9 us (11%)
  starting transfers between devices  16.3 us (5%)
  between operations  14.9 us (5%)
  matrix products  8.26 us (3%)
  other arithmetic  8.07 us (3%)
    reduce_scatter x1, waiting for transfers between devices, local(): lax.psum_scatter(local_grads.astype(jnp.float32).astype(jnp.bfloat16), 'r...  122 us
    all_gather x1, blocking collectives, local(): lax.all_gather(row_part.astype(jnp.bfloat16), 'rep', axis=0, tiled=True)  29 us
    all_gather x1, blocking collectives, local(): dir_panel = lax.all_gather(direction, 'rep', axis=0, tiled=True)  26.1 us
    all_to_all x1, blocking collectives, local(): lax.all_to_all(back_bf, 'fsdp', split_axis=0, concat_axis=1, tiled=True)  25.7 us
    all_to_all x1, waiting for transfers between devices, local(): lax.all_to_all(row_block.astype(jnp.bfloat16), 'fsdp', split_axis=1, conc...  19 us
    all_to_all x1, starting transfers between devices, local(): lax.all_to_all(row_block.astype(jnp.bfloat16), 'fsdp', split_axis=1, conc...  16.2 us
  transfers between devices with their start and end apart: 2, of which 2 were waited for; matrix products, arithmetic and copies ran while one was open for 1% of the time, Pallas kernels for 0%

commit v1 on v0

v1 whole, which is shorter than its diff:
```python
import functools
import math

import jax
import jax.numpy as jnp
from jax import lax
from jax.experimental import pallas as pl
from jax.experimental.pallas import tpu as pltpu
from jax.sharding import PartitionSpec as P

BETA_ONE = 0.9
BETA_TWO = 0.95
EPSILON = 1e-08
LEARN_RATE = 0.25
LANES = 128
WIDE = 256
STEP = 1024
F32 = jnp.float32
BF16 = jnp.bfloat16


def parity_signs(left, right):
    both = jnp.bitwise_and(left, right)
    for shift in (8, 4, 2, 1):
        both = jnp.bitwise_xor(both, jnp.right_shift(both, shift))
    return (1 - 2 * jnp.bitwise_and(both, 1)).astype(F32)


def iota(shape, dim):
    return lax.broadcasted_iota(jnp.int32, shape, dim)


def wide_rows(rows, first, count):
    return jnp.concatenate([rows[first + n : first + n + 1, :] for n in range(count)], axis=1)


def column_tables_kernel(place_ref, kept_ref, one_ref, two_ref, low_ref, high_ref, send_ref, own_ref):
    half = jnp.bitwise_and(place_ref[0], 1)
    kept = kept_ref[...]
    blocks = kept.shape[0]
    digits = jnp.concatenate([jnp.right_shift(kept, 7), jnp.bitwise_and(kept, LANES - 1)], axis=0)
    digits = digits.astype(F32).astype(BF16)
    source, target = iota((LANES, LANES), 0), iota((LANES, LANES), 1)
    same = jnp.logical_and(
        jnp.right_shift(source, 4) == jnp.bitwise_and(jnp.right_shift(target, 3), 7),
        jnp.bitwise_and(source, 7) == jnp.bitwise_and(target, 7),
    )
    source_half = jnp.bitwise_and(jnp.right_shift(source, 3), 1)
    pieces = []
    for wanted in (1 - half, half):
        moved = []
        for part in (0, 1):
            pick = jnp.logical_and(same, source_half == wanted)
            pick = jnp.logical_and(pick, jnp.right_shift(target, 6) == part)
            pick = jnp.where(pick, 1.0, 0.0).astype(BF16)
            moved.append(jnp.dot(digits, pick, preferred_element_type=F32))
        for pair in range(blocks // 2):
            even, odd = 2 * pair, 2 * pair + 1
            top = moved[0][even : even + 1, :] + moved[1][odd : odd + 1, :]
            low = (
                moved[0][blocks + even : blocks + even + 1, :]
                + moved[1][blocks + odd : blocks + odd + 1, :]
            )
            pieces.append(top * LANES + low)
    columns = jnp.concatenate(pieces, axis=1).astype(jnp.int32)
    low_ref[...] = parity_signs(iota(low_ref.shape, 0), columns).astype(BF16)
    high_ref[...] = parity_signs(iota(high_ref.shape, 0), jnp.right_shift(columns, 8))
    for index, ref in enumerate((one_ref, two_ref)):
        upper, lower = ref[0:8, :], ref[8:16, :]
        blank = jnp.zeros_like(upper)
        for out, wanted in ((send_ref, 1 - half), (own_ref, half)):
            mine = jnp.where(wanted == 0, upper, lower)
            out[index] = jnp.where(
                half == 0,
                jnp.concatenate([mine, blank], axis=1),
                jnp.concatenate([blank, mine], axis=1),
            )


def row_tables_kernel(kept_ref, low_ref, high_ref):
    rows = wide_rows(kept_ref[...], 0, kept_ref.shape[0])
    low_ref[...] = parity_signs(iota(low_ref.shape, 0), rows).astype(BF16)
    high_ref[...] = parity_signs(iota(high_ref.shape, 0), jnp.right_shift(rows, 7))


def project_kernel(scale, x_ref, bits_ref, low_ref, high_ref, out_ref, acc_ref):
    step = pl.program_id(0)
    signs = (1 - 2 * bits_ref[...]).astype(F32)
    chunks = STEP // WIDE

    @pl.when(step == 0)
    def _():
        acc_ref[...] = jnp.zeros_like(acc_ref)

    total = acc_ref[...]
    for chunk in range(chunks):
        sign = wide_rows(signs, 2 * chunk, 2).astype(BF16)
        x = x_ref[:, chunk * WIDE : (chunk + 1) * WIDE] * sign
        part = jnp.dot(x, low_ref[...], preferred_element_type=F32)
        total = total + part * high_ref[pl.ds(step * chunks + chunk, 1), :]
    acc_ref[...] = total

    @pl.when(step == pl.num_programs(0) - 1)
    def _():
        done = jnp.transpose(acc_ref[...] * scale)
        out_ref[...] = done.reshape(out_ref.shape).astype(out_ref.dtype)


def compress_kernel(scale, y_ref, bits_ref, low_ref, high_ref, own_ref, got_ref, out_ref, part_ref):
    panels, width, lanes = y_ref.shape
    signs = (1 - 2 * bits_ref[...]).astype(F32)
    y = (y_ref[...].astype(F32) * signs[:, None, :]).reshape(panels * width, lanes).astype(BF16)
    part = jnp.dot(y, low_ref[...], preferred_element_type=F32)
    part_ref[...] = part.reshape(part_ref.shape)

    def add(panel, total):
        return total + part_ref[panel] * high_ref[pl.ds(panel, 1), :]

    total = lax.fori_loop(0, panels, add, jnp.zeros(part_ref.shape[1:], F32), unroll=8)
    total = (total * scale).astype(BF16)
    count = total.shape[1] // LANES
    pieces = [total[:, n * LANES : (n + 1) * LANES] for n in range(count)]
    for index in range(2):
        rest = own_ref[index] + got_ref[index]
        for _ in range(3):
            piece = rest.astype(BF16)
            pieces.append(piece)
            rest = rest - piece.astype(F32)
    for peer in range(out_ref.shape[0]):
        for n, piece in enumerate(pieces):
            out_ref[peer, n] = piece


def adam_kernel(
    scale, place_ref, fix_ref, got_ref, bits_ref, low_ref, high_ref, back_ref, sum_ref, lhs_ref
):
    peers = got_ref.shape[0]
    mine = jnp.right_shift(place_ref[0], 1)
    first_fix, second_fix = fix_ref[0], fix_ref[1]
    tops, rests = [], []
    for n in range(peers):
        total = got_ref[0, n].astype(F32)
        for peer in range(1, peers):
            total = total + got_ref[peer, n].astype(F32)

        @pl.when(mine == n)
        def _():
            sum_ref[...] = total

        one = got_ref[n, peers].astype(F32) + got_ref[n, peers + 1].astype(F32)
        one = one + got_ref[n, peers + 2].astype(F32)
        two = got_ref[n, peers + 3].astype(F32) + got_ref[n, peers + 4].astype(F32)
        two = two + got_ref[n, peers + 5].astype(F32)
        new_one = BETA_ONE * one + (1.0 - BETA_ONE) * total
        new_two = BETA_TWO * two + (1.0 - BETA_TWO) * total * total
        direction = new_one / first_fix / (jnp.sqrt(new_two / second_fix) + EPSILON)
        top = direction.astype(BF16).astype(F32)
        tops.append(top)
        rests.append(direction - top)
    both = jnp.concatenate([jnp.concatenate(tops, axis=1), jnp.concatenate(rests, axis=1)], axis=0)
    panels = lhs_ref.shape[0]

    def fill(panel, carry):
        lhs_ref[panel] = (both * high_ref[pl.ds(panel, 1), :]).astype(BF16)
        return carry

    lax.fori_loop(0, panels, fill, 0, unroll=8)
    lhs = lhs_ref[...].reshape(panels * lhs_ref.shape[1], lhs_ref.shape[2])
    back = lax.dot_general(lhs, low_ref[...], (((1,), (1,)), ((), ())), preferred_element_type=F32)
    back = back.reshape(panels, 2, back.shape[0] // panels // 2, LANES)
    signs = (1 - 2 * bits_ref[...]).astype(F32) * scale
    back_ref[...] = ((back[:, 0] + back[:, 1]) * signs[:, None, :]).astype(BF16)


def expand_kernel(scale, other_ref, own_ref, low_ref, high_ref, bits_ref, weight_ref, out_ref,
                  back_ref, table_ref, lhs_ref):
    step = pl.program_id(0)
    rows = weight_ref.shape[0]
    chunks = STEP // WIDE

    @pl.when(step == 0)
    def _():
        for index, ref in enumerate((other_ref, own_ref)):
            half = ref.shape[0] * ref.shape[1]
            columns = ref[...].astype(F32).reshape(half, rows)
            back_ref[:, index * half : (index + 1) * half] = jnp.transpose(columns)
        table_ref[...] = jnp.transpose(low_ref[...].astype(F32)).astype(BF16)

    for chunk in range(chunks):
        sign = high_ref[pl.ds(step * chunks + chunk, 1), :]
        lhs_ref[chunk * rows : (chunk + 1) * rows, :] = (back_ref[...] * sign).astype(BF16)
    update = jnp.dot(lhs_ref[...], table_ref[...], preferred_element_type=F32)
    signs = (1 - 2 * bits_ref[...]).astype(F32) * scale
    for chunk in range(chunks):
        lanes = slice(chunk * WIDE, (chunk + 1) * WIDE)
        moved = update[chunk * rows : (chunk + 1) * rows, :] * wide_rows(signs, 2 * chunk, 2)
        out_ref[:, lanes] = (weight_ref[:, lanes].astype(F32) - moved).astype(BF16)


def shaped(shape, dtype):
    return jax.ShapeDtypeStruct(shape, dtype)


SMEM = pl.BlockSpec(memory_space=pltpu.SMEM)
VMEM = pl.BlockSpec(memory_space=pltpu.VMEM)


def cost(flops, moved):
    return pl.CostEstimate(flops=flops, bytes_accessed=moved, transcendentals=0)


def local(replica_grads, weight, moment_one, moment_two, sign_bits, kept_rows, step_count):
    reps, panels = lax.axis_size("rep"), lax.axis_size("fsdp")
    full_len, kept_len = sign_bits.shape[0], kept_rows.shape[0]
    rows = weight.shape[0]
    peers = reps // 2
    half_width = kept_len // panels // 2
    half_len = kept_len // 2
    norm_scale = 1.0 / math.sqrt(kept_len)
    place = lax.axis_index("rep").astype(jnp.int32).reshape(1)
    half = jnp.bitwise_and(place[0], 1)
    kept = kept_rows.reshape(kept_len // LANES, LANES)
    bits = sign_bits.reshape(full_len // LANES, LANES)
    one_t, two_t = moment_one.T, moment_two.T
    swap = [(n, n ^ 1) for n in range(reps)]
    wide_count = full_len // WIDE

    col_low, col_high, send_moments, own_moments = pl.pallas_call(
        column_tables_kernel,
        out_shape=(
            shaped((WIDE, kept_len), BF16),
            shaped((wide_count, kept_len), F32),
            shaped((2, half_width, LANES), F32),
            shaped((2, half_width, LANES), F32),
        ),
        in_specs=[SMEM, VMEM, VMEM, VMEM],
        out_specs=(VMEM,) * 4,
        cost_estimate=cost(10 * WIDE * kept_len, 2 * WIDE * kept_len),
    )(place, kept, one_t, two_t)

    def project(index, dtype):
        shape = (panels, half_width, rows)
        return pl.pallas_call(
            functools.partial(project_kernel, norm_scale),
            grid=(full_len // STEP,),
            out_shape=shaped(shape, dtype),
            in_specs=[
                pl.BlockSpec((None, rows, STEP), lambda i: (0, 0, i)),
                pl.BlockSpec((STEP // LANES, LANES), lambda i: (i, 0)),
                pl.BlockSpec((WIDE, half_len), lambda i: (0, index)),
                pl.BlockSpec((wide_count, half_len), lambda i: (0, index)),
            ],
            out_specs=pl.BlockSpec(shape, lambda i: (0, 0, 0)),
            scratch_shapes=[pltpu.VMEM((rows, half_len), F32)],
            cost_estimate=cost(2 * rows * full_len * half_len, 2 * rows * full_len),
        )(replica_grads, bits, col_low, col_high)

    for_other = project(0, BF16)
    from_other = lax.ppermute(for_other, "rep", swap)
    got_moments = lax.ppermute(send_moments, "rep", swap)
    mine = project(1, F32)
    row_low, row_high = pl.pallas_call(
        row_tables_kernel,
        out_shape=(shaped((LANES, kept_len), BF16), shaped((panels, kept_len), F32)),
        in_specs=[VMEM],
        out_specs=(VMEM,) * 2,
        cost_estimate=cost(10 * LANES * kept_len, 2 * LANES * kept_len),
    )(kept)
    columns = (mine + from_other.astype(F32)).astype(BF16)
    columns = lax.all_to_all(columns, "fsdp", 0, 0)

    message = pl.pallas_call(
        functools.partial(compress_kernel, norm_scale),
        out_shape=shaped((peers, kept_len // LANES + 6, half_width, LANES), BF16),
        in_specs=[VMEM] * 6,
        out_specs=VMEM,
        scratch_shapes=[pltpu.VMEM((panels, half_width, kept_len), F32)],
        cost_estimate=cost(2 * full_len * half_width * kept_len // panels, 2 * full_len * half_width),
    )(columns, bits, row_low, row_high, own_moments, got_moments)
    groups = [list(range(core, reps, 2)) for core in (0, 1)]
    message = lax.all_to_all(message, "rep", 0, 0, axis_index_groups=groups)

    steps_done = step_count.astype(F32)
    fixes = jnp.stack(
        [1.0 - jnp.power(F32(BETA_ONE), steps_done), 1.0 - jnp.power(F32(BETA_TWO), steps_done)]
    )
    back, own_sum = pl.pallas_call(
        functools.partial(adam_kernel, norm_scale),
        out_shape=(
            shaped((panels, half_width, rows), BF16),
            shaped((half_width, LANES), F32),
        ),
        in_specs=[SMEM, SMEM] + [VMEM] * 4,
        out_specs=(VMEM,) * 2,
        scratch_shapes=[pltpu.VMEM((panels, 2 * half_width, kept_len), BF16)],
        cost_estimate=cost(4 * full_len * half_width * kept_len, 2 * full_len * half_width),
    )(place, fixes, message, bits, row_low, row_high)
    other_sum = lax.ppermute(own_sum, "rep", swap)
    back = lax.all_to_all(back, "fsdp", 0, 0)
    other_back = lax.ppermute(back, "rep", swap)

    row_count = moment_one.shape[0]
    own_rows = jnp.where(half == 0, own_sum[:, :row_count], own_sum[:, row_count:])
    other_rows = jnp.where(half == 0, other_sum[:, :row_count], other_sum[:, row_count:])
    compressed = jnp.where(
        half == 0,
        jnp.concatenate([own_rows, other_rows], axis=0),
        jnp.concatenate([other_rows, own_rows], axis=0),
    )
    new_one = (BETA_ONE * one_t + (1.0 - BETA_ONE) * compressed).T
    new_two = (BETA_TWO * two_t + (1.0 - BETA_TWO) * compressed * compressed).T

    back_shape = (panels, half_width, rows)
    new_weight = pl.pallas_call(
        functools.partial(expand_kernel, LEARN_RATE * norm_scale),
        grid=(full_len // STEP,),
        out_shape=shaped(weight.shape, BF16),
        in_specs=[
            pl.BlockSpec(back_shape, lambda i: (0, 0, 0)),
            pl.BlockSpec(back_shape, lambda i: (0, 0, 0)),
            pl.BlockSpec((WIDE, kept_len), lambda i: (0, 0)),
            pl.BlockSpec((wide_count, kept_len), lambda i: (0, 0)),
            pl.BlockSpec((STEP // LANES, LANES), lambda i: (i, 0)),
            pl.BlockSpec((rows, STEP), lambda i: (0, i)),
        ],
        out_specs=pl.BlockSpec((rows, STEP), lambda i: (0, i)),
        scratch_shapes=[
            pltpu.VMEM((rows, kept_len), F32),
            pltpu.VMEM((kept_len, WIDE), BF16),
            pltpu.VMEM((rows * STEP // WIDE, kept_len), BF16),
        ],
        cost_estimate=cost(2 * rows * full_len * kept_len, 4 * rows * full_len),
    )(other_back, back, col_low, col_high, bits, weight)
    return (new_weight, new_one, new_two)


def solution(mesh):
    in_specs = (
        P("rep", "fsdp", None),
        P("fsdp", None),
        P("rep", "fsdp"),
        P("rep", "fsdp"),
        P(),
        P(),
        P(),
    )
    out_specs = (P("fsdp", None), P("rep", "fsdp"), P("rep", "fsdp"))
    return jax.shard_map(local, mesh=mesh, in_specs=in_specs, out_specs=out_specs, check_vma=False)
```

time: 305 us -> 121 us (0.40)
  waiting for transfers between devices: 142 us -> 29.3 us
  blocking collectives: 80.8 us -> 0 us
  starting transfers between devices: 16.3 us -> 52.5 us
  local copies, waits for them, and re-layouts: 32.9 us -> 1.99 us
  Pallas kernels: 0 us -> 30.6 us
  between operations: 14.9 us -> 1.47 us
  matrix products: 8.26 us -> 0 us
  other arithmetic: 8.07 us -> 3.83 us
    reduce_scatter x1 -> x0, waiting for transfers between devices: 122 us -> none  [local(): lax.psum_scatter(local_grads.astype(jnp.float32).astype(jnp.bfloat16), 'r...]
    all_gather x2 -> x0, blocking collectives: 55.1 us -> none  [the longest x1 29 us: local(): lax.all_gather(row_part.astype(jnp.bfloat16), 'rep', axis=0, tiled=True)]
    pallas_call x0 -> x7, Pallas kernels: none -> 30.6 us  [the longest x2 12.9 us: project(): pl.pallas_call(functools.partial(project_kernel, norm_scale), grid=(full_...]
    ppermute x0 -> x4, starting transfers between devices: none -> 26.6 us  [the longest x1 16.1 us: local(): from_other = lax.ppermute(for_other, 'rep', swap)]
    all_to_all x1 -> x0, blocking collectives: 25.7 us -> none  [local(): lax.all_to_all(back_bf, 'fsdp', split_axis=0, concat_axis=1, tiled=True)]
    reshape x4 -> x0, local copies, waits for them, and re-layouts: 11.3 us -> none  [the longest x1 3.29 us: transform_last(): values = matrix.reshape(matrix.shape[:-1] + (high_len, low_len))]
    scatter x2 -> x0, local copies, waits for them, and re-layouts: 10.1 us -> none  [the longest x1 5.24 us: local(): jnp.zeros((full_len, dir_panel.shape[1]), jnp.float32).at[kept_rows]]
    gather x2 -> x0, local copies, waits for them, and re-layouts: 9.98 us -> none  [the longest x1 4.99 us: local(): jnp.take(transform_last(summed * sign_vec[None, :]), kept_rows, axis=1)]
  transfers between devices with their start and end apart: 2 -> 7, of which waited for: 2 -> 5; matrix products, arithmetic and copies ran while one was open for 1% -> 2% of each run, Pallas kernels for 0% -> 7%
where the time goes in v1:
time: 121 us; the launch traced here: 120 us
  starting transfers between devices  52.5 us (43%)
  Pallas kernels  30.6 us (25%)
  waiting for transfers between devices  29.3 us (24%)
  other arithmetic  3.83 us (3%)
  local copies, waits for them, and re-layouts  1.99 us (2%)
  between operations  1.47 us (1%)
    ppermute x1, starting transfers between devices, local(): from_other = lax.ppermute(for_other, 'rep', swap)  16.1 us
    pallas_call x2, Pallas kernels, project(): pl.pallas_call(functools.partial(project_kernel, norm_scale), grid=(full_...  12.9 us
    all_to_all x1, waiting for transfers between devices, local(): columns = lax.all_to_all(columns, 'fsdp', 0, 0)  10.9 us
    all_to_all x1, starting transfers between devices, local(): columns = lax.all_to_all(columns, 'fsdp', 0, 0)  9.9 us
    all_to_all x1, starting transfers between devices, local(): back = lax.all_to_all(back, 'fsdp', 0, 0)  9.36 us
    all_to_all x1, waiting for transfers between devices, local(): back = lax.all_to_all(back, 'fsdp', 0, 0)  9.31 us
    all_to_all x1, waiting for transfers between devices, local(): message = lax.all_to_all(message, 'rep', 0, 0, axis_index_groups=groups)  8.55 us
    pallas_call x1, Pallas kernels, local(): pl.pallas_call(functools.partial(expand_kernel, LEARN_RATE * norm_scale),...  7.97 us
  transfers between devices with their start and end apart: 7, of which 5 were waited for; matrix products, arithmetic and copies ran while one was open for 2% of the time, Pallas kernels for 7%

profile of v1, /device:TPU:1, one launch (start us, length us, event | category | flops | bytes accessed | tf_op | source)
XLA Modules:
  0.0 119.7 jit_solution(11764390988692128528)
XLA Ops:
  0.6 2.4 %shard_map.94 = (bf16[256,1024]{1,0:T(8,128)(2,1)}, f32[32,1024]{1,0:T(8,128)}, f32[2,8,128]{2,1,0:T(8,128)}, f32[2,8,128]{2,1,0:T(8,128)}) custom-call(s32[1]{0:T(128)} %bitcast.place_ref, s32[8,128]{1,0:T(8,128)} %bitcast.20, f32[16,64]{1,0:T(8,128)} %bitcast.18, f32[16,64]{1,0:T(8,128)} %bitcast.19), custom_call_target="tpu_custom_call" | custom-call | flops 2621440 | bytes 524288 | tf_op jit(solution)/shard_map/pallas_call | solution.py:228
  3.1 6.4 %shard_map.96 = bf16[64,8,128]{2,1,0:T(8,128)(2,1)} custom-call(bf16[1,128,8192]{2,1,0:T(8,128)(2,1)} %x_ref.3, s32[64,128]{1,0:T(8,128)} %bitcast.13, bf16[256,1024]{1,0:T(8,128)(2,1)} %get-tuple-element.11.low_ref, f32[32,1024]{1,0:T(8,128)} %get-tuple-element.12.high_ref), custom_call_target="tpu_custom_call" | custom-call | flops 1073741824 | bytes 2097152 | tf_op jit(solution)/shard_map/pallas_call | solution.py:243
  9.5 16.1 %collective-permute-start = (bf16[64,8,128]{2,1,0:T(8,128)(2,1)}, bf16[64,8,128]{2,1,0:T(8,128)(2,1)S(1)}, u32[]{:S(2)}, u32[]{:S(2)}) collective-permute-start(bf16[64,8,128]{2,1,0:T(8,128)(2,1)} %shard_map.96), channel_id=1, source_target_pairs={{0,64},{64,0},{128,192},{192,128},{256,320},{320,256},{384,448},{4... | collective-permute-start | bytes 393224 | tf_op jit(solution)/shard_map/ppermute | solution.py:259
  25.6 6.5 %shard_map.95 = f32[64,8,128]{2,1,0:T(8,128)} custom-call(bf16[1,128,8192]{2,1,0:T(8,128)(2,1)} %x_ref.3, s32[64,128]{1,0:T(8,128)} %bitcast.14, bf16[256,1024]{1,0:T(8,128)(2,1)} %get-tuple-element.11.low_ref, f32[32,1024]{1,0:T(8,128)} %get-tuple-element.12.high_ref), custom_call_target="tpu_custom_call" | custom-call | flops 1073741824 | bytes 2097152 | tf_op jit(solution)/shard_map/pallas_call | solution.py:243
  32.1 0.0 collective-permute-done
  32.1 1.6 %add_convert_fusion = bf16[64,8,128]{2,1,0:T(8,128)(2,1)} fusion(f32[64,8,128]{2,1,0:T(8,128)} %shard_map.95, bf16[64,8,128]{2,1,0:T(8,128)(2,1)S(1)} %collective-permute-done), kind=kLoop, calls=%fused_computation | loop fusion | flops 196608 | bytes 524288 | tf_op jit(solution)/shard_map/convert_element_type | solution.py:269
  33.8 9.9 %all-to-all-start = ((bf16[64,8,128]{2,1,0:T(8,128)(2,1)}), bf16[64,8,128]{2,1,0:T(8,128)(2,1)S(1)}, u32[]{:S(2)}, u32[]{:S(2)}) async-start(bf16[64,8,128]{2,1,0:T(8,128)(2,1)} %add_convert_fusion), calls=%async_computation | async-start | bytes 262144 | tf_op jit(solution)/shard_map/all_to_all | solution.py:270
  43.7 0.0 copy-done.7
  43.7 2.2 %collective-permute-start.1 = (f32[2,8,128]{2,1,0:T(8,128)S(1)}, f32[2,8,128]{2,1,0:T(8,128)S(1)}, u32[]{:S(2)}, u32[]{:S(2)}) collective-permute-start(f32[2,8,128]{2,1,0:T(8,128)S(1)} %copy-done.7), channel_id=1, source_target_pairs={{0,64},{64,0},{128,192},{192,128},{256,320},{320,256},{384,448},{4... | collective-permute-start | bytes 24584 | tf_op jit(solution)/shard_map/ppermute | solution.py:260
  45.9 1.7 %shard_map.97 = (bf16[128,1024]{1,0:T(8,128)(2,1)}, f32[64,1024]{1,0:T(8,128)}) custom-call(s32[8,128]{1,0:T(8,128)} %bitcast.21), custom_call_target="tpu_custom_call" | custom-call | flops 1310720 | bytes 262144 | tf_op jit(solution)/shard_map/pallas_call | solution.py:262
  47.7 0.0 collective-permute-done.1.got_ref
  47.7 10.9 %all-to-all-done.y_ref = bf16[64,8,128]{2,1,0:T(8,128)(2,1)S(1)} async-done(((bf16[64,8,128]{2,1,0:T(8,128)(2,1)}), bf16[64,8,128]{2,1,0:T(8,128)(2,1)S(1)}, u32[]{:S(2)}, u32[]{:S(2)}) %all-to-all-start) | async-done | bytes 131104 | tf_op jit(solution)/shard_map/all_to_all | solution.py:270
  58.6 0.0 copy-done.5
  58.6 0.6 copy-done
  59.2 2.5 %shard_map.98 = bf16[8,14,8,128]{3,2,1,0:T(8,128)(2,1)} custom-call(bf16[64,8,128]{2,1,0:T(8,128)(2,1)} %copy-done, s32[64,128]{1,0:T(8,128)} %bitcast.15, bf16[128,1024]{1,0:T(8,128)(2,1)} %get-tuple-element.13.low_ref, f32[64,1024]{1,0:T(8,128)} %get-tuple-element.14.high_ref, f32[2,8,128]{2,1,0:T(8,128)} %get-tuple-element.15.own_ref, f32[2,8,128]{2,1,0:T(8,128)} %copy-done.5), custom_call_target="tpu_custom_call" | custom-call | flops 2097152 | bytes 131072 | tf_op jit(solution)/shard_map/pallas_call | solution.py:272
  61.8 6.6 %all-to-all-start.1 = ((bf16[8,14,8,128]{3,2,1,0:T(8,128)(2,1)}), bf16[8,14,8,128]{3,2,1,0:T(8,128)(2,1)S(1)}, u32[]{:S(2)}, u32[]{:S(2)}) async-start(bf16[8,14,8,128]{3,2,1,0:T(8,128)(2,1)} %shard_map.98), calls=%async_computation.1 | async-start | bytes 458752 | tf_op jit(solution)/shard_map/all_to_all | solution.py:281
  69.1 0.7 pad_maximum_fusion.fix_ref
  69.8 8.6 %all-to-all-done.1.got_ref = bf16[8,14,8,128]{3,2,1,0:T(8,128)(2,1)S(1)} async-done(((bf16[8,14,8,128]{3,2,1,0:T(8,128)(2,1)}), bf16[8,14,8,128]{3,2,1,0:T(8,128)(2,1)S(1)}, u32[]{:S(2)}, u32[]{:S(2)}) %all-to-all-start.1) | async-done | bytes 229408 | tf_op jit(solution)/shard_map/all_to_all | solution.py:281
  78.3 0.7 copy-done.1
  79.0 3.1 %shard_map.99 = (bf16[64,8,128]{2,1,0:T(8,128)(2,1)}, f32[8,128]{1,0:T(8,128)}) custom-call(s32[1]{0:T(128)} %bitcast.place_ref, f32[2]{0:T(128)} %pad_maximum_fusion.fix_ref, bf16[8,14,8,128]{3,2,1,0:T(8,128)(2,1)} %copy-done.1, s32[64,128]{1,0:T(8,128)} %bitcast.16, bf16[128,1024]{1,0:T(8,128)(2,1)} %get-tuple-element.13.low_ref, ...), custom_call_target="tpu_custom_call" | custom-call | flops 268435456 | bytes 131072 | tf_op jit(solution)/shard_map/pallas_call | solution.py:287
  82.1 9.4 %all-to-all-start.2 = ((bf16[64,8,128]{2,1,0:T(8,128)(2,1)}), bf16[64,8,128]{2,1,0:T(8,128)(2,1)S(1)}, u32[]{:S(2)}, u32[]{:S(2)}) async-start(bf16[64,8,128]{2,1,0:T(8,128)(2,1)} %get-tuple-element.17), calls=%async_computation.2 | async-start | bytes 262144 | tf_op jit(solution)/shard_map/all_to_all | solution.py:299
  91.4 3.3 %collective-permute-start.3 = (f32[8,128]{1,0:T(8,128)}, f32[8,128]{1,0:T(8,128)S(1)}, u32[]{:S(2)}, u32[]{:S(2)}) collective-permute-start(f32[8,128]{1,0:T(8,128)} %get-tuple-element.18), channel_id=1, source_target_pairs={{0,64},{64,0},{128,192},{192,128},{256,320},{320,256},{384,448},{4... | collective-permute-start | bytes 12296 | tf_op jit(solution)/shard_map/ppermute | solution.py:298
  94.7 0.8 slice_select_fusion.1
  95.6 0.2 collective-permute-done.3
  95.7 0.1 slice_select_fusion
  95.8 9.3 %all-to-all-done.2.own_ref = bf16[64,8,128]{2,1,0:T(8,128)(2,1)S(1)} async-done(((bf16[64,8,128]{2,1,0:T(8,128)(2,1)}), bf16[64,8,128]{2,1,0:T(8,128)(2,1)S(1)}, u32[]{:S(2)}, u32[]{:S(2)}) %all-to-all-start.2) | async-done | bytes 131104 | tf_op jit(solution)/shard_map/all_to_all | solution.py:299
  105.1 5.0 %collective-permute-start.2 = (bf16[64,8,128]{2,1,0:T(8,128)(2,1)S(1)}, bf16[64,8,128]{2,1,0:T(8,128)(2,1)S(1)}, u32[]{:S(2)}, u32[]{:S(2)}) collective-permute-start(bf16[64,8,128]{2,1,0:T(8,128)(2,1)S(1)} %all-to-all-done.2.own_ref), channel_id=1, source_target_pairs={{0,64},{64,0},{128,192},{192,128},{256,320},{320,256},{384,448},{4... | collective-permute-start | bytes 393224 | tf_op jit(solution)/shard_map/ppermute | solution.py:300
  110.1 0.0 copy-done.3
  110.1 0.6 fusion.1
  110.8 0.3 collective-permute-done.2.other_ref
  111.1 0.7 copy-done.6
  111.7 8.0 %shard_map.100 = bf16[128,8192]{1,0:T(8,128)(2,1)} custom-call(bf16[64,8,128]{2,1,0:T(8,128)(2,1)} %copy-done.6, bf16[64,8,128]{2,1,0:T(8,128)(2,1)} %copy-done.2, bf16[256,1024]{1,0:T(8,128)(2,1)} %get-tuple-element.11.low_ref, f32[32,1024]{1,0:T(8,128)} %get-tuple-element.12.high_ref, s32[64,128]{1,0:T(8,128)} %bitcast.17, bf16[128,8192]{1,0:T(8,128)(2,1)} %weight_ref.1), custom_call_target="tpu_custom_call" | custom-call | flops 2147483648 | bytes 4194304 | tf_op jit(solution)/shard_map/pallas_call | solution.py:314
  (10 shorter events, 0.0 us)
Async XLA Ops:
  9.5 34.2 %copy-start.7 = (f32[2,8,128]{2,1,0:T(8,128)S(1)}, f32[2,8,128]{2,1,0:T(8,128)}, u32[]{:S(2)}) copy-start(f32[2,8,128]{2,1,0:T(8,128)} %get-tuple-element.16) | copy-start | bytes 24580
  9.5 22.7 %collective-permute-start = (bf16[64,8,128]{2,1,0:T(8,128)(2,1)}, bf16[64,8,128]{2,1,0:T(8,128)(2,1)S(1)}, u32[]{:S(2)}, u32[]{:S(2)}) collective-permute-start(bf16[64,8,128]{2,1,0:T(8,128)(2,1)} %shard_map.96), channel_id=1, source_target_pairs={{0,64},{64,0},{128,192},{192,128},{256,320},{320,256},{384,448},{4... | collective-permute-start | bytes 393224 | tf_op jit(solution)/shard_map/ppermute | solution.py:259
  32.1 78.0 %copy-start.3 = (f32[64,16]{0,1:T(8,128)S(1)}, f32[64,16]{0,1:T(8,128)}, u32[]{:S(2)}) copy-start(f32[64,16]{0,1:T(8,128)} %param.9) | copy-start | bytes 12292
  32.1 78.0 %copy-start.4 = (f32[64,16]{0,1:T(8,128)S(1)}, f32[64,16]{0,1:T(8,128)}, u32[]{:S(2)}) copy-start(f32[64,16]{0,1:T(8,128)} %param.10) | copy-start | bytes 12292
  33.8 24.8 %all-to-all-start = ((bf16[64,8,128]{2,1,0:T(8,128)(2,1)}), bf16[64,8,128]{2,1,0:T(8,128)(2,1)S(1)}, u32[]{:S(2)}, u32[]{:S(2)}) async-start(bf16[64,8,128]{2,1,0:T(8,128)(2,1)} %add_convert_fusion), calls=%async_computation | async-start | bytes 262144 | tf_op jit(solution)/shard_map/all_to_all | solution.py:270
  43.7 4.0 %collective-permute-start.1 = (f32[2,8,128]{2,1,0:T(8,128)S(1)}, f32[2,8,128]{2,1,0:T(8,128)S(1)}, u32[]{:S(2)}, u32[]{:S(2)}) collective-permute-start(f32[2,8,128]{2,1,0:T(8,128)S(1)} %copy-done.7), channel_id=1, source_target_pairs={{0,64},{64,0},{128,192},{192,128},{256,320},{320,256},{384,448},{4... | collective-permute-start | bytes 24584 | tf_op jit(solution)/shard_map/ppermute | solution.py:260
  47.7 11.0 %copy-start.5 = (f32[2,8,128]{2,1,0:T(8,128)}, f32[2,8,128]{2,1,0:T(8,128)S(1)}, u32[]{:S(2)}) copy-start(f32[2,8,128]{2,1,0:T(8,128)S(1)} %collective-permute-done.1.got_ref) | copy-start | bytes 24580
  58.6 0.6 copy-start
  61.8 16.5 %all-to-all-start.1 = ((bf16[8,14,8,128]{3,2,1,0:T(8,128)(2,1)}), bf16[8,14,8,128]{3,2,1,0:T(8,128)(2,1)S(1)}, u32[]{:S(2)}, u32[]{:S(2)}) async-start(bf16[8,14,8,128]{3,2,1,0:T(8,128)(2,1)} %shard_map.98), calls=%async_computation.1 | async-start | bytes 458752 | tf_op jit(solution)/shard_map/all_to_all | solution.py:281
  78.3 0.7 copy-start.1
  82.1 23.0 %all-to-all-start.2 = ((bf16[64,8,128]{2,1,0:T(8,128)(2,1)}), bf16[64,8,128]{2,1,0:T(8,128)(2,1)S(1)}, u32[]{:S(2)}, u32[]{:S(2)}) async-start(bf16[64,8,128]{2,1,0:T(8,128)(2,1)} %get-tuple-element.17), calls=%async_computation.2 | async-start | bytes 262144 | tf_op jit(solution)/shard_map/all_to_all | solution.py:299
  91.4 4.3 %collective-permute-start.3 = (f32[8,128]{1,0:T(8,128)}, f32[8,128]{1,0:T(8,128)S(1)}, u32[]{:S(2)}, u32[]{:S(2)}) collective-permute-start(f32[8,128]{1,0:T(8,128)} %get-tuple-element.18), channel_id=1, source_target_pairs={{0,64},{64,0},{128,192},{192,128},{256,320},{320,256},{384,448},{4... | collective-permute-start | bytes 12296 | tf_op jit(solution)/shard_map/ppermute | solution.py:298
  105.1 6.0 %copy-start.2 = (bf16[64,8,128]{2,1,0:T(8,128)(2,1)}, bf16[64,8,128]{2,1,0:T(8,128)(2,1)S(1)}, u32[]{:S(2)}) copy-start(bf16[64,8,128]{2,1,0:T(8,128)(2,1)S(1)} %all-to-all-done.2.own_ref) | copy-start | bytes 393220
  105.1 6.0 %collective-permute-start.2 = (bf16[64,8,128]{2,1,0:T(8,128)(2,1)S(1)}, bf16[64,8,128]{2,1,0:T(8,128)(2,1)S(1)}, u32[]{:S(2)}, u32[]{:S(2)}) collective-permute-start(bf16[64,8,128]{2,1,0:T(8,128)(2,1)S(1)} %all-to-all-done.2.own_ref), channel_id=1, source_target_pairs={{0,64},{64,0},{128,192},{192,128},{256,320},{320,256},{384,448},{4... | collective-permute-start | bytes 393224 | tf_op jit(solution)/shard_map/ppermute | solution.py:300
  111.1 0.7 copy-start.6

commit v2 on v1

v2 whole, which is shorter than its diff:
```python
import functools
import math

import jax
import jax.numpy as jnp
from jax import lax
from jax.experimental import pallas as pl
from jax.experimental.pallas import tpu as pltpu
from jax.sharding import PartitionSpec as P

BETA_ONE = 0.9
BETA_TWO = 0.95
EPSILON = 1e-08
LEARN_RATE = 0.25
LANES = 128
WIDE = 256
STEP = 1024
LONG_STEP = 2048
F32 = jnp.float32
BF16 = jnp.bfloat16


def parity_signs(left, right):
    both = jnp.bitwise_and(left, right)
    for shift in (4, 2, 1):
        both = jnp.bitwise_xor(both, jnp.right_shift(both, shift))
    return (1 - 2 * jnp.bitwise_and(both, 1)).astype(F32)


def iota(shape, dim):
    return lax.broadcasted_iota(jnp.int32, shape, dim)


def wide_rows(rows, first, count):
    return jnp.concatenate([rows[first + n : first + n + 1, :] for n in range(count)], axis=1)


def fill_low_table(ref, columns):
    count = 16
    shape = (count, columns.shape[1])
    fine = parity_signs(iota(shape, 0), columns)
    coarse = parity_signs(iota(shape, 0), jnp.right_shift(columns, 4))
    for n in range(ref.shape[0] // count):
        ref[n * count : (n + 1) * count, :] = (fine * coarse[n : n + 1, :]).astype(BF16)


def order_columns(half, kept):
    blocks = kept.shape[0]
    digits = jnp.concatenate([jnp.right_shift(kept, 7), jnp.bitwise_and(kept, LANES - 1)], axis=0)
    digits = digits.astype(F32).astype(BF16)
    source, target = iota((LANES, LANES), 0), iota((LANES, LANES), 1)
    same = jnp.logical_and(
        jnp.right_shift(source, 4) == jnp.bitwise_and(jnp.right_shift(target, 3), 7),
        jnp.bitwise_and(source, 7) == jnp.bitwise_and(target, 7),
    )
    source_half = jnp.bitwise_and(jnp.right_shift(source, 3), 1)
    pieces = []
    for wanted in (1 - half, half):
        moved = []
        for part in (0, 1):
            pick = jnp.logical_and(same, source_half == wanted)
            pick = jnp.logical_and(pick, jnp.right_shift(target, 6) == part)
            pick = jnp.where(pick, 1.0, 0.0).astype(BF16)
            moved.append(jnp.dot(digits, pick, preferred_element_type=F32))
        for pair in range(blocks // 2):
            even, odd = 2 * pair, 2 * pair + 1
            top = moved[0][even : even + 1, :] + moved[1][odd : odd + 1, :]
            low = (
                moved[0][blocks + even : blocks + even + 1, :]
                + moved[1][blocks + odd : blocks + odd + 1, :]
            )
            pieces.append(top * LANES + low)
    return jnp.concatenate(pieces, axis=1).astype(jnp.int32)


def project_half(scale, first, x_of, low_ref, high_ref, out_ref, acc_ref):
    rows, width = acc_ref.shape
    chunks = STEP // WIDE
    columns = slice(first, first + width)
    acc_ref[...] = jnp.zeros_like(acc_ref)

    def add(step, carry):
        x = x_of(step)
        stacked = jnp.concatenate([x[:, n * WIDE : (n + 1) * WIDE] for n in range(chunks)], axis=0)
        part = jnp.dot(stacked, low_ref[:, columns], preferred_element_type=F32)
        total = acc_ref[...]
        for n in range(chunks):
            sign = high_ref[pl.ds(step * chunks + n, 1), columns]
            total = total + part[n * rows : (n + 1) * rows, :] * sign
        acc_ref[...] = total
        return carry

    steps = high_ref.shape[0] // chunks
    lax.fori_loop(0, steps, add, 0)
    done = jnp.transpose(acc_ref[...] * scale)
    out_ref[...] = done.reshape(out_ref.shape).astype(out_ref.dtype)


def project_other_kernel(
    scale, place_ref, kept_ref, one_ref, two_ref, bits_ref, x_ref,
    low_ref, high_ref, send_ref, own_ref, signed_ref, out_ref, acc_ref, sems
):
    def fetch(step):
        lanes = pl.ds(pl.multiple_of(step * STEP, STEP), STEP)
        return pltpu.make_async_copy(x_ref.at[0, :, lanes], signed_ref.at[:, lanes], sems.at[step])

    for step in range(signed_ref.shape[1] // STEP):
        fetch(step).start()
    half = jnp.bitwise_and(place_ref[0], 1)
    columns = order_columns(half, kept_ref[...])
    fill_low_table(low_ref, columns)
    high_ref[...] = parity_signs(iota(high_ref.shape, 0), jnp.right_shift(columns, 8))
    for index, ref in enumerate((one_ref, two_ref)):
        upper, lower = ref[0:8, :], ref[8:16, :]
        blank = jnp.zeros_like(upper)
        for out, wanted in ((send_ref, 1 - half), (own_ref, half)):
            mine = jnp.where(wanted == 0, upper, lower)
            out[index] = jnp.where(
                half == 0,
                jnp.concatenate([mine, blank], axis=1),
                jnp.concatenate([blank, mine], axis=1),
            )

    def x_of(step):
        fetch(step).wait()
        lanes = pl.ds(pl.multiple_of(step * STEP, STEP), STEP)
        signs = (1 - 2 * bits_ref[pl.ds(step * (STEP // LANES), STEP // LANES), :]).astype(F32)
        x = signed_ref[:, lanes] * wide_rows(signs, 0, STEP // LANES).astype(BF16)
        signed_ref[:, lanes] = x
        return x

    project_half(scale, 0, x_of, low_ref, high_ref, out_ref, acc_ref)


def project_own_kernel(scale, signed_ref, low_ref, high_ref, out_ref, acc_ref):
    def x_of(step):
        return signed_ref[:, pl.ds(pl.multiple_of(step * STEP, STEP), STEP)]

    project_half(scale, acc_ref.shape[1], x_of, low_ref, high_ref, out_ref, acc_ref)


def row_tables_kernel(kept_ref, low_ref, high_ref):
    rows = wide_rows(kept_ref[...], 0, kept_ref.shape[0])
    fill_low_table(low_ref, rows)
    high_ref[...] = parity_signs(iota(high_ref.shape, 0), jnp.right_shift(rows, 8))


def row_turned_kernel(kept_ref, when_ref, turned_ref, high_ref, low_ref):
    row_tables_kernel(kept_ref, low_ref, high_ref)
    turned_ref[...] = jnp.transpose(low_ref[...].astype(F32)).astype(BF16)


def column_turned_kernel(place_ref, kept_ref, when_ref, turned_ref, high_ref, low_ref):
    columns = order_columns(jnp.bitwise_and(place_ref[0], 1), kept_ref[...])
    fill_low_table(low_ref, columns)
    high_ref[...] = parity_signs(iota(high_ref.shape, 0), jnp.right_shift(columns, 8))
    turned_ref[...] = jnp.transpose(low_ref[...].astype(F32)).astype(BF16)


def compress_kernel(scale, y_ref, bits_ref, low_ref, high_ref, own_ref, got_ref, out_ref, part_ref):
    panels, width, lanes = y_ref.shape
    signs = (1 - 2 * bits_ref[...]).astype(F32)
    y = (y_ref[...].astype(F32) * signs[:, None, :]).reshape(panels // 2, 2, width, lanes)
    y = jnp.concatenate([y[:, 0], y[:, 1]], axis=2).reshape(panels // 2 * width, 2 * lanes)
    part = jnp.dot(y.astype(BF16), low_ref[...], preferred_element_type=F32)
    part_ref[...] = part.reshape(part_ref.shape)

    def add(panel, total):
        return total + part_ref[panel] * high_ref[pl.ds(panel, 1), :]

    total = lax.fori_loop(0, panels // 2, add, jnp.zeros(part_ref.shape[1:], F32), unroll=8)
    total = (total * scale).astype(BF16)
    count = total.shape[1] // LANES
    pieces = [total[:, n * LANES : (n + 1) * LANES] for n in range(count)]
    for index in range(2):
        rest = own_ref[index] + got_ref[index]
        for _ in range(3):
            piece = rest.astype(BF16)
            pieces.append(piece)
            rest = rest - piece.astype(F32)
    for peer in range(out_ref.shape[0]):
        for n, piece in enumerate(pieces):
            out_ref[peer, n] = piece


def adam_kernel(
    scale, place_ref, fix_ref, got_ref, bits_ref, turned_ref, high_ref, back_ref, sum_ref, lhs_ref
):
    peers = got_ref.shape[0]
    mine = jnp.right_shift(place_ref[0], 1)
    first_fix, second_fix = fix_ref[0], fix_ref[1]
    tops, rests = [], []
    own = jnp.zeros(sum_ref.shape, F32)
    for n in range(peers):
        total = got_ref[0, n].astype(F32)
        for peer in range(1, peers):
            total = total + got_ref[peer, n].astype(F32)
        own = jnp.where(mine == n, total, own)
        one = got_ref[n, peers].astype(F32) + got_ref[n, peers + 1].astype(F32)
        one = one + got_ref[n, peers + 2].astype(F32)
        two = got_ref[n, peers + 3].astype(F32) + got_ref[n, peers + 4].astype(F32)
        two = two + got_ref[n, peers + 5].astype(F32)
        new_one = BETA_ONE * one + (1.0 - BETA_ONE) * total
        new_two = BETA_TWO * two + (1.0 - BETA_TWO) * total * total
        direction = new_one / first_fix / (jnp.sqrt(new_two / second_fix) + EPSILON)
        top = direction.astype(BF16).astype(F32)
        tops.append(top)
        rests.append(direction - top)
    sum_ref[...] = own
    both = jnp.concatenate([jnp.concatenate(tops, axis=1), jnp.concatenate(rests, axis=1)], axis=0)
    wides = lhs_ref.shape[0]

    def fill(wide, carry):
        lhs_ref[wide] = (both * high_ref[pl.ds(wide, 1), :]).astype(BF16)
        return carry

    lax.fori_loop(0, wides, fill, 0, unroll=8)
    lhs = lhs_ref[...].reshape(wides * lhs_ref.shape[1], lhs_ref.shape[2])
    back = jnp.dot(lhs, turned_ref[...], preferred_element_type=F32)
    back = back.reshape(wides, 2, back.shape[0] // wides // 2, WIDE)
    back = back[:, 0] + back[:, 1]
    back = jnp.stack([back[:, :, :LANES], back[:, :, LANES:]], axis=1).reshape(back_ref.shape)
    signs = (1 - 2 * bits_ref[...]).astype(F32) * scale
    back_ref[...] = (back * signs[:, None, :]).astype(BF16)


def expand_kernel(scale, other_ref, own_ref, turned_ref, high_ref, bits_ref, weight_ref, out_ref,
                  back_ref, lhs_ref):
    step = pl.program_id(0)
    rows = weight_ref.shape[0]
    stride = out_ref.shape[1]
    chunks = stride // WIDE

    @pl.when(step == 0)
    def _():
        for index, ref in enumerate((other_ref, own_ref)):
            half = ref.shape[0] * ref.shape[1]
            columns = ref[...].astype(F32).reshape(half, rows)
            back_ref[:, index * half : (index + 1) * half] = jnp.transpose(columns).astype(BF16)

    for chunk in range(chunks):
        sign = high_ref[pl.ds(step * chunks + chunk, 1), :].astype(BF16)
        lhs_ref[chunk * rows : (chunk + 1) * rows, :] = back_ref[...] * sign
    update = jnp.dot(lhs_ref[...], turned_ref[...], preferred_element_type=F32)
    tiles = stride // LANES
    signs = (1 - 2 * bits_ref[pl.ds(step * tiles, tiles), :]).astype(F32) * scale
    for chunk in range(chunks):
        lanes = pl.ds(pl.multiple_of(step * stride + chunk * WIDE, WIDE), WIDE)
        moved = update[chunk * rows : (chunk + 1) * rows, :] * wide_rows(signs, 2 * chunk, 2)
        moved = weight_ref[:, lanes].astype(F32) - moved
        out_ref[:, chunk * WIDE : (chunk + 1) * WIDE] = moved.astype(BF16)


def shaped(shape, dtype):
    return jax.ShapeDtypeStruct(shape, dtype)


SMEM = pl.BlockSpec(memory_space=pltpu.SMEM)
ROOM = pltpu.CompilerParams(vmem_limit_bytes=24 << 20)
VMEM = pl.BlockSpec(memory_space=pltpu.VMEM)


def cost(flops, moved):
    return pl.CostEstimate(flops=flops, bytes_accessed=moved, transcendentals=0)


def local(replica_grads, weight, moment_one, moment_two, sign_bits, kept_rows, step_count):
    reps, panels = lax.axis_size("rep"), lax.axis_size("fsdp")
    full_len, kept_len = sign_bits.shape[0], kept_rows.shape[0]
    rows = weight.shape[0]
    peers = reps // 2
    half_width = kept_len // panels // 2
    half_len = kept_len // 2
    norm_scale = 1.0 / math.sqrt(kept_len)
    place = lax.axis_index("rep").astype(jnp.int32).reshape(1)
    half = jnp.bitwise_and(place[0], 1)
    kept = kept_rows.reshape(kept_len // LANES, LANES)
    bits = sign_bits.reshape(full_len // LANES, LANES)
    one_t, two_t = moment_one.T, moment_two.T
    swap = [(n, n ^ 1) for n in range(reps)]
    wide_count = full_len // WIDE

    half_shape = (panels, half_width, rows)
    col_low, col_high, send_moments, own_moments, signed, for_other = pl.pallas_call(
        functools.partial(project_other_kernel, norm_scale),
        out_shape=(
            shaped((WIDE, kept_len), BF16),
            shaped((wide_count, kept_len), F32),
            shaped((2, half_width, LANES), F32),
            shaped((2, half_width, LANES), F32),
            shaped((rows, full_len), BF16),
            shaped(half_shape, BF16),
        ),
        in_specs=[SMEM] + [VMEM] * 4 + [pl.BlockSpec(memory_space=pltpu.HBM)],
        out_specs=(VMEM,) * 6,
        scratch_shapes=[
            pltpu.VMEM((rows, half_len), F32),
            pltpu.SemaphoreType.DMA((full_len // STEP,)),
        ],
        compiler_params=ROOM,
        cost_estimate=cost(2 * rows * full_len * half_len, 2 * rows * full_len),
    )(place, kept, one_t, two_t, bits, pltpu.with_memory_space_constraint(replica_grads, pltpu.HBM))
    from_other = lax.ppermute(for_other, "rep", swap)
    mine = pl.pallas_call(
        functools.partial(project_own_kernel, norm_scale),
        out_shape=shaped(half_shape, F32),
        in_specs=[VMEM] * 3,
        out_specs=VMEM,
        scratch_shapes=[pltpu.VMEM((rows, half_len), F32)],
        compiler_params=ROOM,
        cost_estimate=cost(2 * rows * full_len * half_len, 2 * rows * full_len),
    )(signed, col_low, col_high)
    got_moments = lax.ppermute(send_moments, "rep", swap)
    row_low, row_high = pl.pallas_call(
        row_tables_kernel,
        out_shape=(shaped((WIDE, kept_len), BF16), shaped((wide_count, kept_len), F32)),
        in_specs=[VMEM],
        out_specs=(VMEM,) * 2,
        compiler_params=ROOM,
        cost_estimate=cost(10 * LANES * kept_len, 8 * WIDE * kept_len),
    )(kept)

    def turned(kernel, smem, *operands):
        return pl.pallas_call(
            kernel,
            out_shape=(shaped((kept_len, WIDE), BF16), shaped((wide_count, kept_len), F32)),
            in_specs=[SMEM] * smem + [VMEM, pl.BlockSpec(memory_space=pl.ANY)],
            out_specs=(VMEM,) * 2,
            scratch_shapes=[pltpu.VMEM((WIDE, kept_len), BF16)],
            compiler_params=ROOM,
            cost_estimate=cost(10 * LANES * kept_len, 8 * WIDE * kept_len),
        )(*operands)

    columns = (mine + from_other.astype(F32)).astype(BF16)
    columns = lax.all_to_all(columns, "fsdp", 0, 0)

    message = pl.pallas_call(
        functools.partial(compress_kernel, norm_scale),
        out_shape=shaped((peers, kept_len // LANES + 6, half_width, LANES), BF16),
        in_specs=[VMEM] * 6,
        out_specs=VMEM,
        scratch_shapes=[pltpu.VMEM((panels // 2, half_width, kept_len), F32)],
        compiler_params=ROOM,
        cost_estimate=cost(2 * full_len * half_width * kept_len // panels, 2 * full_len * half_width),
    )(columns, bits, row_low, row_high, own_moments, got_moments)
    row_turned, row_high = turned(row_turned_kernel, 0, kept, message)
    groups = [list(range(core, reps, 2)) for core in (0, 1)]
    message = lax.all_to_all(message, "rep", 0, 0, axis_index_groups=groups)

    steps_done = step_count.astype(F32)
    fixes = jnp.stack(
        [1.0 - jnp.power(F32(BETA_ONE), steps_done), 1.0 - jnp.power(F32(BETA_TWO), steps_done)]
    )
    back, own_sum = pl.pallas_call(
        functools.partial(adam_kernel, norm_scale),
        out_shape=(
            shaped((panels, half_width, rows), BF16),
            shaped((half_width, LANES), F32),
        ),
        in_specs=[SMEM, SMEM] + [VMEM] * 4,
        out_specs=(VMEM,) * 2,
        scratch_shapes=[pltpu.VMEM((wide_count, 2 * half_width, kept_len), BF16)],
        compiler_params=ROOM,
        cost_estimate=cost(4 * full_len * half_width * kept_len, 2 * full_len * half_width),
    )(place, fixes, message, bits, row_turned, row_high)
    col_turned, col_high = turned(column_turned_kernel, 1, place, kept, back)
    other_sum = lax.ppermute(own_sum, "rep", swap)
    back = lax.all_to_all(back, "fsdp", 0, 0)
    other_back = lax.ppermute(back, "rep", swap)

    row_count = moment_one.shape[0]
    own_rows = jnp.where(half == 0, own_sum[:, :row_count], own_sum[:, row_count:])
    other_rows = jnp.where(half == 0, other_sum[:, :row_count], other_sum[:, row_count:])
    compressed = jnp.where(
        half == 0,
        jnp.concatenate([own_rows, other_rows], axis=0),
        jnp.concatenate([other_rows, own_rows], axis=0),
    )
    new_one = (BETA_ONE * one_t + (1.0 - BETA_ONE) * compressed).T
    new_two = (BETA_TWO * two_t + (1.0 - BETA_TWO) * compressed * compressed).T

    new_weight = pl.pallas_call(
        functools.partial(expand_kernel, LEARN_RATE * norm_scale),
        grid=(full_len // LONG_STEP,),
        out_shape=shaped(weight.shape, BF16),
        in_specs=[VMEM] * 6,
        out_specs=pl.BlockSpec((rows, LONG_STEP), lambda i: (0, i)),
        scratch_shapes=[
            pltpu.VMEM((rows, kept_len), BF16),
            pltpu.VMEM((rows * LONG_STEP // WIDE, kept_len), BF16),
        ],
        compiler_params=ROOM,
        cost_estimate=cost(2 * rows * full_len * kept_len, 4 * rows * full_len),
    )(other_back, back, col_turned, col_high, bits, weight)
    return (new_weight, new_one, new_two)


def solution(mesh):
    in_specs = (
        P("rep", "fsdp", None),
        P("fsdp", None),
        P("rep", "fsdp"),
        P("rep", "fsdp"),
        P(),
        P(),
        P(),
    )
    out_specs = (P("fsdp", None), P("rep", "fsdp"), P("rep", "fsdp"))
    return jax.shard_map(local, mesh=mesh, in_specs=in_specs, out_specs=out_specs, check_vma=False)
```

time: 121 us -> 104 us (0.86)
  Pallas kernels: 30.6 us -> 14 us
  other arithmetic: 3.83 us -> 1.52 us
  waiting for transfers between devices: 29.3 us -> 31.4 us
    pallas_call x4 -> x5, Pallas kernels: 17.1 us -> 7.03 us  [the longest x1 3.55 us: local(): pl.pallas_call(functools.partial(project_other_kernel, norm_scale), out_s...]
    pallas_call x1, Pallas kernels: 7.97 us -> 3.92 us  [local(): pl.pallas_call(functools.partial(expand_kernel, LEARN_RATE * norm_scale),...]
    pallas_call x1, Pallas kernels: 2.51 us -> 1.14 us  [local(): pl.pallas_call(functools.partial(compress_kernel, norm_scale), out_shape=...]
    unnamed x16 -> x18, local copies, waits for them, and re-layouts: 1.99 us -> 2.86 us
  transfers between devices with their start and end apart: 7 -> 7, of which waited for: 5 -> 6; matrix products, arithmetic and copies ran while one was open for 2% -> 1% of each run, Pallas kernels for 7% -> 3%
where the time goes in v2:
time: 104 us
  starting transfers between devices  52.5 us (50%)
  waiting for transfers between devices  31.4 us (30%)
  Pallas kernels  14 us (13%)
  local copies, waits for them, and re-layouts  2.86 us (3%)
  between operations  1.55 us (1%)
  other arithmetic  1.52 us (1%)
    ppermute x1, starting transfers between devices, local(): from_other = lax.ppermute(for_other, 'rep', swap)  16 us
    all_to_all x1, waiting for transfers between devices, local(): columns = lax.all_to_all(columns, 'fsdp', 0, 0)  11.9 us
    all_to_all x1, starting transfers between devices, local(): columns = lax.all_to_all(columns, 'fsdp', 0, 0)  9.92 us
    all_to_all x1, waiting for transfers between devices, local(): back = lax.all_to_all(back, 'fsdp', 0, 0)  9.45 us
    all_to_all x1, starting transfers between devices, local(): back = lax.all_to_all(back, 'fsdp', 0, 0)  9.38 us
    all_to_all x1, waiting for transfers between devices, local(): message = lax.all_to_all(message, 'rep', 0, 0, axis_index_groups=groups)  8.84 us
    all_to_all x1, starting transfers between devices, local(): message = lax.all_to_all(message, 'rep', 0, 0, axis_index_groups=groups)  6.58 us
    ppermute x1, starting transfers between devices, local(): other_back = lax.ppermute(back, 'rep', swap)  5.06 us
  transfers between devices with their start and end apart: 7, of which 6 were waited for; matrix products, arithmetic and copies ran while one was open for 1% of the time, Pallas kernels for 3%

profile of v2, /device:TPU:1, one launch (start us, length us, event | category | flops | bytes accessed | tf_op | source)
XLA Modules:
  0.0 103.8 jit_solution(12160418896503242844)
XLA Ops:
  0.6 0.0 copy-start
  0.6 0.7 copy-done
  1.4 0.7 copy-done.2
  2.1 0.7 copy-done.4
  2.8 0.7 copy-done.6
  3.5 3.5 %shard_map.94 = (bf16[256,1024]{1,0:T(8,128)(2,1)S(1)}, f32[32,1024]{1,0:T(8,128)S(1)}, f32[2,8,128]{2,1,0:T(8,128)S(1)}, f32[2,8,128]{2,1,0:T(8,128)S(1)}, bf16...) custom-call(s32[1]{0:T(128)} %bitcast.place_ref, s32[8,128]{1,0:T(8,128)S(1)} %bitcast.17, ...), custom_call_target="tpu_custom_call" | custom-call | flops 1073741824 | bytes 2097152 | tf_op jit(solution)/shard_map/pallas_call | solution.py:284
  7.0 16.0 %collective-permute-start = (bf16[64,8,128]{2,1,0:T(8,128)(2,1)S(1)}, bf16[64,8,128]{2,1,0:T(8,128)(2,1)S(1)}, u32[]{:S(2)}, u32[]{:S(2)}) collective-permute-start(bf16[64,8,128]{2,1,0:T(8,128)(2,1)S(1)} %get-tuple-element.20), channel_id=1, source_target_pairs={{0,64},{64,0},{128,192},{192,128},{256,320},{320,256},{384,448},{4... | collective-permute-start | bytes 393224 | tf_op jit(solution)/shard_map/ppermute | solution.py:303
  23.1 0.0 copy-start.3
  23.1 2.5 %shard_map.95 = f32[64,8,128]{2,1,0:T(8,128)S(1)} custom-call(bf16[128,8192]{1,0:T(8,128)(2,1)S(1)} %get-tuple-element.17.signed_ref, bf16[256,1024]{1,0:T(8,128)(2,1)S(1)} %get-tuple-element.18.low_ref, f32[32,1024]{1,0:T(8,128)S(1)} %get-tuple-element.19.high_ref), custom_call_target="tpu_custom_call" | custom-call | flops 1073741824 | bytes 2097152 | tf_op jit(solution)/shard_map/pallas_call | solution.py:304
  25.7 0.7 add_convert_fusion
  26.4 9.9 %all-to-all-start = ((bf16[64,8,128]{2,1,0:T(8,128)(2,1)}), bf16[64,8,128]{2,1,0:T(8,128)(2,1)S(1)}, u32[]{:S(2)}, u32[]{:S(2)}) async-start(bf16[64,8,128]{2,1,0:T(8,128)(2,1)} %add_convert_fusion), calls=%async_computation | async-start | bytes 262144 | tf_op jit(solution)/shard_map/all_to_all | solution.py:335
  36.3 2.2 %collective-permute-start.1 = (f32[2,8,128]{2,1,0:T(8,128)S(1)}, f32[2,8,128]{2,1,0:T(8,128)S(1)}, u32[]{:S(2)}, u32[]{:S(2)}) collective-permute-start(f32[2,8,128]{2,1,0:T(8,128)S(1)} %get-tuple-element.24), channel_id=1, source_target_pairs={{0,64},{64,0},{128,192},{192,128},{256,320},{320,256},{384,448},{4... | collective-permute-start | bytes 24584 | tf_op jit(solution)/shard_map/ppermute | solution.py:313
  38.6 0.2 shard_map.96
  38.7 0.7 collective-permute-done.1.got_ref
  39.4 11.9 %all-to-all-done.y_ref = bf16[64,8,128]{2,1,0:T(8,128)(2,1)S(1)} async-done(((bf16[64,8,128]{2,1,0:T(8,128)(2,1)}), bf16[64,8,128]{2,1,0:T(8,128)(2,1)S(1)}, u32[]{:S(2)}, u32[]{:S(2)}) %all-to-all-start) | async-done | bytes 131104 | tf_op jit(solution)/shard_map/all_to_all | solution.py:335
  51.2 1.1 %shard_map.97.when_ref = bf16[8,14,8,128]{3,2,1,0:T(8,128)(2,1)} custom-call(bf16[64,8,128]{2,1,0:T(8,128)(2,1)S(1)} %all-to-all-done.y_ref, s32[64,128]{1,0:T(8,128)S(1)} %bitcast.14, bf16[256,1024]{1,0:T(8,128)(2,1)S(1)} %get-tuple-element.21.low_ref, f32[32,1024]{1,0:T(8,128)S(1)} %get-tuple-element.22.high_ref, ...), custom_call_target="tpu_custom_call" | custom-call | flops 2097152 | bytes 131072 | tf_op jit(solution)/shard_map/pallas_call | solution.py:337
  52.4 6.6 %all-to-all-start.1 = ((bf16[8,14,8,128]{3,2,1,0:T(8,128)(2,1)}), bf16[8,14,8,128]{3,2,1,0:T(8,128)(2,1)S(1)}, u32[]{:S(2)}, u32[]{:S(2)}) async-start(bf16[8,14,8,128]{3,2,1,0:T(8,128)(2,1)} %shard_map.97.when_ref), calls=%async_computation.1 | async-start | bytes 458752 | tf_op jit(solution)/shard_map/all_to_all | solution.py:348
  59.7 0.1 pad_maximum_fusion.fix_ref
  59.8 0.3 shard_map.98
  60.1 8.8 %all-to-all-done.1.got_ref = bf16[8,14,8,128]{3,2,1,0:T(8,128)(2,1)S(1)} async-done(((bf16[8,14,8,128]{3,2,1,0:T(8,128)(2,1)}), bf16[8,14,8,128]{3,2,1,0:T(8,128)(2,1)S(1)}, u32[]{:S(2)}, u32[]{:S(2)}) %all-to-all-start.1) | async-done | bytes 229408 | tf_op jit(solution)/shard_map/all_to_all | solution.py:348
  68.9 1.9 %shard_map.99 = (bf16[64,8,128]{2,1,0:T(8,128)(2,1)}, f32[8,128]{1,0:T(8,128)S(1)}) custom-call(s32[1]{0:T(128)} %bitcast.place_ref, f32[2]{0:T(128)S(1)} %pad_maximum_fusion.fix_ref, bf16[8,14,8,128]{3,2,1,0:T(8,128)(2,1)S(1)} %all-to-all-done.1.got_ref, s32[64,128]{1,0:T(8,128)S(1)} %bitcast.15, bf16[1024,256]{1,0:T(8,128)(2,1)S(1)} %get-tuple-element.25.turned_ref, ...), custom_call_target="tpu_custom_call" | custom-call | flops 268435456 | bytes 131072 | tf_op jit(solution)/shard_map/pallas_call | solution.py:354
  70.8 9.4 %all-to-all-start.2 = ((bf16[64,8,128]{2,1,0:T(8,128)(2,1)}), bf16[64,8,128]{2,1,0:T(8,128)(2,1)S(1)}, u32[]{:S(2)}, u32[]{:S(2)}) async-start(bf16[64,8,128]{2,1,0:T(8,128)(2,1)} %get-tuple-element.27.when_ref), calls=%async_computation.2 | async-start | bytes 262144 | tf_op jit(solution)/shard_map/all_to_all | solution.py:368
  80.2 3.3 %collective-permute-start.3 = (f32[8,128]{1,0:T(8,128)S(1)}, f32[8,128]{1,0:T(8,128)S(1)}, u32[]{:S(2)}, u32[]{:S(2)}) collective-permute-start(f32[8,128]{1,0:T(8,128)S(1)} %get-tuple-element.30), channel_id=1, source_target_pairs={{0,64},{64,0},{128,192},{192,128},{256,320},{320,256},{384,448},{4... | collective-permute-start | bytes 12296 | tf_op jit(solution)/shard_map/ppermute | solution.py:367
  83.5 0.1 slice_select_fusion.1
  83.5 0.5 shard_map.100
  84.0 0.3 collective-permute-done.3
  84.3 0.1 slice_select_fusion
  84.3 9.5 %all-to-all-done.2.own_ref = bf16[64,8,128]{2,1,0:T(8,128)(2,1)S(1)} async-done(((bf16[64,8,128]{2,1,0:T(8,128)(2,1)}), bf16[64,8,128]{2,1,0:T(8,128)(2,1)S(1)}, u32[]{:S(2)}, u32[]{:S(2)}) %all-to-all-start.2) | async-done | bytes 131104 | tf_op jit(solution)/shard_map/all_to_all | solution.py:368
  93.8 5.1 %collective-permute-start.2 = (bf16[64,8,128]{2,1,0:T(8,128)(2,1)S(1)}, bf16[64,8,128]{2,1,0:T(8,128)(2,1)S(1)}, u32[]{:S(2)}, u32[]{:S(2)}) collective-permute-start(bf16[64,8,128]{2,1,0:T(8,128)(2,1)S(1)} %all-to-all-done.2.own_ref), channel_id=1, source_target_pairs={{0,64},{64,0},{128,192},{192,128},{256,320},{320,256},{384,448},{4... | collective-permute-start | bytes 393224 | tf_op jit(solution)/shard_map/ppermute | solution.py:369
  98.9 0.6 fusion.1
  99.5 0.3 collective-permute-done.2.other_ref
  99.8 3.9 %shard_map.101 = bf16[128,8192]{1,0:T(8,128)(2,1)} custom-call(bf16[64,8,128]{2,1,0:T(8,128)(2,1)S(1)} %collective-permute-done.2.other_ref, bf16[64,8,128]{2,1,0:T(8,128)(2,1)S(1)} %all-to-all-done.2.own_ref, bf16[1024,256]{1,0:T(8,128)(2,1)S(1)} %get-tuple-element.28.turned_ref, f32[32,1024]{1,0:T(8,128)S(1)} %get-tuple-element.29.high_ref, ...), custom_call_target="tpu_custom_call" | custom-call | flops 2147483648 | bytes 4194304 | tf_op jit(solution)/shard_map/pallas_call | solution.py:382
  (13 shorter events, 0.0 us)
Async XLA Ops:
  0.6 0.8 copy-start
  1.4 0.7 copy-start.2
  2.1 0.7 copy-start.4
  2.8 0.7 copy-start.6
  7.0 18.7 %collective-permute-start = (bf16[64,8,128]{2,1,0:T(8,128)(2,1)S(1)}, bf16[64,8,128]{2,1,0:T(8,128)(2,1)S(1)}, u32[]{:S(2)}, u32[]{:S(2)}) collective-permute-start(bf16[64,8,128]{2,1,0:T(8,128)(2,1)S(1)} %get-tuple-element.20), channel_id=1, source_target_pairs={{0,64},{64,0},{128,192},{192,128},{256,320},{320,256},{384,448},{4... | collective-permute-start | bytes 393224 | tf_op jit(solution)/shard_map/ppermute | solution.py:303
  23.1 15.5 %copy-start.3 = (s32[1024]{0:T(1024)S(1)}, s32[1024]{0:T(1024)}, u32[]{:S(2)}) copy-start(s32[1024]{0:T(1024)} %param.12) | copy-start | bytes 12292
  23.1 28.1 %copy-start.1 = (s32[8192]{0:T(1024)S(1)}, s32[8192]{0:T(1024)}, u32[]{:S(2)}) copy-start(s32[8192]{0:T(1024)} %param.11) | copy-start | bytes 98308
  25.7 73.2 %copy-start.5 = (f32[64,16]{0,1:T(8,128)S(1)}, f32[64,16]{0,1:T(8,128)}, u32[]{:S(2)}) copy-start(f32[64,16]{0,1:T(8,128)} %param.9) | copy-start | bytes 12292
  25.7 73.2 %copy-start.7 = (f32[64,16]{0,1:T(8,128)S(1)}, f32[64,16]{0,1:T(8,128)}, u32[]{:S(2)}) copy-start(f32[64,16]{0,1:T(8,128)} %param.10) | copy-start | bytes 12292
  25.7 74.1 %copy-start.8 = (bf16[128,8192]{1,0:T(8,128)(2,1)S(1)}, bf16[128,8192]{1,0:T(8,128)(2,1)}, u32[]{:S(2)}) copy-start(bf16[128,8192]{1,0:T(8,128)(2,1)} %weight_ref.1) | copy-start | bytes 6291460
  26.4 24.8 %all-to-all-start = ((bf16[64,8,128]{2,1,0:T(8,128)(2,1)}), bf16[64,8,128]{2,1,0:T(8,128)(2,1)S(1)}, u32[]{:S(2)}, u32[]{:S(2)}) async-start(bf16[64,8,128]{2,1,0:T(8,128)(2,1)} %add_convert_fusion), calls=%async_computation | async-start | bytes 262144 | tf_op jit(solution)/shard_map/all_to_all | solution.py:335
  36.3 3.1 %collective-permute-start.1 = (f32[2,8,128]{2,1,0:T(8,128)S(1)}, f32[2,8,128]{2,1,0:T(8,128)S(1)}, u32[]{:S(2)}, u32[]{:S(2)}) collective-permute-start(f32[2,8,128]{2,1,0:T(8,128)S(1)} %get-tuple-element.24), channel_id=1, source_target_pairs={{0,64},{64,0},{128,192},{192,128},{256,320},{320,256},{384,448},{4... | collective-permute-start | bytes 24584 | tf_op jit(solution)/shard_map/ppermute | solution.py:313
  52.4 16.5 %all-to-all-start.1 = ((bf16[8,14,8,128]{3,2,1,0:T(8,128)(2,1)}), bf16[8,14,8,128]{3,2,1,0:T(8,128)(2,1)S(1)}, u32[]{:S(2)}, u32[]{:S(2)}) async-start(bf16[8,14,8,128]{3,2,1,0:T(8,128)(2,1)} %shard_map.97.when_ref), calls=%async_computation.1 | async-start | bytes 458752 | tf_op jit(solution)/shard_map/all_to_all | solution.py:348
  70.8 23.0 %all-to-all-start.2 = ((bf16[64,8,128]{2,1,0:T(8,128)(2,1)}), bf16[64,8,128]{2,1,0:T(8,128)(2,1)S(1)}, u32[]{:S(2)}, u32[]{:S(2)}) async-start(bf16[64,8,128]{2,1,0:T(8,128)(2,1)} %get-tuple-element.27.when_ref), calls=%async_computation.2 | async-start | bytes 262144 | tf_op jit(solution)/shard_map/all_to_all | solution.py:368
  80.2 4.1 %collective-permute-start.3 = (f32[8,128]{1,0:T(8,128)S(1)}, f32[8,128]{1,0:T(8,128)S(1)}, u32[]{:S(2)}, u32[]{:S(2)}) collective-permute-start(f32[8,128]{1,0:T(8,128)S(1)} %get-tuple-element.30), channel_id=1, source_target_pairs={{0,64},{64,0},{128,192},{192,128},{256,320},{320,256},{384,448},{4... | collective-permute-start | bytes 12296 | tf_op jit(solution)/shard_map/ppermute | solution.py:367
  93.8 6.0 %collective-permute-start.2 = (bf16[64,8,128]{2,1,0:T(8,128)(2,1)S(1)}, bf16[64,8,128]{2,1,0:T(8,128)(2,1)S(1)}, u32[]{:S(2)}, u32[]{:S(2)}) collective-permute-start(bf16[64,8,128]{2,1,0:T(8,128)(2,1)S(1)} %all-to-all-done.2.own_ref), channel_id=1, source_target_pairs={{0,64},{64,0},{128,192},{192,128},{256,320},{320,256},{384,448},{4... | collective-permute-start | bytes 393224 | tf_op jit(solution)/shard_map/ppermute | solution.py:369

commit v3 on v2

v3 whole, which is shorter than its diff:
```python
import functools
import math

import jax
import jax.numpy as jnp
from jax import lax
from jax.experimental import pallas as pl
from jax.experimental.pallas import tpu as pltpu
from jax.sharding import PartitionSpec as P

BETA_ONE = 0.9
BETA_TWO = 0.95
EPSILON = 1e-08
LEARN_RATE = 0.25
LANES = 128
WIDE = 256
STEP = 1024
LONG_STEP = 2048
F32 = jnp.float32
BF16 = jnp.bfloat16


def parity_signs(left, right):
    both = jnp.bitwise_and(left, right)
    for shift in (4, 2, 1):
        both = jnp.bitwise_xor(both, jnp.right_shift(both, shift))
    return (1 - 2 * jnp.bitwise_and(both, 1)).astype(F32)


def iota(shape, dim):
    return lax.broadcasted_iota(jnp.int32, shape, dim)


def wide_rows(rows, first, count):
    return jnp.concatenate([rows[first + n : first + n + 1, :] for n in range(count)], axis=1)


def fill_low_table(ref, columns):
    count = 16
    shape = (count, columns.shape[1])
    fine = parity_signs(iota(shape, 0), columns)
    coarse = parity_signs(iota(shape, 0), jnp.right_shift(columns, 4))
    for n in range(ref.shape[0] // count):
        ref[n * count : (n + 1) * count, :] = (fine * coarse[n : n + 1, :]).astype(BF16)


def fill_tables(kept, low_ref, high_ref):
    rows = wide_rows(kept, 0, kept.shape[0])
    fill_low_table(low_ref, rows)
    high_ref[...] = parity_signs(iota(high_ref.shape, 0), jnp.right_shift(rows, 8))


def project_kernel(scale, kept_ref, bits_ref, x_ref, out_ref, low_ref, high_ref, raw_ref, acc_ref, sems):
    rows, width = acc_ref.shape
    chunks = STEP // WIDE
    tiles = STEP // LANES

    def fetch(step):
        lanes = pl.ds(pl.multiple_of(step * STEP, STEP), STEP)
        return pltpu.make_async_copy(x_ref.at[0, :, lanes], raw_ref.at[:, lanes], sems.at[step])

    steps = raw_ref.shape[1] // STEP
    for step in range(steps):
        fetch(step).start()
    fill_tables(kept_ref[...], low_ref, high_ref)
    acc_ref[...] = jnp.zeros_like(acc_ref)

    def add(step, carry):
        fetch(step).wait()
        signs = (1 - 2 * bits_ref[pl.ds(step * tiles, tiles), :]).astype(F32)
        pieces = []
        for n in range(chunks):
            lanes = pl.ds(pl.multiple_of(step * STEP + n * WIDE, WIDE), WIDE)
            pieces.append(raw_ref[:, lanes] * wide_rows(signs, 2 * n, 2).astype(BF16))
        stacked = jnp.concatenate(pieces, axis=0)
        for first in range(0, width, WIDE):
            columns = slice(first, first + WIDE)
            part = jnp.dot(stacked, low_ref[:, columns], preferred_element_type=F32)
            total = acc_ref[:, columns]
            for n in range(chunks):
                sign = high_ref[pl.ds(step * chunks + n, 1), columns]
                total = total + part[n * rows : (n + 1) * rows, :] * sign
            acc_ref[:, columns] = total
        return carry

    lax.fori_loop(0, steps, add, 0)
    done = jnp.transpose(acc_ref[...] * scale)
    out_ref[...] = done.reshape(out_ref.shape).astype(out_ref.dtype)


def tables_kernel(place_ref, kept_ref, one_ref, two_ref, when_ref, low_ref, high_ref, send_ref, own_ref):
    fill_tables(kept_ref[...], low_ref, high_ref)
    half = jnp.bitwise_and(place_ref[0], 1)
    for index, ref in enumerate((one_ref, two_ref)):
        upper, lower = ref[0:8, :], ref[8:16, :]
        blank = jnp.zeros_like(upper)
        for out, wanted in ((send_ref, 1 - half), (own_ref, half)):
            mine = jnp.where(wanted == 0, upper, lower)
            out[index] = jnp.where(
                half == 0,
                jnp.concatenate([mine, blank], axis=1),
                jnp.concatenate([blank, mine], axis=1),
            )


def turned_kernel(kept_ref, when_ref, turned_ref, high_ref, low_ref):
    fill_tables(kept_ref[...], low_ref, high_ref)
    turned_ref[...] = jnp.transpose(low_ref[...].astype(F32)).astype(BF16)


def compress_kernel(scale, y_ref, bits_ref, low_ref, high_ref, own_ref, got_ref, out_ref, part_ref):
    panels, lanes = bits_ref.shape
    width = y_ref.shape[0] * y_ref.shape[1] // panels
    signs = (1 - 2 * bits_ref[...]).astype(F32)
    y = y_ref[...].astype(F32).reshape(panels, width, lanes) * signs[:, None, :]
    y = y.reshape(panels // 2, 2, width, lanes)
    y = jnp.concatenate([y[:, 0], y[:, 1]], axis=2).reshape(panels // 2 * width, 2 * lanes)
    part = jnp.dot(y.astype(BF16), low_ref[...], preferred_element_type=F32)
    part_ref[...] = part.reshape(part_ref.shape)

    def add(panel, total):
        return total + part_ref[panel] * high_ref[pl.ds(panel, 1), :]

    total = lax.fori_loop(0, panels // 2, add, jnp.zeros(part_ref.shape[1:], F32), unroll=8)
    total = ((total[: width // 2] + total[width // 2 :]) * scale).astype(BF16)
    count = total.shape[1] // LANES
    pieces = [total[:, n * LANES : (n + 1) * LANES] for n in range(count)]
    for index in range(2):
        rest = own_ref[index] + got_ref[index]
        for _ in range(3):
            piece = rest.astype(BF16)
            pieces.append(piece)
            rest = rest - piece.astype(F32)
    for peer in range(out_ref.shape[0]):
        for n, piece in enumerate(pieces):
            out_ref[peer, n] = piece


def adam_kernel(
    scale, place_ref, fix_ref, got_ref, bits_ref, turned_ref, high_ref, back_ref, sum_ref, lhs_ref
):
    peers = got_ref.shape[0]
    mine = jnp.right_shift(place_ref[0], 1)
    first_fix, second_fix = fix_ref[0], fix_ref[1]
    tops, rests = [], []
    own = jnp.zeros(sum_ref.shape, F32)
    for n in range(peers):
        total = got_ref[0, n].astype(F32)
        for peer in range(1, peers):
            total = total + got_ref[peer, n].astype(F32)
        own = jnp.where(mine == n, total, own)
        one = got_ref[n, peers].astype(F32) + got_ref[n, peers + 1].astype(F32)
        one = one + got_ref[n, peers + 2].astype(F32)
        two = got_ref[n, peers + 3].astype(F32) + got_ref[n, peers + 4].astype(F32)
        two = two + got_ref[n, peers + 5].astype(F32)
        new_one = BETA_ONE * one + (1.0 - BETA_ONE) * total
        new_two = BETA_TWO * two + (1.0 - BETA_TWO) * total * total
        direction = new_one / first_fix / (jnp.sqrt(new_two / second_fix) + EPSILON)
        top = direction.astype(BF16).astype(F32)
        tops.append(top)
        rests.append(direction - top)
    sum_ref[...] = own
    both = jnp.concatenate([jnp.concatenate(tops, axis=1), jnp.concatenate(rests, axis=1)], axis=0)
    wides = lhs_ref.shape[0]

    def fill(wide, carry):
        lhs_ref[wide] = (both * high_ref[pl.ds(wide, 1), :]).astype(BF16)
        return carry

    lax.fori_loop(0, wides, fill, 0, unroll=8)
    lhs = lhs_ref[...].reshape(wides * lhs_ref.shape[1], lhs_ref.shape[2])
    back = jnp.dot(lhs, turned_ref[...], preferred_element_type=F32)
    back = back.reshape(wides, 2, back.shape[0] // wides // 2, WIDE)
    back = back[:, 0] + back[:, 1]
    back = jnp.stack([back[:, :, :LANES], back[:, :, LANES:]], axis=1)
    back = back.reshape(2 * wides, back.shape[2], LANES)
    signs = (1 - 2 * bits_ref[...]).astype(F32) * scale
    back = (back * signs[:, None, :]).astype(BF16)
    for core in range(2):
        back_ref[:, core] = back


def expand_kernel(scale, columns_ref, turned_ref, high_ref, bits_ref, weight_ref, out_ref,
                  back_ref, lhs_ref):
    step = pl.program_id(0)
    rows = weight_ref.shape[0]
    stride = out_ref.shape[1]
    chunks = stride // WIDE

    @pl.when(step == 0)
    def _():
        columns = columns_ref[...].astype(F32).reshape(back_ref.shape[1], rows)
        back_ref[...] = jnp.transpose(columns).astype(BF16)

    for chunk in range(chunks):
        sign = high_ref[pl.ds(step * chunks + chunk, 1), :].astype(BF16)
        lhs_ref[chunk * rows : (chunk + 1) * rows, :] = back_ref[...] * sign
    update = jnp.dot(lhs_ref[...], turned_ref[...], preferred_element_type=F32)
    tiles = stride // LANES
    signs = (1 - 2 * bits_ref[pl.ds(step * tiles, tiles), :]).astype(F32) * scale
    for chunk in range(chunks):
        lanes = pl.ds(pl.multiple_of(step * stride + chunk * WIDE, WIDE), WIDE)
        moved = update[chunk * rows : (chunk + 1) * rows, :] * wide_rows(signs, 2 * chunk, 2)
        moved = weight_ref[:, lanes].astype(F32) - moved
        out_ref[:, chunk * WIDE : (chunk + 1) * WIDE] = moved.astype(BF16)


def shaped(shape, dtype):
    return jax.ShapeDtypeStruct(shape, dtype)


SMEM = pl.BlockSpec(memory_space=pltpu.SMEM)
ROOM = pltpu.CompilerParams(vmem_limit_bytes=24 << 20)
VMEM = pl.BlockSpec(memory_space=pltpu.VMEM)


def cost(flops, moved):
    return pl.CostEstimate(flops=flops, bytes_accessed=moved, transcendentals=0)


def local(replica_grads, weight, moment_one, moment_two, sign_bits, kept_rows, step_count):
    reps, panels = lax.axis_size("rep"), lax.axis_size("fsdp")
    full_len, kept_len = sign_bits.shape[0], kept_rows.shape[0]
    rows = weight.shape[0]
    peers = reps // 2
    half_width = kept_len // panels // 2
    norm_scale = 1.0 / math.sqrt(kept_len)
    place = lax.axis_index("rep").astype(jnp.int32).reshape(1)
    half = jnp.bitwise_and(place[0], 1)
    kept = kept_rows.reshape(kept_len // LANES, LANES)
    bits = sign_bits.reshape(full_len // LANES, LANES)
    one_t, two_t = moment_one.T, moment_two.T
    swap = [(n, n ^ 1) for n in range(reps)]
    wide_count = full_len // WIDE
    low_table, high_table = shaped((WIDE, kept_len), BF16), shaped((wide_count, kept_len), F32)
    half_moments = shaped((2, half_width, LANES), F32)
    everywhere = pl.BlockSpec(memory_space=pl.ANY)
    chips = [
        [(2 * chip + core) * panels + panel for panel in range(panels) for core in (0, 1)]
        for chip in range(peers)
    ]
    cores = [list(range(core, reps, 2)) for core in (0, 1)]

    def turn(when):
        return pl.pallas_call(
            turned_kernel,
            out_shape=(shaped((kept_len, WIDE), BF16), high_table),
            in_specs=[VMEM, everywhere],
            out_specs=(VMEM,) * 2,
            scratch_shapes=[pltpu.VMEM(low_table.shape, BF16)],
            compiler_params=ROOM,
            cost_estimate=cost(10 * LANES * kept_len, 8 * WIDE * kept_len),
        )(kept, when)

    def regroup(blocks):
        return lax.all_to_all(
            blocks, ("rep", "fsdp"), 0, 0, axis_index_groups=chips, tiled=True
        )

    columns = pl.pallas_call(
        functools.partial(project_kernel, norm_scale),
        out_shape=shaped((2 * panels, half_width, rows), BF16),
        in_specs=[VMEM, VMEM, pl.BlockSpec(memory_space=pltpu.HBM)],
        out_specs=VMEM,
        scratch_shapes=[
            pltpu.VMEM(low_table.shape, BF16),
            pltpu.VMEM(high_table.shape, F32),
            pltpu.VMEM((rows, full_len), BF16),
            pltpu.VMEM((rows, kept_len), F32),
            pltpu.SemaphoreType.DMA((full_len // STEP,)),
        ],
        compiler_params=ROOM,
        cost_estimate=cost(2 * rows * full_len * kept_len, 2 * rows * full_len),
    )(*(pltpu.with_memory_space_constraint(x, pltpu.HBM) for x in (kept, bits, replica_grads)))
    low, high, send_moments, own_moments = pl.pallas_call(
        tables_kernel,
        out_shape=(low_table, high_table, half_moments, half_moments),
        in_specs=[SMEM] + [VMEM] * 3 + [everywhere],
        out_specs=(VMEM,) * 4,
        compiler_params=ROOM,
        cost_estimate=cost(10 * LANES * kept_len, 8 * WIDE * kept_len),
    )(place, kept, one_t, two_t, columns)
    got_moments = lax.ppermute(send_moments, "rep", swap)
    columns = regroup(columns)

    message = pl.pallas_call(
        functools.partial(compress_kernel, norm_scale),
        out_shape=shaped((peers, kept_len // LANES + 6, half_width, LANES), BF16),
        in_specs=[VMEM] * 6,
        out_specs=VMEM,
        scratch_shapes=[pltpu.VMEM((panels // 2, 2 * half_width, kept_len), F32)],
        compiler_params=ROOM,
        cost_estimate=cost(2 * full_len * half_width * kept_len // panels, 2 * full_len * half_width),
    )(columns, bits, low, high, own_moments, got_moments)
    turned, high = turn(message)
    message = lax.all_to_all(message, "rep", 0, 0, axis_index_groups=cores)

    steps_done = step_count.astype(F32)
    fixes = jnp.stack(
        [1.0 - jnp.power(F32(BETA_ONE), steps_done), 1.0 - jnp.power(F32(BETA_TWO), steps_done)]
    )
    back, own_sum = pl.pallas_call(
        functools.partial(adam_kernel, norm_scale),
        out_shape=(
            shaped((panels, 2, half_width, rows), BF16),
            shaped((half_width, LANES), F32),
        ),
        in_specs=[SMEM, SMEM] + [VMEM] * 4,
        out_specs=(VMEM,) * 2,
        scratch_shapes=[pltpu.VMEM((wide_count, 2 * half_width, kept_len), BF16)],
        compiler_params=ROOM,
        cost_estimate=cost(4 * full_len * half_width * kept_len, 2 * full_len * half_width),
    )(place, fixes, message, bits, turned, high)
    turned, high = turn(back)
    other_sum = lax.ppermute(own_sum, "rep", swap)
    back = regroup(back.reshape(2 * panels, half_width, rows))

    row_count = moment_one.shape[0]
    own_rows = jnp.where(half == 0, own_sum[:, :row_count], own_sum[:, row_count:])
    other_rows = jnp.where(half == 0, other_sum[:, :row_count], other_sum[:, row_count:])
    compressed = jnp.where(
        half == 0,
        jnp.concatenate([own_rows, other_rows], axis=0),
        jnp.concatenate([other_rows, own_rows], axis=0),
    )
    new_one = (BETA_ONE * one_t + (1.0 - BETA_ONE) * compressed).T
    new_two = (BETA_TWO * two_t + (1.0 - BETA_TWO) * compressed * compressed).T

    new_weight = pl.pallas_call(
        functools.partial(expand_kernel, LEARN_RATE * norm_scale),
        grid=(full_len // LONG_STEP,),
        out_shape=shaped(weight.shape, BF16),
        in_specs=[VMEM] * 5,
        out_specs=pl.BlockSpec((rows, LONG_STEP), lambda i: (0, i)),
        scratch_shapes=[
            pltpu.VMEM((rows, kept_len), BF16),
            pltpu.VMEM((rows * LONG_STEP // WIDE, kept_len), BF16),
        ],
        compiler_params=ROOM,
        cost_estimate=cost(2 * rows * full_len * kept_len, 4 * rows * full_len),
    )(back, turned, high, bits, weight)
    return (new_weight, new_one, new_two)


def solution(mesh):
    in_specs = (
        P("rep", "fsdp", None),
        P("fsdp", None),
        P("rep", "fsdp"),
        P("rep", "fsdp"),
        P(),
        P(),
        P(),
    )
    out_specs = (P("fsdp", None), P("rep", "fsdp"), P("rep", "fsdp"))
    return jax.shard_map(local, mesh=mesh, in_specs=in_specs, out_specs=out_specs, check_vma=False)
```

time: 104 us -> 111 us (1.067)
  waiting for transfers between devices: 31.4 us -> 47.7 us
  starting transfers between devices: 52.5 us -> 46.3 us
  local copies, waits for them, and re-layouts: 2.86 us -> 0.02 us
    ppermute x2 -> x0, starting transfers between devices: 21.1 us -> none  [the longest x1 16 us: local(): from_other = lax.ppermute(for_other, 'rep', swap)]
    all_to_all x3, waiting for transfers between devices: 30.1 us -> 46.5 us  [the longest x2 37.7 us: regroup(): lax.all_to_all(blocks, ('rep', 'fsdp'), 0, 0, axis_index_groups=chips, ti...]
    all_to_all x3, starting transfers between devices: 25.9 us -> 40.6 us  [the longest x2 34 us: regroup(): lax.all_to_all(blocks, ('rep', 'fsdp'), 0, 0, axis_index_groups=chips, ti...]
    unnamed x18 -> x10, local copies, waits for them, and re-layouts: 2.86 us -> 0.02 us
    pallas_call x5 -> x4, Pallas kernels: 7.03 us -> 7.05 us  [the longest x1 6.25 us: local(): pl.pallas_call(functools.partial(project_kernel, norm_scale), out_shape=s...]
  transfers between devices with their start and end apart: 7 -> 5, of which waited for: 6 -> 5; matrix products, arithmetic and copies ran while one was open for 1% -> 1% of each run, Pallas kernels for 3% -> 1%
where the time goes in v3:
time: 111 us
  waiting for transfers between devices  47.7 us (43%)
  starting transfers between devices  46.3 us (42%)
  Pallas kernels  14.2 us (13%)
  between operations  1.5 us (1%)
    all_to_all x2, waiting for transfers between devices, regroup(): lax.all_to_all(blocks, ('rep', 'fsdp'), 0, 0, axis_index_groups=chips, ti...  37.7 us
    all_to_all x2, starting transfers between devices, regroup(): lax.all_to_all(blocks, ('rep', 'fsdp'), 0, 0, axis_index_groups=chips, ti...  34 us
    all_to_all x1, waiting for transfers between devices, local(): message = lax.all_to_all(message, 'rep', 0, 0, axis_index_groups=cores)  8.83 us
    all_to_all x1, starting transfers between devices, local(): message = lax.all_to_all(message, 'rep', 0, 0, axis_index_groups=cores)  6.59 us
    pallas_call x1, Pallas kernels, local(): pl.pallas_call(functools.partial(project_kernel, norm_scale), out_shape=s...  6.25 us
    pallas_call x1, Pallas kernels, local(): pl.pallas_call(functools.partial(expand_kernel, LEARN_RATE * norm_scale),...  3.92 us
    ppermute x1, starting transfers between devices, local(): got_moments = lax.ppermute(send_moments, 'rep', swap)  2.93 us
    ppermute x1, starting transfers between devices, local(): other_sum = lax.ppermute(own_sum, 'rep', swap)  2.8 us
  transfers between devices with their start and end apart: 5, of which 5 were waited for; matrix products, arithmetic and copies ran while one was open for 1% of the time, Pallas kernels for 1%

profile of v3, /device:TPU:1, one launch (start us, length us, event | category | flops | bytes accessed | tf_op | source)
XLA Modules:
  0.0 110.7 jit_solution(10192531923330305447)
XLA Ops:
  0.6 0.0 copy-start
  0.6 0.0 copy-start.2
  0.7 0.0 copy-start.3
  0.7 0.0 copy-start.1
  0.7 6.3 %shard_map.94.when_ref = bf16[128,8,128]{2,1,0:T(8,128)(2,1)} custom-call(s32[8,128]{1,0:T(8,128)} %bitcast.14, s32[64,128]{1,0:T(8,128)} %bitcast.18, bf16[1,128,8192]{2,1,0:T(8,128)(2,1)} %x_ref.1), custom_call_target="tpu_custom_call" | custom-call | flops 2147483648 | bytes 2097152 | tf_op jit(solution)/shard_map/pallas_call | solution.py:260
  6.9 24.6 %all-to-all-start = ((bf16[128,8,128]{2,1,0:T(8,128)(2,1)}), bf16[128,8,128]{2,1,0:T(8,128)(2,1)S(1)}, u32[]{:S(2)}, u32[]{:S(2)}) async-start(bf16[128,8,128]{2,1,0:T(8,128)(2,1)} %shard_map.94.when_ref), calls=%async_computation | async-start | bytes 524288 | tf_op jit(solution)/shard_map/all_to_all | solution.py:256
  31.6 0.0 copy-start.4
  31.6 0.0 copy-done
  31.6 0.0 copy-done.2
  31.6 0.0 copy-done.3
  31.6 0.2 shard_map.95
  31.8 2.9 %collective-permute-start = (f32[2,8,128]{2,1,0:T(8,128)S(1)}, f32[2,8,128]{2,1,0:T(8,128)S(1)}, u32[]{:S(2)}, u32[]{:S(2)}) collective-permute-start(f32[2,8,128]{2,1,0:T(8,128)S(1)} %get-tuple-element.16), channel_id=1, source_target_pairs={{0,64},{64,0},{128,192},{192,128},{256,320},{320,256},{384,448},{4... | collective-permute-start | bytes 24584 | tf_op jit(solution)/shard_map/ppermute | solution.py:283
  34.8 0.8 collective-permute-done.got_ref
  35.6 19.0 %all-to-all-done.y_ref = bf16[128,8,128]{2,1,0:T(8,128)(2,1)S(1)} async-done(((bf16[128,8,128]{2,1,0:T(8,128)(2,1)}), bf16[128,8,128]{2,1,0:T(8,128)(2,1)S(1)}, u32[]{:S(2)}, u32[]{:S(2)}) %all-to-all-start) | async-done | bytes 262176 | tf_op jit(solution)/shard_map/all_to_all | solution.py:256
  54.6 0.0 copy-done.1
  54.6 1.3 %shard_map.96.when_ref = bf16[8,14,8,128]{3,2,1,0:T(8,128)(2,1)} custom-call(bf16[128,8,128]{2,1,0:T(8,128)(2,1)S(1)} %all-to-all-done.y_ref, s32[64,128]{1,0:T(8,128)S(1)} %bitcast.19, bf16[256,1024]{1,0:T(8,128)(2,1)S(1)} %get-tuple-element.13.low_ref, f32[32,1024]{1,0:T(8,128)S(1)} %get-tuple-element.14.high_ref, ...), custom_call_target="tpu_custom_call" | custom-call | flops 2097152 | bytes 131072 | tf_op jit(solution)/shard_map/pallas_call | solution.py:286
  55.9 6.6 %all-to-all-start.1 = ((bf16[8,14,8,128]{3,2,1,0:T(8,128)(2,1)}), bf16[8,14,8,128]{3,2,1,0:T(8,128)(2,1)S(1)}, u32[]{:S(2)}, u32[]{:S(2)}) async-start(bf16[8,14,8,128]{3,2,1,0:T(8,128)(2,1)} %shard_map.96.when_ref), calls=%async_computation.1 | async-start | bytes 458752 | tf_op jit(solution)/shard_map/all_to_all | solution.py:296
  63.2 0.1 pad_maximum_fusion.fix_ref
  63.3 0.3 shard_map.97
  63.6 8.8 %all-to-all-done.1.got_ref = bf16[8,14,8,128]{3,2,1,0:T(8,128)(2,1)S(1)} async-done(((bf16[8,14,8,128]{3,2,1,0:T(8,128)(2,1)}), bf16[8,14,8,128]{3,2,1,0:T(8,128)(2,1)S(1)}, u32[]{:S(2)}, u32[]{:S(2)}) %all-to-all-start.1) | async-done | bytes 229408 | tf_op jit(solution)/shard_map/all_to_all | solution.py:296
  72.5 1.9 %shard_map.98 = (bf16[64,2,8,128]{3,2,1,0:T(8,128)(2,1)}, f32[8,128]{1,0:T(8,128)S(1)}) custom-call(s32[1]{0:T(128)} %bitcast.place_ref, f32[2]{0:T(128)S(1)} %pad_maximum_fusion.fix_ref, bf16[8,14,8,128]{3,2,1,0:T(8,128)(2,1)S(1)} %all-to-all-done.1.got_ref, s32[64,128]{1,0:T(8,128)S(1)} %bitcast.20, bf16[1024,256]{1,0:T(8,128)(2,1)S(1)} %get-tuple-element.17.turned_ref, ...), custom_call_target="tpu_custom_call" | custom-call | flops 268435456 | bytes 131072 | tf_op jit(solution)/shard_map/pallas_call | solution.py:302
  74.4 9.4 %all-to-all-start.2 = ((bf16[128,8,128]{2,1,0:T(8,128)(2,1)}), bf16[128,8,128]{2,1,0:T(8,128)(2,1)S(1)}, u32[]{:S(2)}, u32[]{:S(2)}) async-start(bf16[128,8,128]{2,1,0:T(8,128)(2,1)} %bitcast.7), calls=%async_computation.2 | async-start | bytes 524288 | tf_op jit(solution)/shard_map/all_to_all | solution.py:256
  83.8 2.8 %collective-permute-start.1 = (f32[8,128]{1,0:T(8,128)S(1)}, f32[8,128]{1,0:T(8,128)S(1)}, u32[]{:S(2)}, u32[]{:S(2)}) collective-permute-start(f32[8,128]{1,0:T(8,128)S(1)} %get-tuple-element.22), channel_id=1, source_target_pairs={{0,64},{64,0},{128,192},{192,128},{256,320},{320,256},{384,448},{4... | collective-permute-start | bytes 12296 | tf_op jit(solution)/shard_map/ppermute | solution.py:315
  86.6 0.1 slice_select_fusion.1
  86.7 0.3 shard_map.99
  87.0 0.4 collective-permute-done.1
  87.4 0.1 slice_select_fusion
  87.5 0.6 fusion.1
  88.1 18.7 %all-to-all-done.2.columns_ref = bf16[128,8,128]{2,1,0:T(8,128)(2,1)S(1)} async-done(((bf16[128,8,128]{2,1,0:T(8,128)(2,1)}), bf16[128,8,128]{2,1,0:T(8,128)(2,1)S(1)}, u32[]{:S(2)}, u32[]{:S(2)}) %all-to-all-start.2) | async-done | bytes 262176 | tf_op jit(solution)/shard_map/all_to_all | solution.py:256
  106.7 0.0 copy-done.4
  106.7 3.9 %shard_map.100 = bf16[128,8192]{1,0:T(8,128)(2,1)} custom-call(bf16[128,8,128]{2,1,0:T(8,128)(2,1)S(1)} %all-to-all-done.2.columns_ref, bf16[1024,256]{1,0:T(8,128)(2,1)S(1)} %get-tuple-element.20.turned_ref, f32[32,1024]{1,0:T(8,128)S(1)} %get-tuple-element.21.high_ref, s32[64,128]{1,0:T(8,128)S(1)} %bitcast.21, bf16[128,8192]{1,0:T(8,128)(2,1)S(1)} %copy-done.4), custom_call_target="tpu_custom_call" | custom-call | flops 2147483648 | bytes 4194304 | tf_op jit(solution)/shard_map/pallas_call | solution.py:329
Async XLA Ops:
  0.6 31.0 %copy-start = (s32[1024]{0:T(1024)S(1)}, s32[1024]{0:T(1024)}, u32[]{:S(2)}) copy-start(s32[1024]{0:T(1024)} %param.12) | copy-start | bytes 12292
  0.6 31.0 %copy-start.2 = (f32[64,16]{0,1:T(8,128)S(1)}, f32[64,16]{0,1:T(8,128)}, u32[]{:S(2)}) copy-start(f32[64,16]{0,1:T(8,128)} %param.9) | copy-start | bytes 12292
  0.7 31.0 %copy-start.3 = (f32[64,16]{0,1:T(8,128)S(1)}, f32[64,16]{0,1:T(8,128)}, u32[]{:S(2)}) copy-start(f32[64,16]{0,1:T(8,128)} %param.10) | copy-start | bytes 12292
  0.7 53.9 %copy-start.1 = (s32[8192]{0:T(1024)S(1)}, s32[8192]{0:T(1024)}, u32[]{:S(2)}) copy-start(s32[8192]{0:T(1024)} %param.11) | copy-start | bytes 98308
  6.9 47.6 %all-to-all-start = ((bf16[128,8,128]{2,1,0:T(8,128)(2,1)}), bf16[128,8,128]{2,1,0:T(8,128)(2,1)S(1)}, u32[]{:S(2)}, u32[]{:S(2)}) async-start(bf16[128,8,128]{2,1,0:T(8,128)(2,1)} %shard_map.94.when_ref), calls=%async_computation | async-start | bytes 524288 | tf_op jit(solution)/shard_map/all_to_all | solution.py:256
  31.6 75.2 %copy-start.4 = (bf16[128,8192]{1,0:T(8,128)(2,1)S(1)}, bf16[128,8192]{1,0:T(8,128)(2,1)}, u32[]{:S(2)}) copy-start(bf16[128,8192]{1,0:T(8,128)(2,1)} %weight_ref.1) | copy-start | bytes 6291460
  31.8 3.7 %collective-permute-start = (f32[2,8,128]{2,1,0:T(8,128)S(1)}, f32[2,8,128]{2,1,0:T(8,128)S(1)}, u32[]{:S(2)}, u32[]{:S(2)}) collective-permute-start(f32[2,8,128]{2,1,0:T(8,128)S(1)} %get-tuple-element.16), channel_id=1, source_target_pairs={{0,64},{64,0},{128,192},{192,128},{256,320},{320,256},{384,448},{4... | collective-permute-start | bytes 24584 | tf_op jit(solution)/shard_map/ppermute | solution.py:283
  55.9 16.5 %all-to-all-start.1 = ((bf16[8,14,8,128]{3,2,1,0:T(8,128)(2,1)}), bf16[8,14,8,128]{3,2,1,0:T(8,128)(2,1)S(1)}, u32[]{:S(2)}, u32[]{:S(2)}) async-start(bf16[8,14,8,128]{3,2,1,0:T(8,128)(2,1)} %shard_map.96.when_ref), calls=%async_computation.1 | async-start | bytes 458752 | tf_op jit(solution)/shard_map/all_to_all | solution.py:296
  74.4 32.4 %all-to-all-start.2 = ((bf16[128,8,128]{2,1,0:T(8,128)(2,1)}), bf16[128,8,128]{2,1,0:T(8,128)(2,1)S(1)}, u32[]{:S(2)}, u32[]{:S(2)}) async-start(bf16[128,8,128]{2,1,0:T(8,128)(2,1)} %bitcast.7), calls=%async_computation.2 | async-start | bytes 524288 | tf_op jit(solution)/shard_map/all_to_all | solution.py:256
  83.8 3.6 %collective-permute-start.1 = (f32[8,128]{1,0:T(8,128)S(1)}, f32[8,128]{1,0:T(8,128)S(1)}, u32[]{:S(2)}, u32[]{:S(2)}) collective-permute-start(f32[8,128]{1,0:T(8,128)S(1)} %get-tuple-element.22), channel_id=1, source_target_pairs={{0,64},{64,0},{128,192},{192,128},{256,320},{320,256},{384,448},{4... | collective-permute-start | bytes 12296 | tf_op jit(solution)/shard_map/ppermute | solution.py:315

commit v4 on v3

v4 whole, which is shorter than its diff:
```python
import functools
import math

import jax
import jax.numpy as jnp
from jax import lax
from jax.experimental import pallas as pl
from jax.experimental.pallas import tpu as pltpu
from jax.sharding import PartitionSpec as P

BETA_ONE = 0.9
BETA_TWO = 0.95
EPSILON = 1e-08
LEARN_RATE = 0.25
LANES = 128
WIDE = 256
STEP = 1024
LONG_STEP = 2048
SIDE = 4
F32 = jnp.float32
BF16 = jnp.bfloat16


def parity_signs(left, right):
    both = jnp.bitwise_and(left, right)
    for shift in (4, 2, 1):
        both = jnp.bitwise_xor(both, jnp.right_shift(both, shift))
    return (1 - 2 * jnp.bitwise_and(both, 1)).astype(F32)


def iota(shape, dim):
    return lax.broadcasted_iota(jnp.int32, shape, dim)


def wide_rows(rows, first, count):
    return jnp.concatenate([rows[first + n : first + n + 1, :] for n in range(count)], axis=1)


def fill_low_table(ref, columns):
    count = 16
    shape = (count, columns.shape[1])
    fine = parity_signs(iota(shape, 0), columns)
    coarse = parity_signs(iota(shape, 0), jnp.right_shift(columns, 4))
    for n in range(ref.shape[0] // count):
        ref[n * count : (n + 1) * count, :] = (fine * coarse[n : n + 1, :]).astype(BF16)


def fill_tables(kept, low_ref, high_ref):
    rows = wide_rows(kept, 0, kept.shape[0])
    fill_low_table(low_ref, rows)
    high_ref[...] = parity_signs(iota(high_ref.shape, 0), jnp.right_shift(rows, 8))


def project_kernel(scale, kept_ref, bits_ref, x_ref, out_ref, low_ref, high_ref, raw_ref, acc_ref, sems):
    rows, width = acc_ref.shape
    chunks = STEP // WIDE
    tiles = STEP // LANES

    def fetch(step):
        lanes = pl.ds(pl.multiple_of(step * STEP, STEP), STEP)
        return pltpu.make_async_copy(x_ref.at[0, :, lanes], raw_ref.at[:, lanes], sems.at[step])

    steps = raw_ref.shape[1] // STEP
    for step in range(steps):
        fetch(step).start()
    fill_tables(kept_ref[...], low_ref, high_ref)
    acc_ref[...] = jnp.zeros_like(acc_ref)

    def add(step, carry):
        fetch(step).wait()
        signs = (1 - 2 * bits_ref[pl.ds(step * tiles, tiles), :]).astype(F32)
        pieces = []
        for n in range(chunks):
            lanes = pl.ds(pl.multiple_of(step * STEP + n * WIDE, WIDE), WIDE)
            pieces.append(raw_ref[:, lanes] * wide_rows(signs, 2 * n, 2).astype(BF16))
        stacked = jnp.concatenate(pieces, axis=0)
        for first in range(0, width, WIDE):
            columns = slice(first, first + WIDE)
            part = jnp.dot(stacked, low_ref[:, columns], preferred_element_type=F32)
            total = acc_ref[:, columns]
            for n in range(chunks):
                sign = high_ref[pl.ds(step * chunks + n, 1), columns]
                total = total + part[n * rows : (n + 1) * rows, :] * sign
            acc_ref[:, columns] = total
        return carry

    lax.fori_loop(0, steps, add, 0)
    done = jnp.transpose(acc_ref[...] * scale)
    out_ref[...] = done.reshape(out_ref.shape).astype(out_ref.dtype)


def tables_kernel(kept_ref, one_ref, two_ref, when_ref, low_ref, high_ref, moments_ref):
    fill_tables(kept_ref[...], low_ref, high_ref)
    moments_ref[...] = jnp.concatenate([one_ref[...], two_ref[...]], axis=1)


def turned_kernel(kept_ref, when_ref, turned_ref, high_ref, low_ref):
    fill_tables(kept_ref[...], low_ref, high_ref)
    turned_ref[...] = jnp.transpose(low_ref[...].astype(F32)).astype(BF16)


def compress_kernel(
    scale, panel_ref, y_ref, bits_ref, low_ref, high_ref, moments_ref, out_ref, part_ref
):
    sources, width, lanes = y_ref.shape
    line = sources // SIDE
    place = panel_ref[0] // line
    signs = bits_ref[pl.ds(pl.multiple_of(place * line, line), line), :]
    signs = (1 - 2 * signs).astype(F32)
    y = y_ref[...].astype(F32).reshape(SIDE, line, width, lanes) * signs[None, :, None, :]
    y = y.reshape(sources // 2, 2, width, lanes)
    y = jnp.concatenate([y[:, 0], y[:, 1]], axis=2).reshape(sources // 2 * width, 2 * lanes)
    part = jnp.dot(y.astype(BF16), low_ref[...], preferred_element_type=F32)
    part_ref[...] = part.reshape(part_ref.shape)
    total = jnp.zeros(part_ref.shape[2:], F32)
    for pair in range(line // 2):
        one = part_ref[0, pair]
        for other in range(1, SIDE):
            one = one + part_ref[other, pair]
        total = total + one * high_ref[pl.ds(place * (line // 2) + pair, 1), :]
    total = (total * scale).astype(BF16).astype(F32)
    pieces = [total[:, n : n + LANES] for n in range(0, total.shape[1], LANES)]
    rest = moments_ref[...]
    for _ in range(3):
        piece = rest.astype(BF16).astype(F32)
        pieces.append(piece)
        rest = rest - piece
    half = width // 2
    for core in range(2):
        for n, piece in enumerate(pieces):
            block = piece[core * half : (core + 1) * half, :].astype(BF16)
            for peer in range(out_ref.shape[0]):
                out_ref[peer, core, n] = block


def adam_kernel(
    scale, rep_ref, panel_ref, fix_ref, got_ref, bits_ref, turned_ref, high_ref,
    back_ref, sum_ref, lhs_ref,
):
    peers = got_ref.shape[0]
    line = back_ref.shape[1]
    place = panel_ref[0] // line
    mine = rep_ref[0] // (2 * SIDE) * SIDE + place
    first_fix, second_fix = fix_ref[0], fix_ref[1]
    middle = LANES // 2
    tops, rests = [], []
    own = jnp.zeros(sum_ref.shape, F32)
    for n in range(peers):
        total = jnp.zeros(sum_ref.shape, F32)
        for peer in range(peers):
            for core in range(2):
                total = total + got_ref[peer, core, n].astype(F32)
        own = jnp.where(mine == n, total, own)
        moments = []
        for core in range(2):
            moment = got_ref[n, core, peers].astype(F32) + got_ref[n, core, peers + 1].astype(F32)
            moments.append(moment + got_ref[n, core, peers + 2].astype(F32))
        one = jnp.concatenate([moments[0][:, :middle], moments[1][:, :middle]], axis=1)
        two = jnp.concatenate([moments[0][:, middle:], moments[1][:, middle:]], axis=1)
        new_one = BETA_ONE * one + (1.0 - BETA_ONE) * total
        new_two = BETA_TWO * two + (1.0 - BETA_TWO) * total * total
        direction = new_one / first_fix / (jnp.sqrt(new_two / second_fix) + EPSILON)
        top = direction.astype(BF16).astype(F32)
        tops.append(top)
        rests.append(direction - top)
    sum_ref[...] = own
    both = jnp.concatenate([jnp.concatenate(tops, axis=1), jnp.concatenate(rests, axis=1)], axis=0)
    wides = lhs_ref.shape[0]
    for wide in range(wides):
        lhs_ref[wide] = (both * high_ref[pl.ds(place * wides + wide, 1), :]).astype(BF16)
    lhs = lhs_ref[...].reshape(wides * lhs_ref.shape[1], lhs_ref.shape[2])
    back = jnp.dot(lhs, turned_ref[...], preferred_element_type=F32)
    back = back.reshape(wides, 2, back.shape[0] // wides // 2, WIDE)
    back = back[:, 0] + back[:, 1]
    back = jnp.stack([back[:, :, :LANES], back[:, :, LANES:]], axis=1)
    back = back.reshape(2 * wides, back.shape[2], LANES)
    signs = bits_ref[pl.ds(pl.multiple_of(place * line, line), line), :]
    signs = (1 - 2 * signs).astype(F32) * scale
    back = (back * signs[:, None, :]).astype(BF16)
    for copy in range(SIDE):
        back_ref[copy] = back


def expand_kernel(
    scale, rep_ref, own_ref, other_ref, turned_ref, high_ref, bits_ref, weight_ref, out_ref,
    both_ref, back_ref, lhs_ref,
):
    step = pl.program_id(0)
    rows = weight_ref.shape[0]
    stride = out_ref.shape[1]
    chunks = stride // WIDE

    @pl.when(step == 0)
    def _():
        core = jnp.bitwise_and(rep_ref[0], 1)
        both_ref[:, pl.ds(core, 1)] = own_ref[...].astype(F32)[:, None]
        both_ref[:, pl.ds(1 - core, 1)] = other_ref[...].astype(F32)[:, None]
        columns = both_ref[...].reshape(back_ref.shape[1], rows)
        back_ref[...] = jnp.transpose(columns).astype(BF16)

    for chunk in range(chunks):
        sign = high_ref[pl.ds(step * chunks + chunk, 1), :].astype(BF16)
        lhs_ref[chunk * rows : (chunk + 1) * rows, :] = back_ref[...] * sign
    update = jnp.dot(lhs_ref[...], turned_ref[...], preferred_element_type=F32)
    tiles = stride // LANES
    signs = (1 - 2 * bits_ref[pl.ds(step * tiles, tiles), :]).astype(F32) * scale
    for chunk in range(chunks):
        lanes = pl.ds(pl.multiple_of(step * stride + chunk * WIDE, WIDE), WIDE)
        moved = update[chunk * rows : (chunk + 1) * rows, :] * wide_rows(signs, 2 * chunk, 2)
        moved = weight_ref[:, lanes].astype(F32) - moved
        out_ref[:, chunk * WIDE : (chunk + 1) * WIDE] = moved.astype(BF16)


def shaped(shape, dtype):
    return jax.ShapeDtypeStruct(shape, dtype)


SMEM = pl.BlockSpec(memory_space=pltpu.SMEM)
ROOM = pltpu.CompilerParams(vmem_limit_bytes=24 << 20)
VMEM = pl.BlockSpec(memory_space=pltpu.VMEM)


def cost(flops, moved):
    return pl.CostEstimate(flops=flops, bytes_accessed=moved, transcendentals=0)


def local(replica_grads, weight, moment_one, moment_two, sign_bits, kept_rows, step_count):
    reps, panels = lax.axis_size("rep"), lax.axis_size("fsdp")
    full_len, kept_len = sign_bits.shape[0], kept_rows.shape[0]
    rows = weight.shape[0]
    peers = reps // 2
    half_width = kept_len // panels // 2
    norm_scale = 1.0 / math.sqrt(kept_len)
    rep = lax.axis_index("rep").astype(jnp.int32).reshape(1)
    panel = lax.axis_index("fsdp").astype(jnp.int32).reshape(1)
    core = jnp.bitwise_and(rep[0], 1)
    kept = kept_rows.reshape(kept_len // LANES, LANES)
    bits = sign_bits.reshape(full_len // LANES, LANES)
    one_t, two_t = moment_one.T, moment_two.T
    wide_count = full_len // WIDE
    low_table, high_table = shaped((WIDE, kept_len), BF16), shaped((wide_count, kept_len), F32)
    everywhere = pl.BlockSpec(memory_space=pl.ANY)
    both = ("rep", "fsdp")
    line, far = panels // SIDE, peers // SIDE
    near = range(SIDE)

    def device(y_hi, x, side, y_lo, z):
        return ((y_hi * SIDE + x) * 2 + side) * panels + y_lo * line + z

    planes = [
        [device(y_hi, x, side, y_lo, z) for x in near for z in range(line)]
        for y_hi in range(far) for side in range(2) for y_lo in near
    ]
    columns_of_chips = [
        [device(y_hi, x, side, y_lo, z) for y_hi in range(far) for y_lo in near for side in range(2)]
        for x in near for z in range(line)
    ]

    def turn_over(cross):
        return [
            (device(y_hi, x, side, y_lo, z), device(y_hi, y_lo, side ^ cross, x, z))
            for y_hi in range(far) for x in near for side in range(2)
            for y_lo in near for z in range(line)
        ]

    def turn(when):
        return pl.pallas_call(
            turned_kernel,
            out_shape=(shaped((kept_len, WIDE), BF16), high_table),
            in_specs=[VMEM, everywhere],
            out_specs=(VMEM,) * 2,
            scratch_shapes=[pltpu.VMEM(low_table.shape, BF16)],
            compiler_params=ROOM,
            cost_estimate=cost(10 * LANES * kept_len, 8 * WIDE * kept_len),
        )(kept, when)

    def regroup(blocks, groups):
        return lax.all_to_all(blocks, both, 0, 0, axis_index_groups=groups, tiled=True)

    columns = pl.pallas_call(
        functools.partial(project_kernel, norm_scale),
        out_shape=shaped((panels, 2 * half_width, rows), BF16),
        in_specs=[VMEM, VMEM, pl.BlockSpec(memory_space=pltpu.HBM)],
        out_specs=VMEM,
        scratch_shapes=[
            pltpu.VMEM(low_table.shape, BF16),
            pltpu.VMEM(high_table.shape, F32),
            pltpu.VMEM((rows, full_len), BF16),
            pltpu.VMEM((rows, kept_len), F32),
            pltpu.SemaphoreType.DMA((full_len // STEP,)),
        ],
        compiler_params=ROOM,
        cost_estimate=cost(2 * rows * full_len * kept_len, 2 * rows * full_len),
    )(*(pltpu.with_memory_space_constraint(x, pltpu.HBM) for x in (kept, bits, replica_grads)))
    low, high, moments = pl.pallas_call(
        tables_kernel,
        out_shape=(low_table, high_table, shaped((2 * half_width, LANES), F32)),
        in_specs=[VMEM] * 3 + [everywhere],
        out_specs=(VMEM,) * 3,
        compiler_params=ROOM,
        cost_estimate=cost(10 * LANES * kept_len, 8 * WIDE * kept_len),
    )(kept, one_t, two_t, columns)
    moments = lax.ppermute(moments, both, turn_over(0))
    columns = regroup(columns, planes)

    pieces = kept_len // LANES + 3
    message_shape = (peers, 2, pieces, half_width, LANES)
    message = pl.pallas_call(
        functools.partial(compress_kernel, norm_scale),
        out_shape=shaped(message_shape, BF16),
        in_specs=[SMEM] + [VMEM] * 5,
        out_specs=VMEM,
        scratch_shapes=[pltpu.VMEM((SIDE, line // 2, 2 * half_width, kept_len), F32)],
        compiler_params=ROOM,
        cost_estimate=cost(2 * full_len * half_width * kept_len // panels, 2 * full_len * half_width),
    )(panel, columns, bits, low, high, moments)
    turned, high = turn(message)
    message = regroup(message.reshape((2 * peers,) + message_shape[2:]), columns_of_chips)
    message = message.reshape(message_shape)

    steps_done = step_count.astype(F32)
    fixes = jnp.stack(
        [1.0 - jnp.power(F32(BETA_ONE), steps_done), 1.0 - jnp.power(F32(BETA_TWO), steps_done)]
    )
    back, own_sum = pl.pallas_call(
        functools.partial(adam_kernel, norm_scale),
        out_shape=(
            shaped((SIDE, line, half_width, rows), BF16),
            shaped((half_width, LANES), F32),
        ),
        in_specs=[SMEM] * 3 + [VMEM] * 4,
        out_specs=(VMEM,) * 2,
        scratch_shapes=[pltpu.VMEM((line // 2, 2 * half_width, kept_len), BF16)],
        compiler_params=ROOM,
        cost_estimate=cost(full_len * half_width * kept_len, 2 * full_len * half_width),
    )(rep, panel, fixes, message, bits, turned, high)
    turned, high = turn(back)
    same_sum = lax.ppermute(own_sum, both, turn_over(0))
    cross_sum = lax.ppermute(own_sum, both, turn_over(1))
    back = regroup(back.reshape(panels, half_width, rows), planes)
    other_back = lax.ppermute(back, "rep", [(n, n ^ 1) for n in range(reps)])

    row_count = moment_one.shape[0]
    same_rows = jnp.where(core == 0, same_sum[:, :row_count], same_sum[:, row_count:])
    cross_rows = jnp.where(core == 0, cross_sum[:, :row_count], cross_sum[:, row_count:])
    compressed = jnp.where(
        core == 0,
        jnp.concatenate([same_rows, cross_rows], axis=0),
        jnp.concatenate([cross_rows, same_rows], axis=0),
    )
    new_one = (BETA_ONE * one_t + (1.0 - BETA_ONE) * compressed).T
    new_two = (BETA_TWO * two_t + (1.0 - BETA_TWO) * compressed * compressed).T

    new_weight = pl.pallas_call(
        functools.partial(expand_kernel, LEARN_RATE * norm_scale),
        grid=(full_len // LONG_STEP,),
        out_shape=shaped(weight.shape, BF16),
        in_specs=[SMEM] + [VMEM] * 6,
        out_specs=pl.BlockSpec((rows, LONG_STEP), lambda i: (0, i)),
        scratch_shapes=[
            pltpu.VMEM((panels, 2, half_width, rows), F32),
            pltpu.VMEM((rows, kept_len), BF16),
            pltpu.VMEM((rows * LONG_STEP // WIDE, kept_len), BF16),
        ],
        compiler_params=ROOM,
        cost_estimate=cost(2 * rows * full_len * kept_len, 4 * rows * full_len),
    )(rep, back, other_back, turned, high, bits, weight)
    return (new_weight, new_one, new_two)


def solution(mesh):
    in_specs = (
        P("rep", "fsdp", None),
        P("fsdp", None),
        P("rep", "fsdp"),
        P("rep", "fsdp"),
        P(),
        P(),
        P(),
    )
    out_specs = (P("fsdp", None), P("rep", "fsdp"), P("rep", "fsdp"))
    return jax.shard_map(local, mesh=mesh, in_specs=in_specs, out_specs=out_specs, check_vma=False)
```

time: 111 us -> 105 us (0.946)
  waiting for transfers between devices: 47.7 us -> 43.9 us
  starting transfers between devices: 46.3 us -> 44.6 us
    all_to_all x3, waiting for transfers between devices: 46.5 us -> 43.4 us  [regroup(): lax.all_to_all(blocks, both, 0, 0, axis_index_groups=groups, tiled=True)]
    all_to_all x3, starting transfers between devices: 40.6 us -> 38.9 us  [regroup(): lax.all_to_all(blocks, both, 0, 0, axis_index_groups=groups, tiled=True)]
    ppermute x2 -> x4, starting transfers between devices: 5.73 us -> 5.68 us  [the longest x1 2.3 us: local(): other_back = lax.ppermute(back, 'rep', [(n, n ^ 1) for n in range(reps)])]
  transfers between devices with their start and end apart: 5 -> 7, of which waited for: 5 -> 5; matrix products, arithmetic and copies ran while one was open for 1% -> 1% of each run, Pallas kernels for 1% -> 1%
where the time goes in v4:
time: 105 us
  starting transfers between devices  44.6 us (42%)
  waiting for transfers between devices  43.9 us (42%)
  Pallas kernels  13.7 us (13%)
  between operations  1.52 us (1%)
    all_to_all x3, waiting for transfers between devices, regroup(): lax.all_to_all(blocks, both, 0, 0, axis_index_groups=groups, tiled=True)  43.4 us
    all_to_all x3, starting transfers between devices, regroup(): lax.all_to_all(blocks, both, 0, 0, axis_index_groups=groups, tiled=True)  38.9 us
    pallas_call x1, Pallas kernels, local(): pl.pallas_call(functools.partial(project_kernel, norm_scale), out_shape=s...  6.25 us
    pallas_call x1, Pallas kernels, local(): pl.pallas_call(functools.partial(expand_kernel, LEARN_RATE * norm_scale),...  3.93 us
    ppermute x1, starting transfers between devices, local(): other_back = lax.ppermute(back, 'rep', [(n, n ^ 1) for n in range(reps)])  2.3 us
  transfers between devices with their start and end apart: 7, of which 5 were waited for; matrix products, arithmetic and copies ran while one was open for 1% of the time, Pallas kernels for 1%

profile of v4, /device:TPU:1, one launch (start us, length us, event | category | flops | bytes accessed | tf_op | source)
XLA Modules:
  0.0 104.5 jit_solution(3433218517040388427)
XLA Ops:
  0.6 0.0 copy-start.1
  0.6 0.0 copy-start.2
  0.7 0.0 copy-start.3
  0.7 0.0 copy-start
  0.7 6.3 %shard_map.94.when_ref = bf16[64,16,128]{2,1,0:T(8,128)(2,1)} custom-call(s32[8,128]{1,0:T(8,128)} %bitcast.22, s32[64,128]{1,0:T(8,128)} %bitcast.18, bf16[1,128,8192]{2,1,0:T(8,128)(2,1)} %x_ref.1), custom_call_target="tpu_custom_call" | custom-call | flops 2147483648 | bytes 2097152 | tf_op jit(solution)/shard_map/pallas_call | solution.py:280
  6.9 22.8 %all-to-all-start = ((bf16[64,16,128]{2,1,0:T(8,128)(2,1)}), bf16[64,16,128]{2,1,0:T(8,128)(2,1)S(1)}, u32[]{:S(2)}, u32[]{:S(2)}) async-start(bf16[64,16,128]{2,1,0:T(8,128)(2,1)} %shard_map.94.when_ref), calls=%async_computation | async-start | bytes 524288 | tf_op jit(solution)/shard_map/all_to_all | solution.py:278
  29.7 0.0 copy-done.1
  29.8 0.0 copy-start.4
  29.8 0.2 shard_map.95
  30.0 0.8 collective-permute-start
  30.8 0.0 collective-permute-done.moments_ref
  30.8 18.0 %all-to-all-done.y_ref = bf16[64,16,128]{2,1,0:T(8,128)(2,1)S(1)} async-done(((bf16[64,16,128]{2,1,0:T(8,128)(2,1)}), bf16[64,16,128]{2,1,0:T(8,128)(2,1)S(1)}, u32[]{:S(2)}, u32[]{:S(2)}) %all-to-all-start) | async-done | bytes 262176 | tf_op jit(solution)/shard_map/all_to_all | solution.py:278
  48.8 1.2 %shard_map.96.when_ref = bf16[8,2,11,8,128]{4,3,2,1,0:T(8,128)(2,1)} custom-call(s32[1]{0:T(128)} %bitcast.1.panel_ref, bf16[64,16,128]{2,1,0:T(8,128)(2,1)S(1)} %all-to-all-done.y_ref, s32[64,128]{1,0:T(8,128)S(1)} %bitcast.19, bf16[256,1024]{1,0:T(8,128)(2,1)S(1)} %get-tuple-element.12.low_ref, f32[32,1024]{1,0:T(8,128)S(1)} %get-tuple-element.13.high_ref, ...), custom_call_target="tpu_custom_call" | custom-call | flops 2097152 | bytes 131072 | tf_op jit(solution)/shard_map/pallas_call | solution.py:308
  50.0 10.0 %all-to-all-start.1 = ((bf16[16,11,8,128]{3,2,1,0:T(8,128)(2,1)}), bf16[16,11,8,128]{3,2,1,0:T(8,128)(2,1)S(1)}, u32[]{:S(2)}, u32[]{:S(2)}) async-start(bf16[16,11,8,128]{3,2,1,0:T(8,128)(2,1)} %bitcast.8), calls=%async_computation.1 | async-start | bytes 720896 | tf_op jit(solution)/shard_map/all_to_all | solution.py:278
  60.7 0.1 pad_maximum_fusion.fix_ref
  60.8 0.3 shard_map.97
  61.1 12.6 %all-to-all-done.1 = bf16[16,11,8,128]{3,2,1,0:T(8,128)(2,1)S(1)} async-done(((bf16[16,11,8,128]{3,2,1,0:T(8,128)(2,1)}), bf16[16,11,8,128]{3,2,1,0:T(8,128)(2,1)S(1)}, u32[]{:S(2)}, u32[]{:S(2)}) %all-to-all-start.1) | async-done | bytes 360480 | tf_op jit(solution)/shard_map/all_to_all | solution.py:278
  73.8 1.5 %shard_map.98 = (bf16[4,16,8,128]{3,2,1,0:T(8,128)(2,1)}, f32[8,128]{1,0:T(8,128)S(1)}) custom-call(s32[1]{0:T(128)} %bitcast.rep_ref, s32[1]{0:T(128)} %bitcast.1.panel_ref, f32[2]{0:T(128)S(1)} %pad_maximum_fusion.fix_ref, bf16[8,2,11,8,128]{4,3,2,1,0:T(8,128)(2,1)S(1)} %bitcast.17, s32[64,128]{1,0:T(8,128)S(1)} %bitcast.20, ...), custom_call_target="tpu_custom_call" | custom-call | flops 67108864 | bytes 131072 | tf_op jit(solution)/shard_map/pallas_call | solution.py:325
  75.3 6.1 %all-to-all-start.2 = ((bf16[64,8,128]{2,1,0:T(8,128)(2,1)}), bf16[64,8,128]{2,1,0:T(8,128)(2,1)S(1)}, u32[]{:S(2)}, u32[]{:S(2)}) async-start(bf16[64,8,128]{2,1,0:T(8,128)(2,1)} %bitcast.10), calls=%async_computation.2 | async-start | bytes 262144 | tf_op jit(solution)/shard_map/all_to_all | solution.py:278
  81.4 1.9 %collective-permute-start.3 = (f32[8,128]{1,0:T(8,128)S(1)}, f32[8,128]{1,0:T(8,128)S(1)}, u32[]{:S(2)}, u32[]{:S(2)}) collective-permute-start(f32[8,128]{1,0:T(8,128)S(1)} %get-tuple-element.20), channel_id=1, source_target_pairs={{0,64},{1,65},{2,66},{3,67},{4,68},{5,69},{6,70},{7,71},{8,72},{9,... | collective-permute-start | bytes 12296 | tf_op jit(solution)/shard_map/ppermute | solution.py:339
  83.3 0.7 collective-permute-start.2
  84.0 0.3 shard_map.99
  84.3 0.1 collective-permute-done.3
  84.5 0.1 slice_select_fusion
  84.5 0.0 collective-permute-done.2
  84.6 0.1 slice_select_fusion.1
  84.6 12.7 %all-to-all-done.2.own_ref = bf16[64,8,128]{2,1,0:T(8,128)(2,1)S(1)} async-done(((bf16[64,8,128]{2,1,0:T(8,128)(2,1)}), bf16[64,8,128]{2,1,0:T(8,128)(2,1)S(1)}, u32[]{:S(2)}, u32[]{:S(2)}) %all-to-all-start.2) | async-done | bytes 131104 | tf_op jit(solution)/shard_map/all_to_all | solution.py:278
  97.3 2.3 %collective-permute-start.1 = (bf16[64,8,128]{2,1,0:T(8,128)(2,1)S(1)}, bf16[64,8,128]{2,1,0:T(8,128)(2,1)S(1)}, u32[]{:S(2)}, u32[]{:S(2)}) collective-permute-start(bf16[64,8,128]{2,1,0:T(8,128)(2,1)S(1)} %all-to-all-done.2.own_ref), channel_id=1, source_target_pairs={{0,64},{64,0},{128,192},{192,128},{256,320},{320,256},{384,448},{4... | collective-permute-start | bytes 393224 | tf_op jit(solution)/shard_map/ppermute | solution.py:341
  99.6 0.6 fusion.1
  100.2 0.3 collective-permute-done.1.other_ref
  100.6 0.0 copy-done.4
  100.6 3.9 %shard_map.100 = bf16[128,8192]{1,0:T(8,128)(2,1)} custom-call(s32[1]{0:T(128)} %bitcast.rep_ref, bf16[64,8,128]{2,1,0:T(8,128)(2,1)S(1)} %all-to-all-done.2.own_ref, bf16[64,8,128]{2,1,0:T(8,128)(2,1)S(1)} %collective-permute-done.1.other_ref, bf16[1024,256]{1,0:T(8,128)(2,1)S(1)} %get-tuple-element.18.turned_ref, ...), custom_call_target="tpu_custom_call" | custom-call | flops 2147483648 | bytes 4194304 | tf_op jit(solution)/shard_map/pallas_call | solution.py:354
  (3 shorter events, 0.0 us)
Async XLA Ops:
  0.6 29.1 %copy-start.1 = (s32[1024]{0:T(1024)S(1)}, s32[1024]{0:T(1024)}, u32[]{:S(2)}) copy-start(s32[1024]{0:T(1024)} %param.12) | copy-start | bytes 12292
  0.6 29.1 %copy-start.2 = (f32[64,16]{0,1:T(8,128)S(1)}, f32[64,16]{0,1:T(8,128)}, u32[]{:S(2)}) copy-start(f32[64,16]{0,1:T(8,128)} %param.9) | copy-start | bytes 12292
  0.7 29.1 %copy-start.3 = (f32[64,16]{0,1:T(8,128)S(1)}, f32[64,16]{0,1:T(8,128)}, u32[]{:S(2)}) copy-start(f32[64,16]{0,1:T(8,128)} %param.10) | copy-start | bytes 12292
  0.7 48.2 %copy-start = (s32[8192]{0:T(1024)S(1)}, s32[8192]{0:T(1024)}, u32[]{:S(2)}) copy-start(s32[8192]{0:T(1024)} %param.11) | copy-start | bytes 98308
  6.9 41.9 %all-to-all-start = ((bf16[64,16,128]{2,1,0:T(8,128)(2,1)}), bf16[64,16,128]{2,1,0:T(8,128)(2,1)S(1)}, u32[]{:S(2)}, u32[]{:S(2)}) async-start(bf16[64,16,128]{2,1,0:T(8,128)(2,1)} %shard_map.94.when_ref), calls=%async_computation | async-start | bytes 524288 | tf_op jit(solution)/shard_map/all_to_all | solution.py:278
  29.8 70.8 %copy-start.4 = (bf16[128,8192]{1,0:T(8,128)(2,1)S(1)}, bf16[128,8192]{1,0:T(8,128)(2,1)}, u32[]{:S(2)}) copy-start(bf16[128,8192]{1,0:T(8,128)(2,1)} %weight_ref.1) | copy-start | bytes 6291460
  30.0 0.8 collective-permute-start
  50.0 23.7 %all-to-all-start.1 = ((bf16[16,11,8,128]{3,2,1,0:T(8,128)(2,1)}), bf16[16,11,8,128]{3,2,1,0:T(8,128)(2,1)S(1)}, u32[]{:S(2)}, u32[]{:S(2)}) async-start(bf16[16,11,8,128]{3,2,1,0:T(8,128)(2,1)} %bitcast.8), calls=%async_computation.1 | async-start | bytes 720896 | tf_op jit(solution)/shard_map/all_to_all | solution.py:278
  75.3 22.0 %all-to-all-start.2 = ((bf16[64,8,128]{2,1,0:T(8,128)(2,1)}), bf16[64,8,128]{2,1,0:T(8,128)(2,1)S(1)}, u32[]{:S(2)}, u32[]{:S(2)}) async-start(bf16[64,8,128]{2,1,0:T(8,128)(2,1)} %bitcast.10), calls=%async_computation.2 | async-start | bytes 262144 | tf_op jit(solution)/shard_map/all_to_all | solution.py:278
  81.4 3.1 %collective-permute-start.3 = (f32[8,128]{1,0:T(8,128)S(1)}, f32[8,128]{1,0:T(8,128)S(1)}, u32[]{:S(2)}, u32[]{:S(2)}) collective-permute-start(f32[8,128]{1,0:T(8,128)S(1)} %get-tuple-element.20), channel_id=1, source_target_pairs={{0,64},{1,65},{2,66},{3,67},{4,68},{5,69},{6,70},{7,71},{8,72},{9,... | collective-permute-start | bytes 12296 | tf_op jit(solution)/shard_map/ppermute | solution.py:339
  83.3 1.2 %collective-permute-start.2 = (f32[8,128]{1,0:T(8,128)S(1)}, f32[8,128]{1,0:T(8,128)S(1)}, u32[]{:S(2)}, u32[]{:S(2)}) collective-permute-start(f32[8,128]{1,0:T(8,128)S(1)} %get-tuple-element.20), channel_id=1, source_target_pairs={{0,0},{1,1},{2,2},{3,3},{4,4},{5,5},{6,6},{7,7},{8,8},{9,9},{10,10... | collective-permute-start | bytes 12296 | tf_op jit(solution)/shard_map/ppermute | solution.py:338
  97.3 3.3 %collective-permute-start.1 = (bf16[64,8,128]{2,1,0:T(8,128)(2,1)S(1)}, bf16[64,8,128]{2,1,0:T(8,128)(2,1)S(1)}, u32[]{:S(2)}, u32[]{:S(2)}) collective-permute-start(bf16[64,8,128]{2,1,0:T(8,128)(2,1)S(1)} %all-to-all-done.2.own_ref), channel_id=1, source_target_pairs={{0,64},{64,0},{128,192},{192,128},{256,320},{320,256},{384,448},{4... | collective-permute-start | bytes 393224 | tf_op jit(solution)/shard_map/ppermute | solution.py:341

commit v5 on v4

--- a/solution.py
+++ b/solution.py
@@ -17,6 +17,7 @@
 STEP = 1024
 LONG_STEP = 2048
 SIDE = 4
+PIECES = 2
 F32 = jnp.float32
 BF16 = jnp.bfloat16
 
@@ -51,47 +52,97 @@
     high_ref[...] = parity_signs(iota(high_ref.shape, 0), jnp.right_shift(rows, 8))
 
 
-def project_kernel(scale, kept_ref, bits_ref, x_ref, out_ref, low_ref, high_ref, raw_ref, acc_ref, sems):
+def order_columns(half, kept):
+    blocks = kept.shape[0]
+    digits = jnp.concatenate([jnp.right_shift(kept, 7), jnp.bitwise_and(kept, LANES - 1)], axis=0)
+    digits = digits.astype(F32).astype(BF16)
+    source, target = iota((LANES, LANES), 0), iota((LANES, LANES), 1)
+    same = jnp.logical_and(
+        jnp.right_shift(source, 4) == jnp.bitwise_and(jnp.right_shift(target, 3), 7),
+        jnp.bitwise_and(source, 7) == jnp.bitwise_and(target, 7),
+    )
+    source_half = jnp.bitwise_and(jnp.right_shift(source, 3), 1)
+    pieces = []
+    for wanted in (1 - half, half):
+        moved = []
+        for part in (0, 1):
+            pick = jnp.logical_and(same, source_half == wanted)
+            pick = jnp.logical_and(pick, jnp.right_shift(target, 6) == part)
+            pick = jnp.where(pick, 1.0, 0.0).astype(BF16)
+            moved.append(jnp.dot(digits, pick, preferred_element_type=F32))
+        for pair in range(blocks // 2):
+            even, odd = 2 * pair, 2 * pair + 1
+            top = moved[0][even : even + 1, :] + moved[1][odd : odd + 1, :]
+            low = (
+                moved[0][blocks + even : blocks + even + 1, :]
+                + moved[1][blocks + odd : blocks + odd + 1, :]
+            )
+            pieces.append(top * LANES + low)
+    return jnp.concatenate(pieces, axis=1).astype(jnp.int32)
+
+
+def project_half(scale, first, x_of, low_ref, high_ref, out_ref, acc_ref):
     rows, width = acc_ref.shape
     chunks = STEP // WIDE
-    tiles = STEP // LANES
-
-    def fetch(step):
-        lanes = pl.ds(pl.multiple_of(step * STEP, STEP), STEP)
-        return pltpu.make_async_copy(x_ref.at[0, :, lanes], raw_ref.at[:, lanes], sems.at[step])
-
-    steps = raw_ref.shape[1] // STEP
-    for step in range(steps):
-        fetch(step).start()
-    fill_tables(kept_ref[...], low_ref, high_ref)
+    columns = slice(first, first + width)
     acc_ref[...] = jnp.zeros_like(acc_ref)
 
     def add(step, carry):
-        fetch(step).wait()
-        signs = (1 - 2 * bits_ref[pl.ds(step * tiles, tiles), :]).astype(F32)
-        pieces = []
+        x = x_of(step)
+        stacked = jnp.concatenate([x[:, n * WIDE : (n + 1) * WIDE] for n in range(chunks)], axis=0)
+        part = jnp.dot(stacked, low_ref[:, columns], preferred_element_type=F32)
+        total = acc_ref[...]
         for n in range(chunks):
-            lanes = pl.ds(pl.multiple_of(step * STEP + n * WIDE, WIDE), WIDE)
-            pieces.append(raw_ref[:, lanes] * wide_rows(signs, 2 * n, 2).astype(BF16))
-        stacked = jnp.concatenate(pieces, axis=0)
-        for first in range(0, width, WIDE):
-            columns = slice(first, first + WIDE)
-            part = jnp.dot(stacked, low_ref[:, columns], preferred_element_type=F32)
-            total = acc_ref[:, columns]
-            for n in range(chunks):
-                sign = high_ref[pl.ds(step * chunks + n, 1), columns]
-                total = total + part[n * rows : (n + 1) * rows, :] * sign
-            acc_ref[:, columns] = total
+            sign = high_ref[pl.ds(step * chunks + n, 1), columns]
+            total = total + part[n * rows : (n + 1) * rows, :] * sign
+        acc_ref[...] = total
         return carry
 
+    steps = high_ref.shape[0] // chunks
     lax.fori_loop(0, steps, add, 0)
     done = jnp.transpose(acc_ref[...] * scale)
     out_ref[...] = done.reshape(out_ref.shape).astype(out_ref.dtype)
 
 
-def tables_kernel(kept_ref, one_ref, two_ref, when_ref, low_ref, high_ref, moments_ref):
+def project_other_kernel(
+    scale, rep_ref, kept_ref, bits_ref, x_ref, low_ref, high_ref, signed_ref, out_ref, acc_ref, sems
+):
+    def fetch(step):
+        lanes = pl.ds(pl.multiple_of(step * STEP, STEP), STEP)
+        return pltpu.make_async_copy(x_ref.at[0, :, lanes], signed_ref.at[:, lanes], sems.at[step])
+
+    for step in range(signed_ref.shape[1] // STEP):
+        fetch(step).start()
+    half = jnp.bitwise_and(rep_ref[0], 1)
+    columns = order_columns(half, kept_ref[...])
+    fill_low_table(low_ref, columns)
+    high_ref[...] = parity_signs(iota(high_ref.shape, 0), jnp.right_shift(columns, 8))
+    def x_of(step):
+        fetch(step).wait()
+        lanes = pl.ds(pl.multiple_of(step * STEP, STEP), STEP)
+        signs = (1 - 2 * bits_ref[pl.ds(step * (STEP // LANES), STEP // LANES), :]).astype(F32)
+        x = signed_ref[:, lanes] * wide_rows(signs, 0, STEP // LANES).astype(BF16)
+        signed_ref[:, lanes] = x
+        return x
+
+    project_half(scale, 0, x_of, low_ref, high_ref, out_ref, acc_ref)
+
+
+def project_own_kernel(scale, signed_ref, low_ref, high_ref, out_ref, acc_ref):
+    def x_of(step):
+        return signed_ref[:, pl.ds(pl.multiple_of(step * STEP, STEP), STEP)]
+
+    project_half(scale, acc_ref.shape[1], x_of, low_ref, high_ref, out_ref, acc_ref)
+
+
+def tables_kernel(rep_ref, kept_ref, one_ref, two_ref, when_ref, low_ref, high_ref, same_ref, cross_ref):
     fill_tables(kept_ref[...], low_ref, high_ref)
-    moments_ref[...] = jnp.concatenate([one_ref[...], two_ref[...]], axis=1)
+    core = jnp.bitwise_and(rep_ref[0], 1)
+    both = jnp.concatenate([one_ref[...], two_ref[...]], axis=1)
+    half = both.shape[0] // 2
+    upper, lower = both[:half, :], both[half:, :]
+    same_ref[...] = jnp.where(core == 0, upper, lower)
+    cross_ref[...] = jnp.where(core == 0, lower, upper)
 
 
 def turned_kernel(kept_ref, when_ref, turned_ref, high_ref, low_ref):
@@ -100,7 +151,8 @@
 
 
 def compress_kernel(
-    scale, panel_ref, y_ref, bits_ref, low_ref, high_ref, moments_ref, out_ref, part_ref
+    scale, rep_ref, panel_ref, y_ref, bits_ref, low_ref, high_ref, same_ref, cross_ref,
+    out_ref, part_ref,
 ):
     sources, width, lanes = y_ref.shape
     line = sources // SIDE
@@ -118,19 +170,21 @@
         for other in range(1, SIDE):
             one = one + part_ref[other, pair]
         total = total + one * high_ref[pl.ds(place * (line // 2) + pair, 1), :]
-    total = (total * scale).astype(BF16).astype(F32)
+    total = (total * scale).astype(BF16)
     pieces = [total[:, n : n + LANES] for n in range(0, total.shape[1], LANES)]
-    rest = moments_ref[...]
-    for _ in range(3):
-        piece = rest.astype(BF16).astype(F32)
-        pieces.append(piece)
-        rest = rest - piece
-    half = width // 2
-    for core in range(2):
-        for n, piece in enumerate(pieces):
-            block = piece[core * half : (core + 1) * half, :].astype(BF16)
-            for peer in range(out_ref.shape[0]):
-                out_ref[peer, core, n] = block
+    core = jnp.bitwise_and(rep_ref[0], 1)
+    same, cross = same_ref[...], cross_ref[...]
+    first, second = jnp.where(core == 0, same, cross), jnp.where(core == 0, cross, same)
+    middle = LANES // 2
+    for lanes in (slice(0, middle), slice(middle, LANES)):
+        rest = jnp.concatenate([first[:, lanes], second[:, lanes]], axis=1)
+        for _ in range(PIECES):
+            piece = rest.astype(BF16)
+            pieces.append(piece)
+            rest = rest - piece.astype(F32)
+    for n, piece in enumerate(pieces):
+        for peer in range(out_ref.shape[0]):
+            out_ref[peer, n] = piece
 
 
 def adam_kernel(
@@ -142,21 +196,20 @@
     place = panel_ref[0] // line
     mine = rep_ref[0] // (2 * SIDE) * SIDE + place
     first_fix, second_fix = fix_ref[0], fix_ref[1]
-    middle = LANES // 2
     tops, rests = [], []
     own = jnp.zeros(sum_ref.shape, F32)
     for n in range(peers):
         total = jnp.zeros(sum_ref.shape, F32)
         for peer in range(peers):
-            for core in range(2):
-                total = total + got_ref[peer, core, n].astype(F32)
+            total = total + got_ref[peer, n].astype(F32)
         own = jnp.where(mine == n, total, own)
         moments = []
-        for core in range(2):
-            moment = got_ref[n, core, peers].astype(F32) + got_ref[n, core, peers + 1].astype(F32)
-            moments.append(moment + got_ref[n, core, peers + 2].astype(F32))
-        one = jnp.concatenate([moments[0][:, :middle], moments[1][:, :middle]], axis=1)
-        two = jnp.concatenate([moments[0][:, middle:], moments[1][:, middle:]], axis=1)
+        for index in range(2):
+            moment = jnp.zeros(sum_ref.shape, F32)
+            for piece in reversed(range(PIECES)):
+                moment = moment + got_ref[n, peers + index * PIECES + piece].astype(F32)
+            moments.append(moment)
+        one, two = moments
         new_one = BETA_ONE * one + (1.0 - BETA_ONE) * total
         new_two = BETA_TWO * two + (1.0 - BETA_TWO) * total * total
         direction = new_one / first_fix / (jnp.sqrt(new_two / second_fix) + EPSILON)
@@ -241,6 +294,7 @@
     low_table, high_table = shaped((WIDE, kept_len), BF16), shaped((wide_count, kept_len), F32)
     everywhere = pl.BlockSpec(memory_space=pl.ANY)
     both = ("rep", "fsdp")
+    swap = [(n, n ^ 1) for n in range(reps)]
     line, far = panels // SIDE, peers // SIDE
     near = range(SIDE)
 
@@ -251,9 +305,9 @@
         [device(y_hi, x, side, y_lo, z) for x in near for z in range(line)]
         for y_hi in range(far) for side in range(2) for y_lo in near
     ]
-    columns_of_chips = [
-        [device(y_hi, x, side, y_lo, z) for y_hi in range(far) for y_lo in near for side in range(2)]
-        for x in near for z in range(line)
+    rings = [
+        [device(y_hi, x, side, y_lo, z) for y_hi in range(far) for y_lo in near]
+        for x in near for side in range(2) for z in range(line)
     ]
 
     def turn_over(cross):
@@ -277,46 +331,57 @@
     def regroup(blocks, groups):
         return lax.all_to_all(blocks, both, 0, 0, axis_index_groups=groups, tiled=True)
 
-    columns = pl.pallas_call(
-        functools.partial(project_kernel, norm_scale),
-        out_shape=shaped((panels, 2 * half_width, rows), BF16),
-        in_specs=[VMEM, VMEM, pl.BlockSpec(memory_space=pltpu.HBM)],
-        out_specs=VMEM,
+    half_shape = (panels, half_width, rows)
+    half_len = kept_len // 2
+    in_hbm = [pltpu.with_memory_space_constraint(x, pltpu.HBM) for x in (kept, bits, replica_grads)]
+    col_low, col_high, signed, for_other = pl.pallas_call(
+        functools.partial(project_other_kernel, norm_scale),
+        out_shape=(low_table, high_table, shaped((rows, full_len), BF16), shaped(half_shape, BF16)),
+        in_specs=[SMEM] + [VMEM] * 2 + [pl.BlockSpec(memory_space=pltpu.HBM)],
+        out_specs=(VMEM,) * 4,
         scratch_shapes=[
-            pltpu.VMEM(low_table.shape, BF16),
-            pltpu.VMEM(high_table.shape, F32),
-            pltpu.VMEM((rows, full_len), BF16),
-            pltpu.VMEM((rows, kept_len), F32),
+            pltpu.VMEM((rows, half_len), F32),
             pltpu.SemaphoreType.DMA((full_len // STEP,)),
         ],
         compiler_params=ROOM,
-        cost_estimate=cost(2 * rows * full_len * kept_len, 2 * rows * full_len),
-    )(*(pltpu.with_memory_space_constraint(x, pltpu.HBM) for x in (kept, bits, replica_grads)))
-    low, high, moments = pl.pallas_call(
+        cost_estimate=cost(2 * rows * full_len * half_len, 2 * rows * full_len),
+    )(rep, *in_hbm)
+    from_other = lax.ppermute(for_other, "rep", swap)
+    mine = pl.pallas_call(
+        functools.partial(project_own_kernel, norm_scale),
+        out_shape=shaped(half_shape, F32),
+        in_specs=[VMEM] * 3,
+        out_specs=VMEM,
+        scratch_shapes=[pltpu.VMEM((rows, half_len), F32)],
+        compiler_params=ROOM,
+        cost_estimate=cost(2 * rows * full_len * half_len, 2 * rows * full_len),
+    )(signed, col_low, col_high)
+    columns = (mine + from_other.astype(F32)).astype(BF16)
+    half_moments = shaped((half_width, LANES), F32)
+    low, high, for_same, for_cross = pl.pallas_call(
         tables_kernel,
-        out_shape=(low_table, high_table, shaped((2 * half_width, LANES), F32)),
-        in_specs=[VMEM] * 3 + [everywhere],
-        out_specs=(VMEM,) * 3,
+        out_shape=(low_table, high_table, half_moments, half_moments),
+        in_specs=[SMEM] + [VMEM] * 3 + [everywhere],
+        out_specs=(VMEM,) * 4,
         compiler_params=ROOM,
         cost_estimate=cost(10 * LANES * kept_len, 8 * WIDE * kept_len),
-    )(kept, one_t, two_t, columns)
-    moments = lax.ppermute(moments, both, turn_over(0))
+    )(rep, kept, one_t, two_t, columns)
+    from_same = lax.ppermute(for_same, both, turn_over(0))
+    from_cross = lax.ppermute(for_cross, both, turn_over(1))
     columns = regroup(columns, planes)
 
-    pieces = kept_len // LANES + 3
-    message_shape = (peers, 2, pieces, half_width, LANES)
+    message_shape = (peers, kept_len // LANES + 2 * PIECES, half_width, LANES)
     message = pl.pallas_call(
         functools.partial(compress_kernel, norm_scale),
         out_shape=shaped(message_shape, BF16),
-        in_specs=[SMEM] + [VMEM] * 5,
+        in_specs=[SMEM] * 2 + [VMEM] * 6,
         out_specs=VMEM,
-        scratch_shapes=[pltpu.VMEM((SIDE, line // 2, 2 * half_width, kept_len), F32)],
+        scratch_shapes=[pltpu.VMEM((SIDE, line // 2, half_width, kept_len), F32)],
         compiler_params=ROOM,
         cost_estimate=cost(2 * full_len * half_width * kept_len // panels, 2 * full_len * half_width),
-    )(panel, columns, bits, low, high, moments)
+    )(rep, panel, columns, bits, low, high, from_same, from_cross)
     turned, high = turn(message)
-    message = regroup(message.reshape((2 * peers,) + message_shape[2:]), columns_of_chips)
-    message = message.reshape(message_shape)
+    message = regroup(message, rings)
 
     steps_done = step_count.astype(F32)
     fixes = jnp.stack(
@@ -338,7 +403,7 @@
     same_sum = lax.ppermute(own_sum, both, turn_over(0))
     cross_sum = lax.ppermute(own_sum, both, turn_over(1))
     back = regroup(back.reshape(panels, half_width, rows), planes)
-    other_back = lax.ppermute(back, "rep", [(n, n ^ 1) for n in range(reps)])
+    other_back = lax.ppermute(back, "rep", swap)
 
     row_count = moment_one.shape[0]
     same_rows = jnp.where(core == 0, same_sum[:, :row_count], same_sum[:, row_count:])

time: 105 us -> 104 us (level)
  waiting for transfers between devices: 43.9 us -> 28.4 us
  starting transfers between devices: 44.6 us -> 57.3 us
    ppermute x2 -> x4, starting transfers between devices: 3.1 us -> 24.4 us  [the longest x1 16 us: local(): from_other = lax.ppermute(for_other, 'rep', swap)]
    all_to_all x3, waiting for transfers between devices: 43.4 us -> 27.2 us  [regroup(): lax.all_to_all(blocks, both, 0, 0, axis_index_groups=groups, tiled=True)]
    all_to_all x3, starting transfers between devices: 38.9 us -> 28 us  [regroup(): lax.all_to_all(blocks, both, 0, 0, axis_index_groups=groups, tiled=True)]
    ppermute x1, starting transfers between devices: 1.92 us -> 4.23 us  [local(): cross_sum = lax.ppermute(own_sum, both, turn_over(1))]
    pallas_call x2 -> x3, Pallas kernels: 6.44 us -> 7.18 us  [the longest x1 4.41 us: local(): pl.pallas_call(functools.partial(project_other_kernel, norm_scale), out_s...]
  transfers between devices with their start and end apart: 7 -> 9, of which waited for: 5 -> 5; matrix products, arithmetic and copies ran while one was open for 1% -> 1% of each run, Pallas kernels for 1% -> 3%
where the time goes in v5:
time: 104 us; the launch traced here: 103 us
  starting transfers between devices  57.3 us (55%)
  waiting for transfers between devices  28.4 us (27%)
  Pallas kernels  14.2 us (14%)
  between operations  1.57 us (2%)
  other arithmetic  1.52 us (1%)
    all_to_all x3, starting transfers between devices, regroup(): lax.all_to_all(blocks, both, 0, 0, axis_index_groups=groups, tiled=True)  28 us
    all_to_all x3, waiting for transfers between devices, regroup(): lax.all_to_all(blocks, both, 0, 0, axis_index_groups=groups, tiled=True)  27.2 us
    ppermute x1, starting transfers between devices, local(): from_other = lax.ppermute(for_other, 'rep', swap)  16 us
    ppermute x1, starting transfers between devices, local(): other_back = lax.ppermute(back, 'rep', swap)  5.52 us
    pallas_call x1, Pallas kernels, local(): pl.pallas_call(functools.partial(project_other_kernel, norm_scale), out_s...  4.41 us
    ppermute x1, starting transfers between devices, local(): cross_sum = lax.ppermute(own_sum, both, turn_over(1))  4.23 us
    pallas_call x1, Pallas kernels, local(): pl.pallas_call(functools.partial(expand_kernel, LEARN_RATE * norm_scale),...  3.94 us
    pallas_call x1, Pallas kernels, local(): pl.pallas_call(functools.partial(project_own_kernel, norm_scale), out_sha...  2.58 us
  transfers between devices with their start and end apart: 9, of which 5 were waited for; matrix products, arithmetic and copies ran while one was open for 1% of the time, Pallas kernels for 3%

profile of v5, /device:TPU:1, one launch (start us, length us, event | category | flops | bytes accessed | tf_op | source)
XLA Modules:
  0.0 103.0 jit_solution(18274142387054980554)
XLA Ops:
  0.6 4.4 %shard_map.94 = (bf16[256,1024]{1,0:T(8,128)(2,1)S(1)}, f32[32,1024]{1,0:T(8,128)S(1)}, bf16[128,8192]{1,0:T(8,128)(2,1)S(1)}, bf16[64,8,128]{2,1,0:T(8,128)(2,1)S(1)}) custom-call(s32[1]{0:T(128)} %bitcast.rep_ref, s32[8,128]{1,0:T(8,128)} %bitcast.19, s32[64,128]{1,0:T(8,128)} %bitcast.15, bf16[1,128,8192]{2,1,0:T(8,128)(2,1)} %x_ref.1), custom_call_target="tpu_custom_call" | custom-call | flops 1073741824 | bytes 2097152 | tf_op jit(solution)/shard_map/pallas_call | solution.py:337
  5.1 16.0 %collective-permute-start = (bf16[64,8,128]{2,1,0:T(8,128)(2,1)S(1)}, bf16[64,8,128]{2,1,0:T(8,128)(2,1)S(1)}, u32[]{:S(2)}, u32[]{:S(2)}) collective-permute-start(bf16[64,8,128]{2,1,0:T(8,128)(2,1)S(1)} %get-tuple-element.20), channel_id=1, source_target_pairs={{0,64},{64,0},{128,192},{192,128},{256,320},{320,256},{384,448},{4... | collective-permute-start | bytes 393224 | tf_op jit(solution)/shard_map/ppermute | solution.py:349
  21.1 0.0 copy-start.1
  21.1 0.0 copy-start.2
  21.1 0.0 copy-start.3
  21.1 0.0 copy-start
  21.1 2.6 %shard_map.95 = f32[64,8,128]{2,1,0:T(8,128)S(1)} custom-call(bf16[128,8192]{1,0:T(8,128)(2,1)S(1)} %get-tuple-element.17.signed_ref, bf16[256,1024]{1,0:T(8,128)(2,1)S(1)} %get-tuple-element.18.low_ref, f32[32,1024]{1,0:T(8,128)S(1)} %get-tuple-element.19.high_ref), custom_call_target="tpu_custom_call" | custom-call | flops 1073741824 | bytes 2097152 | tf_op jit(solution)/shard_map/pallas_call | solution.py:350
  23.7 0.0 copy-start.4
  23.7 0.7 add_convert_fusion.when_ref
  24.4 9.3 %all-to-all-start = ((bf16[64,8,128]{2,1,0:T(8,128)(2,1)}), bf16[64,8,128]{2,1,0:T(8,128)(2,1)S(1)}, u32[]{:S(2)}, u32[]{:S(2)}) async-start(bf16[64,8,128]{2,1,0:T(8,128)(2,1)} %add_convert_fusion.when_ref), calls=%async_computation | async-start | bytes 262144 | tf_op jit(solution)/shard_map/all_to_all | solution.py:332
  33.8 0.2 shard_map.96
  34.0 0.7 collective-permute-start.1
  34.7 2.2 %collective-permute-start.2 = (f32[8,128]{1,0:T(8,128)S(1)}, f32[8,128]{1,0:T(8,128)S(1)}, u32[]{:S(2)}, u32[]{:S(2)}) collective-permute-start(f32[8,128]{1,0:T(8,128)S(1)} %get-tuple-element.24), channel_id=1, source_target_pairs={{0,64},{1,65},{2,66},{3,67},{4,68},{5,69},{6,70},{7,71},{8,72},{9,... | collective-permute-start | bytes 12296 | tf_op jit(solution)/shard_map/ppermute | solution.py:370
  36.9 0.8 collective-permute-done.2.cross_ref
  37.7 11.0 %all-to-all-done.y_ref = bf16[64,8,128]{2,1,0:T(8,128)(2,1)S(1)} async-done(((bf16[64,8,128]{2,1,0:T(8,128)(2,1)}), bf16[64,8,128]{2,1,0:T(8,128)(2,1)S(1)}, u32[]{:S(2)}, u32[]{:S(2)}) %all-to-all-start) | async-done | bytes 131104 | tf_op jit(solution)/shard_map/all_to_all | solution.py:332
  48.7 1.0 shard_map.97.when_ref
  49.7 6.8 %all-to-all-start.1 = ((bf16[8,12,8,128]{3,2,1,0:T(8,128)(2,1)}), bf16[8,12,8,128]{3,2,1,0:T(8,128)(2,1)S(1)}, u32[]{:S(2)}, u32[]{:S(2)}) async-start(bf16[8,12,8,128]{3,2,1,0:T(8,128)(2,1)} %shard_map.97.when_ref), calls=%async_computation.1 | async-start | bytes 393216 | tf_op jit(solution)/shard_map/all_to_all | solution.py:332
  57.2 0.1 pad_maximum_fusion.fix_ref
  57.3 0.3 shard_map.98
  57.6 7.6 %all-to-all-done.1.got_ref = bf16[8,12,8,128]{3,2,1,0:T(8,128)(2,1)S(1)} async-done(((bf16[8,12,8,128]{3,2,1,0:T(8,128)(2,1)}), bf16[8,12,8,128]{3,2,1,0:T(8,128)(2,1)S(1)}, u32[]{:S(2)}, u32[]{:S(2)}) %all-to-all-start.1) | async-done | bytes 196640 | tf_op jit(solution)/shard_map/all_to_all | solution.py:332
  65.2 1.5 %shard_map.99 = (bf16[4,16,8,128]{3,2,1,0:T(8,128)(2,1)}, f32[8,128]{1,0:T(8,128)S(1)}) custom-call(s32[1]{0:T(128)} %bitcast.rep_ref, s32[1]{0:T(128)} %bitcast.1.panel_ref, f32[2]{0:T(128)S(1)} %pad_maximum_fusion.fix_ref, bf16[8,12,8,128]{3,2,1,0:T(8,128)(2,1)S(1)} %all-to-all-done.1.got_ref, s32[64,128]{1,0:T(8,128)S(1)} %bitcast.17, ...), custom_call_target="tpu_custom_call" | custom-call | flops 67108864 | bytes 131072 | tf_op jit(solution)/shard_map/pallas_call | solution.py:390
  66.7 11.9 %all-to-all-start.2 = ((bf16[64,8,128]{2,1,0:T(8,128)(2,1)}), bf16[64,8,128]{2,1,0:T(8,128)(2,1)S(1)}, u32[]{:S(2)}, u32[]{:S(2)}) async-start(bf16[64,8,128]{2,1,0:T(8,128)(2,1)} %bitcast.8), calls=%async_computation.2 | async-start | bytes 262144 | tf_op jit(solution)/shard_map/all_to_all | solution.py:332
  78.6 4.2 %collective-permute-start.5 = (f32[8,128]{1,0:T(8,128)S(1)}, f32[8,128]{1,0:T(8,128)S(1)}, u32[]{:S(2)}, u32[]{:S(2)}) collective-permute-start(f32[8,128]{1,0:T(8,128)S(1)} %get-tuple-element.30), channel_id=1, source_target_pairs={{0,64},{1,65},{2,66},{3,67},{4,68},{5,69},{6,70},{7,71},{8,72},{9,... | collective-permute-start | bytes 12296 | tf_op jit(solution)/shard_map/ppermute | solution.py:404
  82.8 0.7 collective-permute-start.4
  83.5 0.3 shard_map.100
  83.8 0.1 slice_select_fusion
  83.9 0.1 slice_select_fusion.1
  84.0 8.6 %all-to-all-done.2.own_ref = bf16[64,8,128]{2,1,0:T(8,128)(2,1)S(1)} async-done(((bf16[64,8,128]{2,1,0:T(8,128)(2,1)}), bf16[64,8,128]{2,1,0:T(8,128)(2,1)S(1)}, u32[]{:S(2)}, u32[]{:S(2)}) %all-to-all-start.2) | async-done | bytes 131104 | tf_op jit(solution)/shard_map/all_to_all | solution.py:332
  92.5 5.5 %collective-permute-start.3 = (bf16[64,8,128]{2,1,0:T(8,128)(2,1)S(1)}, bf16[64,8,128]{2,1,0:T(8,128)(2,1)S(1)}, u32[]{:S(2)}, u32[]{:S(2)}) collective-permute-start(bf16[64,8,128]{2,1,0:T(8,128)(2,1)S(1)} %all-to-all-done.2.own_ref), channel_id=1, source_target_pairs={{0,64},{64,0},{128,192},{192,128},{256,320},{320,256},{384,448},{4... | collective-permute-start | bytes 393224 | tf_op jit(solution)/shard_map/ppermute | solution.py:406
  98.1 0.6 fusion.1
  98.7 0.3 collective-permute-done.3.other_ref
  99.0 3.9 %shard_map.101 = bf16[128,8192]{1,0:T(8,128)(2,1)} custom-call(s32[1]{0:T(128)} %bitcast.rep_ref, bf16[64,8,128]{2,1,0:T(8,128)(2,1)S(1)} %all-to-all-done.2.own_ref, bf16[64,8,128]{2,1,0:T(8,128)(2,1)S(1)} %collective-permute-done.3.other_ref, bf16[1024,256]{1,0:T(8,128)(2,1)S(1)} %get-tuple-element.28.turned_ref, ...), custom_call_target="tpu_custom_call" | custom-call | flops 2147483648 | bytes 4194304 | tf_op jit(solution)/shard_map/pallas_call | solution.py:419
  (9 shorter events, 0.0 us)
Async XLA Ops:
  5.1 18.7 %collective-permute-start = (bf16[64,8,128]{2,1,0:T(8,128)(2,1)S(1)}, bf16[64,8,128]{2,1,0:T(8,128)(2,1)S(1)}, u32[]{:S(2)}, u32[]{:S(2)}) collective-permute-start(bf16[64,8,128]{2,1,0:T(8,128)(2,1)S(1)} %get-tuple-element.20), channel_id=1, source_target_pairs={{0,64},{64,0},{128,192},{192,128},{256,320},{320,256},{384,448},{4... | collective-permute-start | bytes 393224 | tf_op jit(solution)/shard_map/ppermute | solution.py:349
  21.1 12.7 %copy-start.1 = (s32[1024]{0:T(1024)S(1)}, s32[1024]{0:T(1024)}, u32[]{:S(2)}) copy-start(s32[1024]{0:T(1024)} %param.12) | copy-start | bytes 12292
  21.1 12.7 %copy-start.2 = (f32[64,16]{0,1:T(8,128)S(1)}, f32[64,16]{0,1:T(8,128)}, u32[]{:S(2)}) copy-start(f32[64,16]{0,1:T(8,128)} %param.9) | copy-start | bytes 12292
  21.1 12.7 %copy-start.3 = (f32[64,16]{0,1:T(8,128)S(1)}, f32[64,16]{0,1:T(8,128)}, u32[]{:S(2)}) copy-start(f32[64,16]{0,1:T(8,128)} %param.10) | copy-start | bytes 12292
  21.1 27.6 %copy-start = (s32[8192]{0:T(1024)S(1)}, s32[8192]{0:T(1024)}, u32[]{:S(2)}) copy-start(s32[8192]{0:T(1024)} %param.11) | copy-start | bytes 98308
  23.7 75.3 %copy-start.4 = (bf16[128,8192]{1,0:T(8,128)(2,1)S(1)}, bf16[128,8192]{1,0:T(8,128)(2,1)}, u32[]{:S(2)}) copy-start(bf16[128,8192]{1,0:T(8,128)(2,1)} %weight_ref.1) | copy-start | bytes 6291460
  24.4 24.3 %all-to-all-start = ((bf16[64,8,128]{2,1,0:T(8,128)(2,1)}), bf16[64,8,128]{2,1,0:T(8,128)(2,1)S(1)}, u32[]{:S(2)}, u32[]{:S(2)}) async-start(bf16[64,8,128]{2,1,0:T(8,128)(2,1)} %add_convert_fusion.when_ref), calls=%async_computation | async-start | bytes 262144 | tf_op jit(solution)/shard_map/all_to_all | solution.py:332
  34.0 2.9 %collective-permute-start.1 = (f32[8,128]{1,0:T(8,128)S(1)}, f32[8,128]{1,0:T(8,128)S(1)}, u32[]{:S(2)}, u32[]{:S(2)}) collective-permute-start(f32[8,128]{1,0:T(8,128)S(1)} %get-tuple-element.23), channel_id=1, source_target_pairs={{0,0},{1,1},{2,2},{3,3},{4,4},{5,5},{6,6},{7,7},{8,8},{9,9},{10,10... | collective-permute-start | bytes 12296 | tf_op jit(solution)/shard_map/ppermute | solution.py:369
  34.7 3.1 %collective-permute-start.2 = (f32[8,128]{1,0:T(8,128)S(1)}, f32[8,128]{1,0:T(8,128)S(1)}, u32[]{:S(2)}, u32[]{:S(2)}) collective-permute-start(f32[8,128]{1,0:T(8,128)S(1)} %get-tuple-element.24), channel_id=1, source_target_pairs={{0,64},{1,65},{2,66},{3,67},{4,68},{5,69},{6,70},{7,71},{8,72},{9,... | collective-permute-start | bytes 12296 | tf_op jit(solution)/shard_map/ppermute | solution.py:370
  49.7 15.6 %all-to-all-start.1 = ((bf16[8,12,8,128]{3,2,1,0:T(8,128)(2,1)}), bf16[8,12,8,128]{3,2,1,0:T(8,128)(2,1)S(1)}, u32[]{:S(2)}, u32[]{:S(2)}) async-start(bf16[8,12,8,128]{3,2,1,0:T(8,128)(2,1)} %shard_map.97.when_ref), calls=%async_computation.1 | async-start | bytes 393216 | tf_op jit(solution)/shard_map/all_to_all | solution.py:332
  66.7 25.8 %all-to-all-start.2 = ((bf16[64,8,128]{2,1,0:T(8,128)(2,1)}), bf16[64,8,128]{2,1,0:T(8,128)(2,1)S(1)}, u32[]{:S(2)}, u32[]{:S(2)}) async-start(bf16[64,8,128]{2,1,0:T(8,128)(2,1)} %bitcast.8), calls=%async_computation.2 | async-start | bytes 262144 | tf_op jit(solution)/shard_map/all_to_all | solution.py:332
  78.6 5.2 %collective-permute-start.5 = (f32[8,128]{1,0:T(8,128)S(1)}, f32[8,128]{1,0:T(8,128)S(1)}, u32[]{:S(2)}, u32[]{:S(2)}) collective-permute-start(f32[8,128]{1,0:T(8,128)S(1)} %get-tuple-element.30), channel_id=1, source_target_pairs={{0,64},{1,65},{2,66},{3,67},{4,68},{5,69},{6,70},{7,71},{8,72},{9,... | collective-permute-start | bytes 12296 | tf_op jit(solution)/shard_map/ppermute | solution.py:404
  82.8 1.1 %collective-permute-start.4 = (f32[8,128]{1,0:T(8,128)S(1)}, f32[8,128]{1,0:T(8,128)S(1)}, u32[]{:S(2)}, u32[]{:S(2)}) collective-permute-start(f32[8,128]{1,0:T(8,128)S(1)} %get-tuple-element.30), channel_id=1, source_target_pairs={{0,0},{1,1},{2,2},{3,3},{4,4},{5,5},{6,6},{7,7},{8,8},{9,9},{10,10... | collective-permute-start | bytes 12296 | tf_op jit(solution)/shard_map/ppermute | solution.py:403
  92.5 6.5 %collective-permute-start.3 = (bf16[64,8,128]{2,1,0:T(8,128)(2,1)S(1)}, bf16[64,8,128]{2,1,0:T(8,128)(2,1)S(1)}, u32[]{:S(2)}, u32[]{:S(2)}) collective-permute-start(bf16[64,8,128]{2,1,0:T(8,128)(2,1)S(1)} %all-to-all-done.2.own_ref), channel_id=1, source_target_pairs={{0,64},{64,0},{128,192},{192,128},{256,320},{320,256},{384,448},{4... | collective-permute-start | bytes 393224 | tf_op jit(solution)/shard_map/ppermute | solution.py:406

commit v6 on v5

--- a/solution.py
+++ b/solution.py
@@ -50,6 +50,12 @@
     rows = wide_rows(kept, 0, kept.shape[0])
     fill_low_table(low_ref, rows)
     high_ref[...] = parity_signs(iota(high_ref.shape, 0), jnp.right_shift(rows, 8))
+
+
+def split_moments(one_ref, two_ref):
+    both = jnp.concatenate([one_ref[...], two_ref[...]], axis=1)
+    half = both.shape[0] // 2
+    return both[:half, :], both[half:, :]
 
 
 def order_columns(half, kept):
@@ -99,24 +105,41 @@
         return carry
 
     steps = high_ref.shape[0] // chunks
-    lax.fori_loop(0, steps, add, 0)
-    done = jnp.transpose(acc_ref[...] * scale)
-    out_ref[...] = done.reshape(out_ref.shape).astype(out_ref.dtype)
+    lax.fori_loop(0, steps, add, 0, unroll=True)
+    done = jnp.transpose(acc_ref[...] * scale).reshape((-1,) + out_ref.shape[1:])
+    out_ref[: done.shape[0]] = done.astype(out_ref.dtype)
 
 
 def project_other_kernel(
-    scale, rep_ref, kept_ref, bits_ref, x_ref, low_ref, high_ref, signed_ref, out_ref, acc_ref, sems
+    scale, rep_ref, kept_hbm, bits_hbm, one_hbm, two_hbm, x_ref,
+    low_ref, high_ref, signed_ref, out_ref,
+    acc_ref, kept_ref, bits_ref, one_ref, two_ref, sems, small_sems,
 ):
     def fetch(step):
         lanes = pl.ds(pl.multiple_of(step * STEP, STEP), STEP)
         return pltpu.make_async_copy(x_ref.at[0, :, lanes], signed_ref.at[:, lanes], sems.at[step])
 
+    pairs = ((kept_hbm, kept_ref), (bits_hbm, bits_ref), (one_hbm, one_ref), (two_hbm, two_ref))
+    small = [
+        pltpu.make_async_copy(far, near, small_sems.at[n]) for n, (far, near) in enumerate(pairs)
+    ]
+    for copy in small:
+        copy.start()
     for step in range(signed_ref.shape[1] // STEP):
         fetch(step).start()
+    for copy in small:
+        copy.wait()
     half = jnp.bitwise_and(rep_ref[0], 1)
     columns = order_columns(half, kept_ref[...])
     fill_low_table(low_ref, columns)
     high_ref[...] = parity_signs(iota(high_ref.shape, 0), jnp.right_shift(columns, 8))
+    upper, lower = split_moments(one_ref, two_ref)
+    rest = jnp.where(half == 0, lower, upper)
+    for n in range(PIECES):
+        piece = rest.astype(BF16)
+        out_ref[out_ref.shape[0] - PIECES + n] = piece
+        rest = rest - piece.astype(F32)
+
     def x_of(step):
         fetch(step).wait()
         lanes = pl.ds(pl.multiple_of(step * STEP, STEP), STEP)
@@ -135,14 +158,18 @@
     project_half(scale, acc_ref.shape[1], x_of, low_ref, high_ref, out_ref, acc_ref)
 
 
-def tables_kernel(rep_ref, kept_ref, one_ref, two_ref, when_ref, low_ref, high_ref, same_ref, cross_ref):
+def tables_kernel(
+    rep_ref, kept_ref, one_ref, two_ref, other_ref, when_ref, low_ref, high_ref, moments_ref
+):
     fill_tables(kept_ref[...], low_ref, high_ref)
     core = jnp.bitwise_and(rep_ref[0], 1)
-    both = jnp.concatenate([one_ref[...], two_ref[...]], axis=1)
-    half = both.shape[0] // 2
-    upper, lower = both[:half, :], both[half:, :]
-    same_ref[...] = jnp.where(core == 0, upper, lower)
-    cross_ref[...] = jnp.where(core == 0, lower, upper)
+    upper, lower = split_moments(one_ref, two_ref)
+    same = jnp.where(core == 0, upper, lower)
+    cross = jnp.zeros_like(same)
+    for n in reversed(range(PIECES)):
+        cross = cross + other_ref[other_ref.shape[0] - PIECES + n].astype(F32)
+    moments_ref[0] = jnp.where(core == 0, same, cross)
+    moments_ref[1] = jnp.where(core == 0, cross, same)
 
 
 def turned_kernel(kept_ref, when_ref, turned_ref, high_ref, low_ref):
@@ -151,8 +178,7 @@
 
 
 def compress_kernel(
-    scale, rep_ref, panel_ref, y_ref, bits_ref, low_ref, high_ref, same_ref, cross_ref,
-    out_ref, part_ref,
+    scale, panel_ref, y_ref, bits_ref, low_ref, high_ref, moments_ref, out_ref, part_ref
 ):
     sources, width, lanes = y_ref.shape
     line = sources // SIDE
@@ -172,9 +198,7 @@
         total = total + one * high_ref[pl.ds(place * (line // 2) + pair, 1), :]
     total = (total * scale).astype(BF16)
     pieces = [total[:, n : n + LANES] for n in range(0, total.shape[1], LANES)]
-    core = jnp.bitwise_and(rep_ref[0], 1)
-    same, cross = same_ref[...], cross_ref[...]
-    first, second = jnp.where(core == 0, same, cross), jnp.where(core == 0, cross, same)
+    first, second = moments_ref[0], moments_ref[1]
     middle = LANES // 2
     for lanes in (slice(0, middle), slice(middle, LANES)):
         rest = jnp.concatenate([first[:, lanes], second[:, lanes]], axis=1)
@@ -333,15 +357,28 @@
 
     half_shape = (panels, half_width, rows)
     half_len = kept_len // 2
-    in_hbm = [pltpu.with_memory_space_constraint(x, pltpu.HBM) for x in (kept, bits, replica_grads)]
+    in_hbm = [
+        pltpu.with_memory_space_constraint(x, pltpu.HBM)
+        for x in (kept, bits, one_t, two_t, replica_grads)
+    ]
     col_low, col_high, signed, for_other = pl.pallas_call(
         functools.partial(project_other_kernel, norm_scale),
-        out_shape=(low_table, high_table, shaped((rows, full_len), BF16), shaped(half_shape, BF16)),
-        in_specs=[SMEM] + [VMEM] * 2 + [pl.BlockSpec(memory_space=pltpu.HBM)],
+        out_shape=(
+            low_table,
+            high_table,
+            shaped((rows, full_len), BF16),
+            shaped((panels + PIECES, half_width, rows), BF16),
+        ),
+        in_specs=[SMEM] + [pl.BlockSpec(memory_space=pltpu.HBM)] * 5,
         out_specs=(VMEM,) * 4,
         scratch_shapes=[
             pltpu.VMEM((rows, half_len), F32),
+            pltpu.VMEM(kept.shape, jnp.int32),
+            pltpu.VMEM(bits.shape, jnp.int32),
+            pltpu.VMEM(one_t.shape, F32),
+            pltpu.VMEM(two_t.shape, F32),
             pltpu.SemaphoreType.DMA((full_len // STEP,)),
+            pltpu.SemaphoreType.DMA((4,)),
         ],
         compiler_params=ROOM,
         cost_estimate=cost(2 * rows * full_len * half_len, 2 * rows * full_len),
@@ -356,30 +393,28 @@
         compiler_params=ROOM,
         cost_estimate=cost(2 * rows * full_len * half_len, 2 * rows * full_len),
     )(signed, col_low, col_high)
-    columns = (mine + from_other.astype(F32)).astype(BF16)
-    half_moments = shaped((half_width, LANES), F32)
-    low, high, for_same, for_cross = pl.pallas_call(
+    columns = (mine + from_other[:panels].astype(F32)).astype(BF16)
+    low, high, moments = pl.pallas_call(
         tables_kernel,
-        out_shape=(low_table, high_table, half_moments, half_moments),
-        in_specs=[SMEM] + [VMEM] * 3 + [everywhere],
-        out_specs=(VMEM,) * 4,
+        out_shape=(low_table, high_table, shaped((2, half_width, LANES), F32)),
+        in_specs=[SMEM] + [VMEM] * 4 + [everywhere],
+        out_specs=(VMEM,) * 3,
         compiler_params=ROOM,
         cost_estimate=cost(10 * LANES * kept_len, 8 * WIDE * kept_len),
-    )(rep, kept, one_t, two_t, columns)
-    from_same = lax.ppermute(for_same, both, turn_over(0))
-    from_cross = lax.ppermute(for_cross, both, turn_over(1))
+    )(rep, kept, one_t, two_t, from_other, columns)
+    moments = lax.ppermute(moments, both, turn_over(0))
     columns = regroup(columns, planes)
 
     message_shape = (peers, kept_len // LANES + 2 * PIECES, half_width, LANES)
     message = pl.pallas_call(
         functools.partial(compress_kernel, norm_scale),
         out_shape=shaped(message_shape, BF16),
-        in_specs=[SMEM] * 2 + [VMEM] * 6,
+        in_specs=[SMEM] + [VMEM] * 5,
         out_specs=VMEM,
         scratch_shapes=[pltpu.VMEM((SIDE, line // 2, half_width, kept_len), F32)],
         compiler_params=ROOM,
         cost_estimate=cost(2 * full_len * half_width * kept_len // panels, 2 * full_len * half_width),
-    )(rep, panel, columns, bits, low, high, from_same, from_cross)
+    )(panel, columns, bits, low, high, moments)
     turned, high = turn(message)
     message = regroup(message, rings)
 

time: 104 us -> 99.1 us (0.953)
  starting transfers between devices: 57.3 us -> 53.1 us
  Pallas kernels: 14.2 us -> 12.9 us
  waiting for transfers between devices: 28.4 us -> 29.6 us
    all_to_all x3, starting transfers between devices: 28 us -> 24.1 us  [regroup(): lax.all_to_all(blocks, both, 0, 0, axis_index_groups=groups, tiled=True)]
    ppermute x2 -> x1, starting transfers between devices: 2.86 us -> 0.66 us  [local(): moments = lax.ppermute(moments, both, turn_over(0))]
    all_to_all x3, waiting for transfers between devices: 27.2 us -> 29.2 us  [regroup(): lax.all_to_all(blocks, both, 0, 0, axis_index_groups=groups, tiled=True)]
    pallas_call x1, Pallas kernels: 2.58 us -> 1.4 us  [local(): pl.pallas_call(functools.partial(project_own_kernel, norm_scale), out_sha...]
  transfers between devices with their start and end apart: 9 -> 8, of which waited for: 5 -> 4; matrix products, arithmetic and copies ran while one was open for 1% -> 1% of each run, Pallas kernels for 3% -> 2%
where the time goes in v6:
time: 99.1 us; the launch traced here: 98.7 us
  starting transfers between devices  53.1 us (54%)
  waiting for transfers between devices  29.6 us (30%)
  Pallas kernels  12.9 us (13%)
  between operations  1.56 us (2%)
  other arithmetic  1.52 us (2%)
    all_to_all x3, waiting for transfers between devices, regroup(): lax.all_to_all(blocks, both, 0, 0, axis_index_groups=groups, tiled=True)  29.2 us
    all_to_all x3, starting transfers between devices, regroup(): lax.all_to_all(blocks, both, 0, 0, axis_index_groups=groups, tiled=True)  24.1 us
    ppermute x1, starting transfers between devices, local(): from_other = lax.ppermute(for_other, 'rep', swap)  16 us
    ppermute x1, starting transfers between devices, local(): other_back = lax.ppermute(back, 'rep', swap)  6.39 us
    ppermute x1, starting transfers between devices, local(): cross_sum = lax.ppermute(own_sum, both, turn_over(1))  5.24 us
    pallas_call x1, Pallas kernels, local(): pl.pallas_call(functools.partial(project_other_kernel, norm_scale), out_s...  4.28 us
    pallas_call x1, Pallas kernels, local(): pl.pallas_call(functools.partial(expand_kernel, LEARN_RATE * norm_scale),...  3.93 us
  transfers between devices with their start and end apart: 8, of which 4 were waited for; matrix products, arithmetic and copies ran while one was open for 1% of the time, Pallas kernels for 2%

profile of v6, /device:TPU:1, one launch (start us, length us, event | category | flops | bytes accessed | tf_op | source)
XLA Modules:
  0.0 98.7 jit_solution(4954779083592722738)
XLA Ops:
  0.6 4.3 %shard_map.94 = (bf16[256,1024]{1,0:T(8,128)(2,1)S(1)}, f32[32,1024]{1,0:T(8,128)S(1)}, bf16[128,8192]{1,0:T(8,128)(2,1)S(1)}, bf16[66,8,128]{2,1,0:T(8,128)(2,1)S(1)}) custom-call(s32[1]{0:T(128)} %bitcast.rep_ref, s32[8,128]{1,0:T(8,128)} %bitcast.19, s32[64,128]{1,0:T(8,128)} %bitcast.15, f32[16,64]{1,0:T(8,128)} %bitcast.23, f32[16,64]{1,0:T(8,128)} %bitcast.25, ...), custom_call_target="tpu_custom_call" | custom-call | flops 1073741824 | bytes 2097152 | tf_op jit(solution)/shard_map/pallas_call | solution.py:364
  4.9 16.0 %collective-permute-start = (bf16[66,8,128]{2,1,0:T(8,128)(2,1)S(1)}, bf16[66,8,128]{2,1,0:T(8,128)(2,1)S(1)}, u32[]{:S(2)}, u32[]{:S(2)}) collective-permute-start(bf16[66,8,128]{2,1,0:T(8,128)(2,1)S(1)} %get-tuple-element.19), channel_id=1, source_target_pairs={{0,64},{64,0},{128,192},{192,128},{256,320},{320,256},{384,448},{4... | collective-permute-start | bytes 405512 | tf_op jit(solution)/shard_map/ppermute | solution.py:386
  21.0 0.0 copy-start.1
  21.0 0.0 copy-start.2
  21.0 0.0 copy-start.3
  21.0 0.0 copy-start
  21.0 1.4 %shard_map.95 = f32[64,8,128]{2,1,0:T(8,128)S(1)} custom-call(bf16[128,8192]{1,0:T(8,128)(2,1)S(1)} %get-tuple-element.16.signed_ref, bf16[256,1024]{1,0:T(8,128)(2,1)S(1)} %get-tuple-element.17.low_ref, f32[32,1024]{1,0:T(8,128)S(1)} %get-tuple-element.18.high_ref), custom_call_target="tpu_custom_call" | custom-call | flops 1073741824 | bytes 2097152 | tf_op jit(solution)/shard_map/pallas_call | solution.py:387
  22.4 0.0 copy-start.4
  22.4 0.0 collective-permute-done.other_ref
  22.4 0.7 add_convert_fusion.when_ref
  23.1 9.3 %all-to-all-start = ((bf16[64,8,128]{2,1,0:T(8,128)(2,1)}), bf16[64,8,128]{2,1,0:T(8,128)(2,1)S(1)}, u32[]{:S(2)}, u32[]{:S(2)}) async-start(bf16[64,8,128]{2,1,0:T(8,128)(2,1)} %add_convert_fusion.when_ref), calls=%async_computation | async-start | bytes 262144 | tf_op jit(solution)/shard_map/all_to_all | solution.py:356
  32.5 0.2 shard_map.96
  32.7 0.7 collective-permute-start.1
  33.4 14.0 %all-to-all-done.y_ref = bf16[64,8,128]{2,1,0:T(8,128)(2,1)S(1)} async-done(((bf16[64,8,128]{2,1,0:T(8,128)(2,1)}), bf16[64,8,128]{2,1,0:T(8,128)(2,1)S(1)}, u32[]{:S(2)}, u32[]{:S(2)}) %all-to-all-start) | async-done | bytes 131104 | tf_op jit(solution)/shard_map/all_to_all | solution.py:356
  47.4 1.0 %shard_map.97.when_ref = bf16[8,12,8,128]{3,2,1,0:T(8,128)(2,1)} custom-call(s32[1]{0:T(128)} %bitcast.1.panel_ref, bf16[64,8,128]{2,1,0:T(8,128)(2,1)S(1)} %all-to-all-done.y_ref, s32[64,128]{1,0:T(8,128)S(1)} %bitcast.16, bf16[256,1024]{1,0:T(8,128)(2,1)S(1)} %get-tuple-element.20.low_ref, f32[32,1024]{1,0:T(8,128)S(1)} %get-tuple-element.21.high_ref, ...), custom_call_target="tpu_custom_call" | custom-call | flops 2097152 | bytes 131072 | tf_op jit(solution)/shard_map/pallas_call | solution.py:409
  48.4 6.8 %all-to-all-start.1 = ((bf16[8,12,8,128]{3,2,1,0:T(8,128)(2,1)}), bf16[8,12,8,128]{3,2,1,0:T(8,128)(2,1)S(1)}, u32[]{:S(2)}, u32[]{:S(2)}) async-start(bf16[8,12,8,128]{3,2,1,0:T(8,128)(2,1)} %shard_map.97.when_ref), calls=%async_computation.1 | async-start | bytes 393216 | tf_op jit(solution)/shard_map/all_to_all | solution.py:356
  55.9 0.1 pad_maximum_fusion.fix_ref
  56.0 0.3 shard_map.98
  56.3 7.6 %all-to-all-done.1.got_ref = bf16[8,12,8,128]{3,2,1,0:T(8,128)(2,1)S(1)} async-done(((bf16[8,12,8,128]{3,2,1,0:T(8,128)(2,1)}), bf16[8,12,8,128]{3,2,1,0:T(8,128)(2,1)S(1)}, u32[]{:S(2)}, u32[]{:S(2)}) %all-to-all-start.1) | async-done | bytes 196640 | tf_op jit(solution)/shard_map/all_to_all | solution.py:356
  63.9 1.5 %shard_map.99 = (bf16[4,16,8,128]{3,2,1,0:T(8,128)(2,1)}, f32[8,128]{1,0:T(8,128)S(1)}) custom-call(s32[1]{0:T(128)} %bitcast.rep_ref, s32[1]{0:T(128)} %bitcast.1.panel_ref, f32[2]{0:T(128)S(1)} %pad_maximum_fusion.fix_ref, bf16[8,12,8,128]{3,2,1,0:T(8,128)(2,1)S(1)} %all-to-all-done.1.got_ref, s32[64,128]{1,0:T(8,128)S(1)} %bitcast.17, ...), custom_call_target="tpu_custom_call" | custom-call | flops 67108864 | bytes 131072 | tf_op jit(solution)/shard_map/pallas_call | solution.py:425
  65.4 8.0 %all-to-all-start.2 = ((bf16[64,8,128]{2,1,0:T(8,128)(2,1)}), bf16[64,8,128]{2,1,0:T(8,128)(2,1)S(1)}, u32[]{:S(2)}, u32[]{:S(2)}) async-start(bf16[64,8,128]{2,1,0:T(8,128)(2,1)} %bitcast.8), calls=%async_computation.2 | async-start | bytes 262144 | tf_op jit(solution)/shard_map/all_to_all | solution.py:356
  73.4 5.2 %collective-permute-start.4 = (f32[8,128]{1,0:T(8,128)S(1)}, f32[8,128]{1,0:T(8,128)S(1)}, u32[]{:S(2)}, u32[]{:S(2)}) collective-permute-start(f32[8,128]{1,0:T(8,128)S(1)} %get-tuple-element.28), channel_id=1, source_target_pairs={{0,64},{1,65},{2,66},{3,67},{4,68},{5,69},{6,70},{7,71},{8,72},{9,... | collective-permute-start | bytes 12296 | tf_op jit(solution)/shard_map/ppermute | solution.py:439
  78.7 0.7 collective-permute-start.3
  79.3 0.3 shard_map.100
  79.6 0.0 collective-permute-done.4
  79.6 0.1 slice_select_fusion
  79.7 0.1 slice_select_fusion.1
  79.8 7.6 %all-to-all-done.2.own_ref = bf16[64,8,128]{2,1,0:T(8,128)(2,1)S(1)} async-done(((bf16[64,8,128]{2,1,0:T(8,128)(2,1)}), bf16[64,8,128]{2,1,0:T(8,128)(2,1)S(1)}, u32[]{:S(2)}, u32[]{:S(2)}) %all-to-all-start.2) | async-done | bytes 131104 | tf_op jit(solution)/shard_map/all_to_all | solution.py:356
  87.4 6.4 %collective-permute-start.2 = (bf16[64,8,128]{2,1,0:T(8,128)(2,1)S(1)}, bf16[64,8,128]{2,1,0:T(8,128)(2,1)S(1)}, u32[]{:S(2)}, u32[]{:S(2)}) collective-permute-start(bf16[64,8,128]{2,1,0:T(8,128)(2,1)S(1)} %all-to-all-done.2.own_ref), channel_id=1, source_target_pairs={{0,64},{64,0},{128,192},{192,128},{256,320},{320,256},{384,448},{4... | collective-permute-start | bytes 393224 | tf_op jit(solution)/shard_map/ppermute | solution.py:441
  93.8 0.6 fusion.1
  94.4 0.3 collective-permute-done.2.other_ref
  94.7 3.9 %shard_map.101 = bf16[128,8192]{1,0:T(8,128)(2,1)} custom-call(s32[1]{0:T(128)} %bitcast.rep_ref, bf16[64,8,128]{2,1,0:T(8,128)(2,1)S(1)} %all-to-all-done.2.own_ref, bf16[64,8,128]{2,1,0:T(8,128)(2,1)S(1)} %collective-permute-done.2.other_ref, bf16[1024,256]{1,0:T(8,128)(2,1)S(1)} %get-tuple-element.26.turned_ref, ...), custom_call_target="tpu_custom_call" | custom-call | flops 2147483648 | bytes 4194304 | tf_op jit(solution)/shard_map/pallas_call | solution.py:454
  (7 shorter events, 0.0 us)
Async XLA Ops:
  4.9 17.5 %collective-permute-start = (bf16[66,8,128]{2,1,0:T(8,128)(2,1)S(1)}, bf16[66,8,128]{2,1,0:T(8,128)(2,1)S(1)}, u32[]{:S(2)}, u32[]{:S(2)}) collective-permute-start(bf16[66,8,128]{2,1,0:T(8,128)(2,1)S(1)} %get-tuple-element.19), channel_id=1, source_target_pairs={{0,64},{64,0},{128,192},{192,128},{256,320},{320,256},{384,448},{4... | collective-permute-start | bytes 405512 | tf_op jit(solution)/shard_map/ppermute | solution.py:386
  21.0 11.5 %copy-start.1 = (s32[1024]{0:T(1024)S(1)}, s32[1024]{0:T(1024)}, u32[]{:S(2)}) copy-start(s32[1024]{0:T(1024)} %param.12) | copy-start | bytes 12292
  21.0 11.5 %copy-start.2 = (f32[64,16]{0,1:T(8,128)S(1)}, f32[64,16]{0,1:T(8,128)}, u32[]{:S(2)}) copy-start(f32[64,16]{0,1:T(8,128)} %param.9) | copy-start | bytes 12292
  21.0 11.5 %copy-start.3 = (f32[64,16]{0,1:T(8,128)S(1)}, f32[64,16]{0,1:T(8,128)}, u32[]{:S(2)}) copy-start(f32[64,16]{0,1:T(8,128)} %param.10) | copy-start | bytes 12292
  21.0 26.4 %copy-start = (s32[8192]{0:T(1024)S(1)}, s32[8192]{0:T(1024)}, u32[]{:S(2)}) copy-start(s32[8192]{0:T(1024)} %param.11) | copy-start | bytes 98308
  22.4 72.3 %copy-start.4 = (bf16[128,8192]{1,0:T(8,128)(2,1)S(1)}, bf16[128,8192]{1,0:T(8,128)(2,1)}, u32[]{:S(2)}) copy-start(bf16[128,8192]{1,0:T(8,128)(2,1)} %weight_ref.1) | copy-start | bytes 6291460
  23.1 24.3 %all-to-all-start = ((bf16[64,8,128]{2,1,0:T(8,128)(2,1)}), bf16[64,8,128]{2,1,0:T(8,128)(2,1)S(1)}, u32[]{:S(2)}, u32[]{:S(2)}) async-start(bf16[64,8,128]{2,1,0:T(8,128)(2,1)} %add_convert_fusion.when_ref), calls=%async_computation | async-start | bytes 262144 | tf_op jit(solution)/shard_map/all_to_all | solution.py:356
  32.7 0.7 collective-permute-start.1
  48.4 15.5 %all-to-all-start.1 = ((bf16[8,12,8,128]{3,2,1,0:T(8,128)(2,1)}), bf16[8,12,8,128]{3,2,1,0:T(8,128)(2,1)S(1)}, u32[]{:S(2)}, u32[]{:S(2)}) async-start(bf16[8,12,8,128]{3,2,1,0:T(8,128)(2,1)} %shard_map.97.when_ref), calls=%async_computation.1 | async-start | bytes 393216 | tf_op jit(solution)/shard_map/all_to_all | solution.py:356
  65.4 22.0 %all-to-all-start.2 = ((bf16[64,8,128]{2,1,0:T(8,128)(2,1)}), bf16[64,8,128]{2,1,0:T(8,128)(2,1)S(1)}, u32[]{:S(2)}, u32[]{:S(2)}) async-start(bf16[64,8,128]{2,1,0:T(8,128)(2,1)} %bitcast.8), calls=%async_computation.2 | async-start | bytes 262144 | tf_op jit(solution)/shard_map/all_to_all | solution.py:356
  73.4 6.2 %collective-permute-start.4 = (f32[8,128]{1,0:T(8,128)S(1)}, f32[8,128]{1,0:T(8,128)S(1)}, u32[]{:S(2)}, u32[]{:S(2)}) collective-permute-start(f32[8,128]{1,0:T(8,128)S(1)} %get-tuple-element.28), channel_id=1, source_target_pairs={{0,64},{1,65},{2,66},{3,67},{4,68},{5,69},{6,70},{7,71},{8,72},{9,... | collective-permute-start | bytes 12296 | tf_op jit(solution)/shard_map/ppermute | solution.py:439
  78.7 1.1 %collective-permute-start.3 = (f32[8,128]{1,0:T(8,128)S(1)}, f32[8,128]{1,0:T(8,128)S(1)}, u32[]{:S(2)}, u32[]{:S(2)}) collective-permute-start(f32[8,128]{1,0:T(8,128)S(1)} %get-tuple-element.28), channel_id=1, source_target_pairs={{0,0},{1,1},{2,2},{3,3},{4,4},{5,5},{6,6},{7,7},{8,8},{9,9},{10,10... | collective-permute-start | bytes 12296 | tf_op jit(solution)/shard_map/ppermute | solution.py:438
  87.4 7.4 %collective-permute-start.2 = (bf16[64,8,128]{2,1,0:T(8,128)(2,1)S(1)}, bf16[64,8,128]{2,1,0:T(8,128)(2,1)S(1)}, u32[]{:S(2)}, u32[]{:S(2)}) collective-permute-start(bf16[64,8,128]{2,1,0:T(8,128)(2,1)S(1)} %all-to-all-done.2.own_ref), channel_id=1, source_target_pairs={{0,64},{64,0},{128,192},{192,128},{256,320},{320,256},{384,448},{4... | collective-permute-start | bytes 393224 | tf_op jit(solution)/shard_map/ppermute | solution.py:441

commit v7 on v6

--- a/solution.py
+++ b/solution.py
@@ -15,7 +15,6 @@
 LANES = 128
 WIDE = 256
 STEP = 1024
-LONG_STEP = 2048
 SIDE = 4
 PIECES = 2
 F32 = jnp.float32
@@ -175,6 +174,20 @@
 def turned_kernel(kept_ref, when_ref, turned_ref, high_ref, low_ref):
     fill_tables(kept_ref[...], low_ref, high_ref)
     turned_ref[...] = jnp.transpose(low_ref[...].astype(F32)).astype(BF16)
+
+
+def turned_and_sums_kernel(
+    rep_ref, kept_ref, own_ref, other_ref, when_ref, turned_ref, high_ref, sums_ref, low_ref
+):
+    turned_kernel(kept_ref, when_ref, turned_ref, high_ref, low_ref)
+    core = jnp.bitwise_and(rep_ref[0], 1)
+    own, other = own_ref[...], other_ref[...]
+    middle = LANES // 2
+    sums_ref[...] = jnp.where(
+        core == 0,
+        jnp.concatenate([own[:, :middle], other[:, :middle]], axis=1),
+        jnp.concatenate([other[:, middle:], own[:, middle:]], axis=1),
+    )
 
 
 def compress_kernel(
@@ -259,33 +272,38 @@
 
 
 def expand_kernel(
-    scale, rep_ref, own_ref, other_ref, turned_ref, high_ref, bits_ref, weight_ref, out_ref,
-    both_ref, back_ref, lhs_ref,
+    scale, rep_ref, own_ref, other_ref, turned_ref, high_ref, bits_ref, weight_ref, out_hbm,
+    both_ref, lhs_ref, out_ref, sems,
 ):
-    step = pl.program_id(0)
     rows = weight_ref.shape[0]
-    stride = out_ref.shape[1]
-    chunks = stride // WIDE
-
-    @pl.when(step == 0)
-    def _():
-        core = jnp.bitwise_and(rep_ref[0], 1)
-        both_ref[:, pl.ds(core, 1)] = own_ref[...].astype(F32)[:, None]
-        both_ref[:, pl.ds(1 - core, 1)] = other_ref[...].astype(F32)[:, None]
-        columns = both_ref[...].reshape(back_ref.shape[1], rows)
-        back_ref[...] = jnp.transpose(columns).astype(BF16)
-
-    for chunk in range(chunks):
-        sign = high_ref[pl.ds(step * chunks + chunk, 1), :].astype(BF16)
-        lhs_ref[chunk * rows : (chunk + 1) * rows, :] = back_ref[...] * sign
-    update = jnp.dot(lhs_ref[...], turned_ref[...], preferred_element_type=F32)
-    tiles = stride // LANES
-    signs = (1 - 2 * bits_ref[pl.ds(step * tiles, tiles), :]).astype(F32) * scale
-    for chunk in range(chunks):
-        lanes = pl.ds(pl.multiple_of(step * stride + chunk * WIDE, WIDE), WIDE)
-        moved = update[chunk * rows : (chunk + 1) * rows, :] * wide_rows(signs, 2 * chunk, 2)
-        moved = weight_ref[:, lanes].astype(F32) - moved
-        out_ref[:, chunk * WIDE : (chunk + 1) * WIDE] = moved.astype(BF16)
+    chunks = STEP // WIDE
+    tiles = STEP // LANES
+    core = jnp.bitwise_and(rep_ref[0], 1)
+    both_ref[:, pl.ds(core, 1)] = own_ref[...].astype(F32)[:, None]
+    both_ref[:, pl.ds(1 - core, 1)] = other_ref[...].astype(F32)[:, None]
+    back = jnp.transpose(both_ref[...].reshape(turned_ref.shape[0], rows)).astype(BF16)
+    steps = weight_ref.shape[1] // STEP
+
+    def store(step):
+        lanes = slice(step * STEP, (step + 1) * STEP)
+        return pltpu.make_async_copy(out_ref.at[:, lanes], out_hbm.at[:, lanes], sems.at[step])
+
+    for step in range(steps):
+        slot = step % 2
+        for chunk in range(chunks):
+            wide = step * chunks + chunk
+            sign = high_ref[wide : wide + 1, :].astype(BF16)
+            lhs_ref[slot, chunk * rows : (chunk + 1) * rows, :] = back * sign
+        update = jnp.dot(lhs_ref[slot], turned_ref[...], preferred_element_type=F32)
+        signs = (1 - 2 * bits_ref[step * tiles : (step + 1) * tiles, :]).astype(F32) * scale
+        for chunk in range(chunks):
+            first = step * STEP + chunk * WIDE
+            lanes = slice(first, first + WIDE)
+            moved = update[chunk * rows : (chunk + 1) * rows, :] * wide_rows(signs, 2 * chunk, 2)
+            out_ref[:, lanes] = (weight_ref[:, lanes].astype(F32) - moved).astype(BF16)
+        store(step).start()
+    for step in range(steps):
+        store(step).wait()
 
 
 def shaped(shape, dtype):
@@ -310,7 +328,6 @@
     norm_scale = 1.0 / math.sqrt(kept_len)
     rep = lax.axis_index("rep").astype(jnp.int32).reshape(1)
     panel = lax.axis_index("fsdp").astype(jnp.int32).reshape(1)
-    core = jnp.bitwise_and(rep[0], 1)
     kept = kept_rows.reshape(kept_len // LANES, LANES)
     bits = sign_bits.reshape(full_len // LANES, LANES)
     one_t, two_t = moment_one.T, moment_two.T
@@ -334,9 +351,9 @@
         for x in near for side in range(2) for z in range(line)
     ]
 
-    def turn_over(cross):
+    def turn_over():
         return [
-            (device(y_hi, x, side, y_lo, z), device(y_hi, y_lo, side ^ cross, x, z))
+            (device(y_hi, x, side, y_lo, z), device(y_hi, y_lo, side, x, z))
             for y_hi in range(far) for x in near for side in range(2)
             for y_lo in near for z in range(line)
         ]
@@ -357,6 +374,7 @@
 
     half_shape = (panels, half_width, rows)
     half_len = kept_len // 2
+    half_moments = shaped((half_width, LANES), F32)
     in_hbm = [
         pltpu.with_memory_space_constraint(x, pltpu.HBM)
         for x in (kept, bits, one_t, two_t, replica_grads)
@@ -402,7 +420,7 @@
         compiler_params=ROOM,
         cost_estimate=cost(10 * LANES * kept_len, 8 * WIDE * kept_len),
     )(rep, kept, one_t, two_t, from_other, columns)
-    moments = lax.ppermute(moments, both, turn_over(0))
+    moments = lax.ppermute(moments, both, turn_over())
     columns = regroup(columns, planes)
 
     message_shape = (peers, kept_len // LANES + 2 * PIECES, half_width, LANES)
@@ -434,33 +452,35 @@
         compiler_params=ROOM,
         cost_estimate=cost(full_len * half_width * kept_len, 2 * full_len * half_width),
     )(rep, panel, fixes, message, bits, turned, high)
-    turned, high = turn(back)
-    same_sum = lax.ppermute(own_sum, both, turn_over(0))
-    cross_sum = lax.ppermute(own_sum, both, turn_over(1))
+    other_sum = lax.ppermute(own_sum, "rep", swap)
+    turned, high, sums = pl.pallas_call(
+        turned_and_sums_kernel,
+        out_shape=(shaped((kept_len, WIDE), BF16), high_table, half_moments),
+        in_specs=[SMEM] + [VMEM] * 3 + [everywhere],
+        out_specs=(VMEM,) * 3,
+        scratch_shapes=[pltpu.VMEM(low_table.shape, BF16)],
+        compiler_params=ROOM,
+        cost_estimate=cost(10 * LANES * kept_len, 8 * WIDE * kept_len),
+    )(rep, kept, own_sum, other_sum, back)
+    sums = lax.ppermute(sums, both, turn_over())
     back = regroup(back.reshape(panels, half_width, rows), planes)
     other_back = lax.ppermute(back, "rep", swap)
 
     row_count = moment_one.shape[0]
-    same_rows = jnp.where(core == 0, same_sum[:, :row_count], same_sum[:, row_count:])
-    cross_rows = jnp.where(core == 0, cross_sum[:, :row_count], cross_sum[:, row_count:])
-    compressed = jnp.where(
-        core == 0,
-        jnp.concatenate([same_rows, cross_rows], axis=0),
-        jnp.concatenate([cross_rows, same_rows], axis=0),
-    )
+    compressed = jnp.concatenate([sums[:, :row_count], sums[:, row_count:]], axis=0)
     new_one = (BETA_ONE * one_t + (1.0 - BETA_ONE) * compressed).T
     new_two = (BETA_TWO * two_t + (1.0 - BETA_TWO) * compressed * compressed).T
 
     new_weight = pl.pallas_call(
         functools.partial(expand_kernel, LEARN_RATE * norm_scale),
-        grid=(full_len // LONG_STEP,),
         out_shape=shaped(weight.shape, BF16),
         in_specs=[SMEM] + [VMEM] * 6,
-        out_specs=pl.BlockSpec((rows, LONG_STEP), lambda i: (0, i)),
+        out_specs=pl.BlockSpec(memory_space=pltpu.HBM),
         scratch_shapes=[
             pltpu.VMEM((panels, 2, half_width, rows), F32),
-            pltpu.VMEM((rows, kept_len), BF16),
-            pltpu.VMEM((rows * LONG_STEP // WIDE, kept_len), BF16),
+            pltpu.VMEM((2, rows * STEP // WIDE, kept_len), BF16),
+            pltpu.VMEM(weight.shape, BF16),
+            pltpu.SemaphoreType.DMA((full_len // STEP,)),
         ],
         compiler_params=ROOM,
         cost_estimate=cost(2 * rows * full_len * kept_len, 4 * rows * full_len),

time: 99.1 us -> 98.6 us (level)
  transfers between devices with their start and end apart: 8 -> 8, of which waited for: 4 -> 5; matrix products, arithmetic and copies ran while one was open for 1% -> 1% of each run, Pallas kernels for 2% -> 2%
where the time goes in v7:
time: 98.6 us; the launch traced here: 98.2 us
  starting transfers between devices  53.1 us (54%)
  waiting for transfers between devices  29.6 us (30%)
  Pallas kernels  12.4 us (13%)
  between operations  1.55 us (2%)
  other arithmetic  1.37 us (1%)
    all_to_all x3, waiting for transfers between devices, regroup(): lax.all_to_all(blocks, both, 0, 0, axis_index_groups=groups, tiled=True)  28.5 us
    all_to_all x3, starting transfers between devices, regroup(): lax.all_to_all(blocks, both, 0, 0, axis_index_groups=groups, tiled=True)  24.1 us
    ppermute x1, starting transfers between devices, local(): from_other = lax.ppermute(for_other, 'rep', swap)  16 us
    ppermute x1, starting transfers between devices, local(): other_back = lax.ppermute(back, 'rep', swap)  6.39 us
    ppermute x1, starting transfers between devices, local(): other_sum = lax.ppermute(own_sum, 'rep', swap)  5.24 us
    pallas_call x1, Pallas kernels, local(): pl.pallas_call(functools.partial(project_other_kernel, norm_scale), out_s...  4.28 us
    pallas_call x1, Pallas kernels, local(): pl.pallas_call(functools.partial(expand_kernel, LEARN_RATE * norm_scale),...  3.42 us
  transfers between devices with their start and end apart: 8, of which 5 were waited for; matrix products, arithmetic and copies ran while one was open for 1% of the time, Pallas kernels for 2%

profile of v7, /device:TPU:1, one launch (start us, length us, event | category | flops | bytes accessed | tf_op | source)
XLA Modules:
  0.0 98.2 jit_solution(9342883900326216816)
XLA Ops:
  0.6 4.3 %shard_map.94 = (bf16[256,1024]{1,0:T(8,128)(2,1)S(1)}, f32[32,1024]{1,0:T(8,128)S(1)}, bf16[128,8192]{1,0:T(8,128)(2,1)S(1)}, bf16[66,8,128]{2,1,0:T(8,128)(2,1)S(1)}) custom-call(s32[1]{0:T(128)} %bitcast.rep_ref, s32[8,128]{1,0:T(8,128)} %bitcast.19, s32[64,128]{1,0:T(8,128)} %bitcast.15, f32[16,64]{1,0:T(8,128)} %bitcast.23, f32[16,64]{1,0:T(8,128)} %bitcast.25, ...), custom_call_target="tpu_custom_call" | custom-call | flops 1073741824 | bytes 2097152 | tf_op jit(solution)/shard_map/pallas_call | solution.py:382
  4.9 16.0 %collective-permute-start = (bf16[66,8,128]{2,1,0:T(8,128)(2,1)S(1)}, bf16[66,8,128]{2,1,0:T(8,128)(2,1)S(1)}, u32[]{:S(2)}, u32[]{:S(2)}) collective-permute-start(bf16[66,8,128]{2,1,0:T(8,128)(2,1)S(1)} %get-tuple-element.20), channel_id=1, source_target_pairs={{0,64},{64,0},{128,192},{192,128},{256,320},{320,256},{384,448},{4... | collective-permute-start | bytes 405512 | tf_op jit(solution)/shard_map/ppermute | solution.py:404
  21.0 0.0 copy-start.1
  21.0 0.0 copy-start.2
  21.0 0.0 copy-start.3
  21.0 0.0 copy-start
  21.0 1.4 %shard_map.95 = f32[64,8,128]{2,1,0:T(8,128)S(1)} custom-call(bf16[128,8192]{1,0:T(8,128)(2,1)S(1)} %get-tuple-element.17.signed_ref, bf16[256,1024]{1,0:T(8,128)(2,1)S(1)} %get-tuple-element.18.low_ref, f32[32,1024]{1,0:T(8,128)S(1)} %get-tuple-element.19.high_ref), custom_call_target="tpu_custom_call" | custom-call | flops 1073741824 | bytes 2097152 | tf_op jit(solution)/shard_map/pallas_call | solution.py:405
  22.4 0.0 copy-start.4
  22.4 0.0 collective-permute-done.other_ref
  22.4 0.7 add_convert_fusion.when_ref
  23.1 9.3 %all-to-all-start = ((bf16[64,8,128]{2,1,0:T(8,128)(2,1)}), bf16[64,8,128]{2,1,0:T(8,128)(2,1)S(1)}, u32[]{:S(2)}, u32[]{:S(2)}) async-start(bf16[64,8,128]{2,1,0:T(8,128)(2,1)} %add_convert_fusion.when_ref), calls=%async_computation | async-start | bytes 262144 | tf_op jit(solution)/shard_map/all_to_all | solution.py:373
  32.5 0.2 shard_map.96
  32.7 0.7 collective-permute-start.1
  33.4 0.0 collective-permute-done.1.moments_ref
  33.4 14.0 %all-to-all-done.y_ref = bf16[64,8,128]{2,1,0:T(8,128)(2,1)S(1)} async-done(((bf16[64,8,128]{2,1,0:T(8,128)(2,1)}), bf16[64,8,128]{2,1,0:T(8,128)(2,1)S(1)}, u32[]{:S(2)}, u32[]{:S(2)}) %all-to-all-start) | async-done | bytes 131104 | tf_op jit(solution)/shard_map/all_to_all | solution.py:373
  47.4 1.0 %shard_map.97.when_ref = bf16[8,12,8,128]{3,2,1,0:T(8,128)(2,1)} custom-call(s32[1]{0:T(128)} %bitcast.1.panel_ref, bf16[64,8,128]{2,1,0:T(8,128)(2,1)S(1)} %all-to-all-done.y_ref, s32[64,128]{1,0:T(8,128)S(1)} %bitcast.16, bf16[256,1024]{1,0:T(8,128)(2,1)S(1)} %get-tuple-element.21.low_ref, f32[32,1024]{1,0:T(8,128)S(1)} %get-tuple-element.22.high_ref, ...), custom_call_target="tpu_custom_call" | custom-call | flops 2097152 | bytes 131072 | tf_op jit(solution)/shard_map/pallas_call | solution.py:427
  48.4 6.8 %all-to-all-start.1 = ((bf16[8,12,8,128]{3,2,1,0:T(8,128)(2,1)}), bf16[8,12,8,128]{3,2,1,0:T(8,128)(2,1)S(1)}, u32[]{:S(2)}, u32[]{:S(2)}) async-start(bf16[8,12,8,128]{3,2,1,0:T(8,128)(2,1)} %shard_map.97.when_ref), calls=%async_computation.1 | async-start | bytes 393216 | tf_op jit(solution)/shard_map/all_to_all | solution.py:373
  55.9 0.1 pad_maximum_fusion.1.fix_ref
  56.0 0.3 shard_map.98
  56.3 7.6 %all-to-all-done.1.got_ref = bf16[8,12,8,128]{3,2,1,0:T(8,128)(2,1)S(1)} async-done(((bf16[8,12,8,128]{3,2,1,0:T(8,128)(2,1)}), bf16[8,12,8,128]{3,2,1,0:T(8,128)(2,1)S(1)}, u32[]{:S(2)}, u32[]{:S(2)}) %all-to-all-start.1) | async-done | bytes 196640 | tf_op jit(solution)/shard_map/all_to_all | solution.py:373
  63.9 1.5 %shard_map.99 = (bf16[4,16,8,128]{3,2,1,0:T(8,128)(2,1)}, f32[8,128]{1,0:T(8,128)S(1)}) custom-call(s32[1]{0:T(128)} %bitcast.rep_ref, s32[1]{0:T(128)} %bitcast.1.panel_ref, f32[2]{0:T(128)S(1)} %pad_maximum_fusion.1.fix_ref, bf16[8,12,8,128]{3,2,1,0:T(8,128)(2,1)S(1)} %all-to-all-done.1.got_ref, s32[64,128]{1,0:T(8,128)S(1)} %bitcast.17, ...), custom_call_target="tpu_custom_call" | custom-call | flops 67108864 | bytes 131072 | tf_op jit(solution)/shard_map/pallas_call | solution.py:443
  65.4 8.0 %all-to-all-start.2 = ((bf16[64,8,128]{2,1,0:T(8,128)(2,1)}), bf16[64,8,128]{2,1,0:T(8,128)(2,1)S(1)}, u32[]{:S(2)}, u32[]{:S(2)}) async-start(bf16[64,8,128]{2,1,0:T(8,128)(2,1)} %bitcast.8), calls=%async_computation.2 | async-start | bytes 262144 | tf_op jit(solution)/shard_map/all_to_all | solution.py:373
  73.4 5.2 %collective-permute-start.3 = (f32[8,128]{1,0:T(8,128)S(1)}, f32[8,128]{1,0:T(8,128)S(1)}, u32[]{:S(2)}, u32[]{:S(2)}) collective-permute-start(f32[8,128]{1,0:T(8,128)S(1)} %get-tuple-element.27.own_ref), channel_id=1, source_target_pairs={{0,64},{64,0},{128,192},{192,128},{256,320},{320,256},{384,448},{4... | collective-permute-start | bytes 12296 | tf_op jit(solution)/shard_map/ppermute | solution.py:455
  78.7 0.8 collective-permute-done.3.other_ref
  79.5 0.3 shard_map.100
  79.8 0.7 collective-permute-start.4
  80.4 0.1 fusion.2
  80.5 6.8 %all-to-all-done.2.own_ref = bf16[64,8,128]{2,1,0:T(8,128)(2,1)S(1)} async-done(((bf16[64,8,128]{2,1,0:T(8,128)(2,1)}), bf16[64,8,128]{2,1,0:T(8,128)(2,1)S(1)}, u32[]{:S(2)}, u32[]{:S(2)}) %all-to-all-start.2) | async-done | bytes 131104 | tf_op jit(solution)/shard_map/all_to_all | solution.py:373
  87.4 6.4 %collective-permute-start.2 = (bf16[64,8,128]{2,1,0:T(8,128)(2,1)S(1)}, bf16[64,8,128]{2,1,0:T(8,128)(2,1)S(1)}, u32[]{:S(2)}, u32[]{:S(2)}) collective-permute-start(bf16[64,8,128]{2,1,0:T(8,128)(2,1)S(1)} %all-to-all-done.2.own_ref), channel_id=1, source_target_pairs={{0,64},{64,0},{128,192},{192,128},{256,320},{320,256},{384,448},{4... | collective-permute-start | bytes 393224 | tf_op jit(solution)/shard_map/ppermute | solution.py:467
  93.8 0.6 fusion.1
  94.4 0.4 collective-permute-done.2.other_ref
  94.7 3.4 %shard_map.101 = bf16[128,8192]{1,0:T(8,128)(2,1)} custom-call(s32[1]{0:T(128)} %bitcast.rep_ref, bf16[64,8,128]{2,1,0:T(8,128)(2,1)S(1)} %all-to-all-done.2.own_ref, bf16[64,8,128]{2,1,0:T(8,128)(2,1)S(1)} %collective-permute-done.2.other_ref, bf16[1024,256]{1,0:T(8,128)(2,1)S(1)} %get-tuple-element.28.turned_ref, ...), custom_call_target="tpu_custom_call" | custom-call | flops 2147483648 | bytes 4194304 | tf_op jit(solution)/shard_map/pallas_call | solution.py:474
  (6 shorter events, 0.0 us)
Async XLA Ops:
  4.9 17.5 %collective-permute-start = (bf16[66,8,128]{2,1,0:T(8,128)(2,1)S(1)}, bf16[66,8,128]{2,1,0:T(8,128)(2,1)S(1)}, u32[]{:S(2)}, u32[]{:S(2)}) collective-permute-start(bf16[66,8,128]{2,1,0:T(8,128)(2,1)S(1)} %get-tuple-element.20), channel_id=1, source_target_pairs={{0,64},{64,0},{128,192},{192,128},{256,320},{320,256},{384,448},{4... | collective-permute-start | bytes 405512 | tf_op jit(solution)/shard_map/ppermute | solution.py:404
  21.0 11.5 %copy-start.1 = (s32[1024]{0:T(1024)S(1)}, s32[1024]{0:T(1024)}, u32[]{:S(2)}) copy-start(s32[1024]{0:T(1024)} %param.12) | copy-start | bytes 12292
  21.0 11.5 %copy-start.2 = (f32[64,16]{0,1:T(8,128)S(1)}, f32[64,16]{0,1:T(8,128)}, u32[]{:S(2)}) copy-start(f32[64,16]{0,1:T(8,128)} %param.9) | copy-start | bytes 12292
  21.0 11.5 %copy-start.3 = (f32[64,16]{0,1:T(8,128)S(1)}, f32[64,16]{0,1:T(8,128)}, u32[]{:S(2)}) copy-start(f32[64,16]{0,1:T(8,128)} %param.10) | copy-start | bytes 12292
  21.0 26.4 %copy-start = (s32[8192]{0:T(1024)S(1)}, s32[8192]{0:T(1024)}, u32[]{:S(2)}) copy-start(s32[8192]{0:T(1024)} %param.11) | copy-start | bytes 98308
  22.4 72.3 %copy-start.4 = (bf16[128,8192]{1,0:T(8,128)(2,1)S(1)}, bf16[128,8192]{1,0:T(8,128)(2,1)}, u32[]{:S(2)}) copy-start(bf16[128,8192]{1,0:T(8,128)(2,1)} %weight_ref.1) | copy-start | bytes 6291460
  23.1 24.3 %all-to-all-start = ((bf16[64,8,128]{2,1,0:T(8,128)(2,1)}), bf16[64,8,128]{2,1,0:T(8,128)(2,1)S(1)}, u32[]{:S(2)}, u32[]{:S(2)}) async-start(bf16[64,8,128]{2,1,0:T(8,128)(2,1)} %add_convert_fusion.when_ref), calls=%async_computation | async-start | bytes 262144 | tf_op jit(solution)/shard_map/all_to_all | solution.py:373
  32.7 0.7 collective-permute-start.1
  48.4 15.5 %all-to-all-start.1 = ((bf16[8,12,8,128]{3,2,1,0:T(8,128)(2,1)}), bf16[8,12,8,128]{3,2,1,0:T(8,128)(2,1)S(1)}, u32[]{:S(2)}, u32[]{:S(2)}) async-start(bf16[8,12,8,128]{3,2,1,0:T(8,128)(2,1)} %shard_map.97.when_ref), calls=%async_computation.1 | async-start | bytes 393216 | tf_op jit(solution)/shard_map/all_to_all | solution.py:373
  65.4 22.0 %all-to-all-start.2 = ((bf16[64,8,128]{2,1,0:T(8,128)(2,1)}), bf16[64,8,128]{2,1,0:T(8,128)(2,1)S(1)}, u32[]{:S(2)}, u32[]{:S(2)}) async-start(bf16[64,8,128]{2,1,0:T(8,128)(2,1)} %bitcast.8), calls=%async_computation.2 | async-start | bytes 262144 | tf_op jit(solution)/shard_map/all_to_all | solution.py:373
  73.4 6.0 %collective-permute-start.3 = (f32[8,128]{1,0:T(8,128)S(1)}, f32[8,128]{1,0:T(8,128)S(1)}, u32[]{:S(2)}, u32[]{:S(2)}) collective-permute-start(f32[8,128]{1,0:T(8,128)S(1)} %get-tuple-element.27.own_ref), channel_id=1, source_target_pairs={{0,64},{64,0},{128,192},{192,128},{256,320},{320,256},{384,448},{4... | collective-permute-start | bytes 12296 | tf_op jit(solution)/shard_map/ppermute | solution.py:455
  79.8 0.7 collective-permute-start.4
  87.4 7.4 %collective-permute-start.2 = (bf16[64,8,128]{2,1,0:T(8,128)(2,1)S(1)}, bf16[64,8,128]{2,1,0:T(8,128)(2,1)S(1)}, u32[]{:S(2)}, u32[]{:S(2)}) collective-permute-start(bf16[64,8,128]{2,1,0:T(8,128)(2,1)S(1)} %all-to-all-done.2.own_ref), channel_id=1, source_target_pairs={{0,64},{64,0},{128,192},{192,128},{256,320},{320,256},{384,448},{4... | collective-permute-start | bytes 393224 | tf_op jit(solution)/shard_map/ppermute | solution.py:467
